TPU v7x, 128 devices: a whole 4x4x4 slice. The times are simulated.
128 devices in a mesh: space: 16 (over x_lo, y, core), tm: 8 (over x_hi, z).
Axes of the slice: x: 4 (x_hi: 2, x_lo: 2; x = x_hi * 2 + x_lo), y: 4, z: 4, core: 2. Of those that a mesh axis runs over, the one named last changes fastest.
Arguments:
- vectors: bfloat16 [8, 2, 3, 96, 8192], P('tm', None, None, None, 'space'), may hold values from -6 to 6
- momenta: int32 [2, 3], replicated, may hold values from -3 to 3
- offsets: int32 [16, 3], replicated, may hold values from 0 to 56, as said below
Outputs:
- elementals: float32 [8, 96, 2, 18432], P(None, 'space')
Inputs may be any that keep to these rules, and one draw needn't show every extreme that they name: `offsets`: each row is the corner of one block of 8 x 8 x 8 sites of the 64^3 lattice: its first two coordinates are multiples of 8, its third a multiple of 8; no two rows name the same block, so the blocks never intersect.
All inputs are finite; a program needn't handle non-finite values.
Results may differ from a plain program's by a relative error of at most 0.0055.
Values may be sent and summed in bfloat16 or wider, within the bound.
No kernel may reach another device: no remote copies, remote signals or barrier semaphores. Data moves between devices by JAX's collectives and lax.ppermute only.
A program may use at most 128 MiB of HBM per device.

v0:
```python
import math

import jax
import jax.numpy as jnp
from jax import lax
from jax.sharding import PartitionSpec as P

LAT = 64
BRICK = 8
BRICK_Z = 8


def local_coords(site):
    return jnp.stack([site // (BRICK * BRICK_Z), site // BRICK_Z % BRICK, site % BRICK_Z])


def phases(momenta, coords):
    product = jnp.sum(momenta[:, :, None] * coords[None, :, :], axis=1)
    angle = (product % LAT).astype(jnp.float32) * (2.0 * math.pi / LAT)
    return jnp.stack([jnp.cos(angle), jnp.sin(angle)], axis=1)


def complex_term(w_real, w_imag, v_real, v_imag):
    return (w_real * v_real - w_imag * v_imag, w_real * v_imag + w_imag * v_real)


def cross_rows(phase, row_vecs, vecs):
    rows_f = row_vecs.astype(jnp.float32)
    cosine = phase[:, 0][:, None, None, :]
    sine = phase[:, 1][:, None, None, :]
    real_w = cosine * rows_f[0][None] - sine * rows_f[1][None]
    imag_w = cosine * rows_f[1][None] + sine * rows_f[0][None]
    real_w = jnp.transpose(real_w, (2, 0, 1, 3))
    imag_w = jnp.transpose(imag_w, (2, 0, 1, 3))
    real_v = vecs[0].astype(jnp.float32)
    imag_v = vecs[1].astype(jnp.float32)
    real_parts = []
    imag_parts = []
    for colour in range(3):
        first = (colour + 1) % 3
        second = (colour + 2) % 3
        plus_re, plus_im = complex_term(
            real_w[:, :, first, None, :],
            imag_w[:, :, first, None, :],
            real_v[second][None, None],
            imag_v[second][None, None],
        )
        minus_re, minus_im = complex_term(
            real_w[:, :, second, None, :],
            imag_w[:, :, second, None, :],
            real_v[first][None, None],
            imag_v[first][None, None],
        )
        real_parts.append(plus_re - minus_re)
        imag_parts.append(plus_im - minus_im)
    stacked = jnp.stack([jnp.stack(real_parts, axis=3), jnp.stack(imag_parts, axis=3)], axis=3)
    return stacked.astype(jnp.bfloat16)


def mixing(vecs):
    real_v = vecs[0]
    imag_v = vecs[1]
    return jnp.stack([jnp.stack([real_v, imag_v], axis=1), jnp.stack([-imag_v, real_v], axis=1)])


def body(vectors, momenta, offsets):
    local = vectors[0]
    nvec = local.shape[2]
    sites = local.shape[3]
    groups = lax.axis_size("space")
    rows = nvec // groups
    width = 2 * nvec * nvec
    moments = momenta.shape[0]
    mine = lax.axis_index("space") * rows
    empty = jnp.zeros((rows, moments, width), jnp.float32)
    vec_piece = lax.all_gather(local.reshape(6 * nvec, sites), "space", axis=1, tiled=True)
    length = vec_piece.shape[1]
    block = math.gcd(length, sites)

    def advance(index, acc):
        vec_block = lax.dynamic_slice_in_dim(vec_piece, index * block, block, 1).reshape(
            2, 3, nvec, block
        )
        site_ids = index * block + jnp.arange(block, dtype=jnp.int32)
        brick_ids = site_ids // sites
        coords = local_coords(site_ids % sites) + jnp.transpose(
            jnp.take(offsets, brick_ids, axis=0)
        )
        phase_block = phases(momenta, coords)
        row_vecs = lax.dynamic_slice_in_dim(vec_block, mine, rows, 2)
        crossed = cross_rows(phase_block, row_vecs, vec_block)
        part = jnp.einsum(
            "imjqcg,qcrkg->imjrk", crossed, mixing(vec_block), preferred_element_type=jnp.float32
        )
        return acc + part.reshape(rows, moments, width)

    summed = lax.fori_loop(0, length // block, advance, empty)
    finished = summed * (1.0 / math.sqrt(sites * groups))
    gathered = lax.all_gather(finished[None], "tm", axis=0, tiled=True)
    return gathered


def solution(mesh):
    return jax.shard_map(
        body,
        mesh=mesh,
        in_specs=(P("tm", None, None, None, "space"), P(), P()),
        out_specs=P(None, "space", None, None),
        check_vma=False,
    )
```

profile of v0, /device:TPU:0, one launch (start us, length us, event | category | flops | bytes accessed | tf_op | source)
XLA Modules:
  0.0 420.3 jit_solution(780666687985766581)
XLA Ops:
  8.8 59.7 %all-gather.4.cloned.1.call-done = bf16[576,8192]{1,0:T(8,128)(2,1)} async-done(((bf16[576,512]{1,0:T(8,128)(2,1)}), bf16[576,8192]{1,0:T(8,128)(2,1)}) %all-gather.4.cloned.1.call-update) | async-done | bytes 9437200 | tf_op jit(solution)/shard_map/all_gather | solution.py:76
  68.5 240.3 %while.17 = (s32[]{:T(128)}, f32[6,2,18432]{2,1,0:T(2,128)S(1)}, s32[2,3]{0,1:T(4,128)S(1)}, s32[16,3]{1,0:T(8,128)S(1)}, bf16[576,8192]{1,0:T(8,128)(2,1)}, /*i...) while((s32[]{:T(128)}, f32[6,2,18432]{2,1,0:T(2,128)S(1)}, ...), condition=%wide.region_2.3_spmd.clone, body=%wide.region_0.2_spmd.clone.sunk | while | flops 1412249600 | bytes 46142696 | solution.py:97
  72.6 4.4 %subtract_convert_fusion.7 = (bf16[6,2,96,1,512]{4,2,3,1,0:T(8,128)(2,1)S(1)}, bf16[6,2,96,1,512]{4,2,3,1,0:T(8,128)(2,1)S(1)}, bf16[6,2,96,1,512]{4,2,3,1,0:T(8...) fusion(f32[96,512]{1,0:T(8,128)S(1)} %get-tuple-element.381, ...), kind=kLoop, calls=%fused_computation.12.clone.1 | loop fusion | flops 28311552 | bytes 8404992 | tf_op jit(solution)/shard_map/convert.7
  78.1 2.0 fusion.24
  87.7 4.4 %subtract_convert_fusion.7 = (bf16[6,2,96,1,512]{4,2,3,1,0:T(8,128)(2,1)S(1)}, bf16[6,2,96,1,512]{4,2,3,1,0:T(8,128)(2,1)S(1)}, bf16[6,2,96,1,512]{4,2,3,1,0:T(8...) fusion(f32[96,512]{1,0:T(8,128)S(1)} %get-tuple-element.381, ...), kind=kLoop, calls=%fused_computation.12.clone.1 | loop fusion | flops 28311552 | bytes 8404992 | tf_op jit(solution)/shard_map/convert.7
  102.7 4.4 %subtract_convert_fusion.7 = (bf16[6,2,96,1,512]{4,2,3,1,0:T(8,128)(2,1)S(1)}, bf16[6,2,96,1,512]{4,2,3,1,0:T(8,128)(2,1)S(1)}, bf16[6,2,96,1,512]{4,2,3,1,0:T(8...) fusion(f32[96,512]{1,0:T(8,128)S(1)} %get-tuple-element.381, ...), kind=kLoop, calls=%fused_computation.12.clone.1 | loop fusion | flops 28311552 | bytes 8404992 | tf_op jit(solution)/shard_map/convert.7
  108.2 2.0 fusion.24
  117.7 4.4 %subtract_convert_fusion.7 = (bf16[6,2,96,1,512]{4,2,3,1,0:T(8,128)(2,1)S(1)}, bf16[6,2,96,1,512]{4,2,3,1,0:T(8,128)(2,1)S(1)}, bf16[6,2,96,1,512]{4,2,3,1,0:T(8...) fusion(f32[96,512]{1,0:T(8,128)S(1)} %get-tuple-element.381, ...), kind=kLoop, calls=%fused_computation.12.clone.1 | loop fusion | flops 28311552 | bytes 8404992 | tf_op jit(solution)/shard_map/convert.7
  123.2 2.0 fusion.24
  132.7 4.4 %subtract_convert_fusion.7 = (bf16[6,2,96,1,512]{4,2,3,1,0:T(8,128)(2,1)S(1)}, bf16[6,2,96,1,512]{4,2,3,1,0:T(8,128)(2,1)S(1)}, bf16[6,2,96,1,512]{4,2,3,1,0:T(8...) fusion(f32[96,512]{1,0:T(8,128)S(1)} %get-tuple-element.381, ...), kind=kLoop, calls=%fused_computation.12.clone.1 | loop fusion | flops 28311552 | bytes 8404992 | tf_op jit(solution)/shard_map/convert.7
  138.2 2.0 fusion.24
  147.7 4.4 %subtract_convert_fusion.7 = (bf16[6,2,96,1,512]{4,2,3,1,0:T(8,128)(2,1)S(1)}, bf16[6,2,96,1,512]{4,2,3,1,0:T(8,128)(2,1)S(1)}, bf16[6,2,96,1,512]{4,2,3,1,0:T(8...) fusion(f32[96,512]{1,0:T(8,128)S(1)} %get-tuple-element.381, ...), kind=kLoop, calls=%fused_computation.12.clone.1 | loop fusion | flops 28311552 | bytes 8404992 | tf_op jit(solution)/shard_map/convert.7
  153.2 2.0 fusion.24
  162.7 4.4 %subtract_convert_fusion.7 = (bf16[6,2,96,1,512]{4,2,3,1,0:T(8,128)(2,1)S(1)}, bf16[6,2,96,1,512]{4,2,3,1,0:T(8,128)(2,1)S(1)}, bf16[6,2,96,1,512]{4,2,3,1,0:T(8...) fusion(f32[96,512]{1,0:T(8,128)S(1)} %get-tuple-element.381, ...), kind=kLoop, calls=%fused_computation.12.clone.1 | loop fusion | flops 28311552 | bytes 8404992 | tf_op jit(solution)/shard_map/convert.7
  168.2 2.0 fusion.24
  177.8 4.4 %subtract_convert_fusion.7 = (bf16[6,2,96,1,512]{4,2,3,1,0:T(8,128)(2,1)S(1)}, bf16[6,2,96,1,512]{4,2,3,1,0:T(8,128)(2,1)S(1)}, bf16[6,2,96,1,512]{4,2,3,1,0:T(8...) fusion(f32[96,512]{1,0:T(8,128)S(1)} %get-tuple-element.381, ...), kind=kLoop, calls=%fused_computation.12.clone.1 | loop fusion | flops 28311552 | bytes 8404992 | tf_op jit(solution)/shard_map/convert.7
  183.3 2.0 fusion.24
  192.8 4.4 %subtract_convert_fusion.7 = (bf16[6,2,96,1,512]{4,2,3,1,0:T(8,128)(2,1)S(1)}, bf16[6,2,96,1,512]{4,2,3,1,0:T(8,128)(2,1)S(1)}, bf16[6,2,96,1,512]{4,2,3,1,0:T(8...) fusion(f32[96,512]{1,0:T(8,128)S(1)} %get-tuple-element.381, ...), kind=kLoop, calls=%fused_computation.12.clone.1 | loop fusion | flops 28311552 | bytes 8404992 | tf_op jit(solution)/shard_map/convert.7
  198.3 2.0 fusion.24
  207.8 4.4 %subtract_convert_fusion.7 = (bf16[6,2,96,1,512]{4,2,3,1,0:T(8,128)(2,1)S(1)}, bf16[6,2,96,1,512]{4,2,3,1,0:T(8,128)(2,1)S(1)}, bf16[6,2,96,1,512]{4,2,3,1,0:T(8...) fusion(f32[96,512]{1,0:T(8,128)S(1)} %get-tuple-element.381, ...), kind=kLoop, calls=%fused_computation.12.clone.1 | loop fusion | flops 28311552 | bytes 8404992 | tf_op jit(solution)/shard_map/convert.7
  222.8 4.4 %subtract_convert_fusion.7 = (bf16[6,2,96,1,512]{4,2,3,1,0:T(8,128)(2,1)S(1)}, bf16[6,2,96,1,512]{4,2,3,1,0:T(8,128)(2,1)S(1)}, bf16[6,2,96,1,512]{4,2,3,1,0:T(8...) fusion(f32[96,512]{1,0:T(8,128)S(1)} %get-tuple-element.381, ...), kind=kLoop, calls=%fused_computation.12.clone.1 | loop fusion | flops 28311552 | bytes 8404992 | tf_op jit(solution)/shard_map/convert.7
  228.3 2.0 fusion.24
  237.8 4.4 %subtract_convert_fusion.7 = (bf16[6,2,96,1,512]{4,2,3,1,0:T(8,128)(2,1)S(1)}, bf16[6,2,96,1,512]{4,2,3,1,0:T(8,128)(2,1)S(1)}, bf16[6,2,96,1,512]{4,2,3,1,0:T(8...) fusion(f32[96,512]{1,0:T(8,128)S(1)} %get-tuple-element.381, ...), kind=kLoop, calls=%fused_computation.12.clone.1 | loop fusion | flops 28311552 | bytes 8404992 | tf_op jit(solution)/shard_map/convert.7
  243.3 2.0 fusion.24
  252.9 4.4 %subtract_convert_fusion.7 = (bf16[6,2,96,1,512]{4,2,3,1,0:T(8,128)(2,1)S(1)}, bf16[6,2,96,1,512]{4,2,3,1,0:T(8,128)(2,1)S(1)}, bf16[6,2,96,1,512]{4,2,3,1,0:T(8...) fusion(f32[96,512]{1,0:T(8,128)S(1)} %get-tuple-element.381, ...), kind=kLoop, calls=%fused_computation.12.clone.1 | loop fusion | flops 28311552 | bytes 8404992 | tf_op jit(solution)/shard_map/convert.7
  267.9 4.4 %subtract_convert_fusion.7 = (bf16[6,2,96,1,512]{4,2,3,1,0:T(8,128)(2,1)S(1)}, bf16[6,2,96,1,512]{4,2,3,1,0:T(8,128)(2,1)S(1)}, bf16[6,2,96,1,512]{4,2,3,1,0:T(8...) fusion(f32[96,512]{1,0:T(8,128)S(1)} %get-tuple-element.381, ...), kind=kLoop, calls=%fused_computation.12.clone.1 | loop fusion | flops 28311552 | bytes 8404992 | tf_op jit(solution)/shard_map/convert.7
  273.4 2.0 fusion.24
  282.9 4.4 %subtract_convert_fusion.7 = (bf16[6,2,96,1,512]{4,2,3,1,0:T(8,128)(2,1)S(1)}, bf16[6,2,96,1,512]{4,2,3,1,0:T(8,128)(2,1)S(1)}, bf16[6,2,96,1,512]{4,2,3,1,0:T(8...) fusion(f32[96,512]{1,0:T(8,128)S(1)} %get-tuple-element.381, ...), kind=kLoop, calls=%fused_computation.12.clone.1 | loop fusion | flops 28311552 | bytes 8404992 | tf_op jit(solution)/shard_map/convert.7
  288.4 2.0 fusion.24
  297.9 4.4 %subtract_convert_fusion.7 = (bf16[6,2,96,1,512]{4,2,3,1,0:T(8,128)(2,1)S(1)}, bf16[6,2,96,1,512]{4,2,3,1,0:T(8,128)(2,1)S(1)}, bf16[6,2,96,1,512]{4,2,3,1,0:T(8...) fusion(f32[96,512]{1,0:T(8,128)S(1)} %get-tuple-element.381, ...), kind=kLoop, calls=%fused_computation.12.clone.1 | loop fusion | flops 28311552 | bytes 8404992 | tf_op jit(solution)/shard_map/convert.7
  310.2 96.7 %all-gather.6.cloned.1.call-done = f32[48,2,18432]{2,1,0:T(2,128)} async-done(((f32[6,2,18432]{2,1,0:T(2,128)}), f32[48,2,18432]{2,1,0:T(2,128)}) %all-gather.6.cloned.1.call-update) | async-done | bytes 7077904 | tf_op jit(solution)/shard_map/all_gather | solution.py:99
  407.0 6.4 %copy.46 = f32[8,6,2,18432]{3,2,1,0:T(2,128)} copy(f32[8,6,2,18432]{3,2,1,0:T(2,128)} %bitcast.88) | data formatting | bytes 14155776
  (428 shorter events, 145.4 us)
Async XLA Ops:
  6.5 62.0 %all-gather.4.cloned.1.call-start = ((), (), s32[]{:S(2)}) async-start(), calls=%async_computation | async-start | bytes 10027008 | tf_op jit(solution)/shard_map/all_gather | solution.py:76
  7.3 399.7 %all-gather.6.cloned.1.call-start = ((), (), s32[]{:S(2)}) async-start(), calls=%async_computation.1 | async-start | bytes 7962624 | tf_op jit(solution)/shard_map/all_gather | solution.py:99
Sparse Core Ops, SparseCore 0:
  9.0 59.4 all-gather.3
  310.4 96.5 all-gather.5
where the time goes:
time: 422 us; the launch traced here: 420 us
  waiting for transfers between devices  157 us (37%)
  other arithmetic  109 us (26%)
  local copies, waits for them, and re-layouts  105 us (25%)
  matrix products  32.4 us (8%)
  between operations  13.4 us (3%)
    all_gather x1, waiting for transfers between devices, body(): gathered = lax.all_gather(finished[None], 'tm', axis=0, tiled=True)  96.7 us
    another operation x16, other arithmetic  71.1 us
    all_gather x1, waiting for transfers between devices, body(): lax.all_gather(local.reshape(6 * nvec, sites), 'space', axis=1, tiled=True)  59.7 us
    dot_general x16, matrix products, advance(): jnp.einsum('imjqcg,qcrkg->imjrk', crossed, mixing(vec_block), preferred_e...  32.4 us
    reshape x16, local copies, waits for them, and re-layouts, advance(): return acc + part.reshape(rows, moments, width)  25.2 us
    gather x32, local copies, waits for them, and re-layouts, advance(): jnp.take(offsets, brick_ids, axis=0)  18.3 us
    dynamic_slice x16, local copies, waits for them, and re-layouts, advance(): lax.dynamic_slice_in_dim(vec_piece, index * block, block, 1)  17.7 us
    slice x16, local copies, waits for them, and re-layouts, cross_rows(): real_v = vecs[0].astype(jnp.float32)  17.6 us
  transfers between devices with their start and end apart: 2, of which 2 were waited for; matrix products, arithmetic and copies ran while one was open for 0% of the time, Pallas kernels for 0%

commit v1 on v0

v1 whole, which is shorter than its diff:
```python
import math

import jax
import jax.numpy as jnp
from jax import lax
from jax.experimental import pallas as pl
from jax.experimental.pallas import tpu as pltpu
from jax.sharding import PartitionSpec as P

LAT = 64
BRICK = 8
BRICK_Z = 8
LANES = 128
ORDER = ((0, 1, 2, 3), (2, 0, 3, 1))
GROUP = 4


def local_coords(site):
    return jnp.stack([site // (BRICK * BRICK_Z), site // BRICK_Z % BRICK, site % BRICK_Z])


def phases(momenta, coords):
    product = jnp.sum(momenta[:, :, None] * coords[None, :, :], axis=1)
    angle = (product % LAT).astype(jnp.float32) * (2.0 * math.pi / LAT)
    return jnp.stack([jnp.cos(angle), jnp.sin(angle)], axis=1)


def cross(j, k):
    real, imag = [], []
    for colour in range(3):
        a, b = (colour + 1) % 3, (colour + 2) % 3
        real.append(
            (j[0][a] * k[0][b] - j[1][a] * k[1][b]) - (j[0][b] * k[0][a] - j[1][b] * k[1][a])
        )
        imag.append(
            (j[0][a] * k[1][b] + j[1][a] * k[0][b]) - (j[0][b] * k[1][a] + j[1][b] * k[0][a])
        )
    return real + imag


def pair_kernel(quarter_ref, own_ref, sib_ref, phase_ref, out_ref, vec_ref, mix_ref, pair_ref, acc_ref):
    nvec = own_ref.shape[1]
    sites = own_ref.shape[2]
    fourth = nvec // 4
    chunks = 2 * sites // LANES
    wide = 6 * LANES
    for half, ref in enumerate((own_ref, sib_ref)):
        for step in range(sites // LANES):
            here = pl.ds(step * LANES, LANES)
            chunk = half * (sites // LANES) + step
            there = pl.ds(chunk * LANES, LANES)
            phase = [phase_ref[pl.ds(n, 1), there] for n in range(4)]
            for colour in range(3):
                real = ref[colour, :, here].astype(jnp.float32)
                imag = ref[3 + colour, :, here].astype(jnp.float32)
                for p in range(2):
                    cosine, sine = phase[2 * p], phase[2 * p + 1]
                    w_real = (cosine * real - sine * imag).astype(jnp.bfloat16)
                    w_imag = (cosine * imag + sine * real).astype(jnp.bfloat16)
                    first = pl.ds(2 * p * nvec, nvec)
                    second = pl.ds((2 * p + 1) * nvec, nvec)
                    on_real = pl.ds(colour * LANES, LANES)
                    on_imag = pl.ds((3 + colour) * LANES, LANES)
                    mix_ref[chunk, first, on_real] = w_real
                    mix_ref[chunk, second, on_real] = w_imag
                    mix_ref[chunk, first, on_imag] = -w_imag
                    mix_ref[chunk, second, on_imag] = w_real
            for m in range(4):
                rows = pl.ds(pl.multiple_of(quarter_ref[m], 8), fourth)
                for part in range(6):
                    vec_ref[chunk, part, pl.ds(m * fourth, fourth), :] = ref[
                        part, rows, here
                    ].astype(jnp.float32)
    acc_ref[...] = jnp.zeros_like(acc_ref)

    def advance(chunk, carry):
        def rows_of(first, count):
            return [
                [vec_ref[chunk, 3 * part + c, pl.ds(first, count), :] for c in range(3)]
                for part in range(2)
            ]

        for group in range(fourth // GROUP):
            for local in range(GROUP):
                r = group * GROUP + local
                pieces = [[] for _ in range(6)]
                for m in range(3):
                    found = cross(rows_of(m * fourth + r, 1), rows_of((m + 1) * fourth, fourth))
                    for n in range(6):
                        pieces[n].append(found[n])
                for unit in range(fourth // 8):
                    low = unit * 8
                    if low + 7 > r:
                        upper = cross(rows_of(r, 1), rows_of(low, 8))
                    if low < r:
                        lower = cross(rows_of(3 * fourth + r, 1), rows_of(3 * fourth + low, 8))
                    if low >= r:
                        found = upper
                    elif low + 7 <= r:
                        found = lower
                    else:
                        above = lax.broadcasted_iota(jnp.int32, (8, LANES), 0) > r - low
                        found = [jnp.where(above, u, w) for u, w in zip(upper, lower)]
                    for n in range(6):
                        pieces[n].append(found[n])
                for n in range(6):
                    pair_ref[
                        group, pl.ds(local * nvec, nvec), pl.ds(n * LANES, LANES)
                    ] = jnp.concatenate(pieces[n], axis=0).astype(jnp.bfloat16)
            width = GROUP * nvec
            cols = pl.ds(group * width, width)
            acc_ref[:, cols] += lax.dot_general(
                mix_ref[chunk],
                pair_ref[group],
                (((1,), (1,)), ((), ())),
                preferred_element_type=jnp.float32,
            )
        return carry

    lax.fori_loop(0, chunks, advance, 0)
    row = lax.broadcasted_iota(jnp.int32, (4 * nvec, 4 * nvec), 0)
    col = lax.broadcasted_iota(jnp.int32, (4 * nvec, 4 * nvec), 1)
    perm = jnp.where(col == (row % 4) * nvec + row // 4, 1.0, 0.0).astype(jnp.bfloat16)
    for group in range(fourth // GROUP):
        width = GROUP * nvec
        cols = pl.ds(group * width, width)
        out_ref[:, cols] = jnp.dot(
            perm, acc_ref[:, cols].astype(jnp.bfloat16), preferred_element_type=jnp.float32
        ).astype(jnp.bfloat16)


def pair_sums(quarters, own, sib, phase):
    nvec, sites = own.shape[1], own.shape[2]
    chunks = 2 * sites // LANES
    pairs = nvec // 4 * nvec
    vmem = pl.BlockSpec(memory_space=pltpu.VMEM)
    return pl.pallas_call(
        pair_kernel,
        out_shape=jax.ShapeDtypeStruct((4 * nvec, pairs), jnp.bfloat16),
        in_specs=[pl.BlockSpec(memory_space=pltpu.SMEM), vmem, vmem, vmem],
        out_specs=vmem,
        scratch_shapes=[
            pltpu.VMEM((chunks, 6, nvec, LANES), jnp.float32),
            pltpu.VMEM((chunks, 4 * nvec, 6 * LANES), jnp.bfloat16),
            pltpu.VMEM((nvec // 4 // GROUP, GROUP * nvec, 6 * LANES), jnp.bfloat16),
            pltpu.VMEM((4 * nvec, pairs), jnp.float32),
        ],
        compiler_params=pltpu.CompilerParams(vmem_limit_bytes=48 << 20),
        name="pair_sums",
    )(quarters, own, sib, phase)


def assemble(found):
    b = [[found[..., c, :, m, :] for m in range(4)] for c in range(2)]
    t = [[-jnp.swapaxes(b[c][m], -1, -2) for m in range(4)] for c in range(2)]
    n = found.shape[-1]
    upper = jnp.arange(n)[None, :] > jnp.arange(n)[:, None]
    lower = jnp.arange(n)[None, :] < jnp.arange(n)[:, None]
    d0 = jnp.where(upper, b[0][3], t[0][3])
    d3 = jnp.where(lower, b[0][3], t[0][3])
    d2 = jnp.where(upper, b[1][3], t[1][3])
    d1 = jnp.where(lower, b[1][3], t[1][3])
    rows = [
        [d0, b[0][0], t[1][0], b[1][1]],
        [t[0][0], d1, b[0][1], t[1][2]],
        [b[1][0], t[0][1], d2, b[0][2]],
        [t[1][1], b[1][2], t[0][2], d3],
    ]
    return jnp.concatenate([jnp.concatenate(row, axis=-1) for row in rows], axis=-2)


def body(vectors, momenta, offsets):
    nvec, sites = vectors.shape[3], vectors.shape[4]
    groups = lax.axis_size("space")
    times = lax.axis_size("tm")
    rows = nvec // groups
    fourth = nvec // 4
    place = lax.axis_index("space")
    own = vectors.reshape(6, nvec, sites)
    sib = lax.ppermute(own, "space", [(n, n ^ 1) for n in range(groups)])
    corner = jnp.stack([offsets[place], offsets[place ^ 1]])
    coords = (
        local_coords(jnp.arange(sites, dtype=jnp.int32))[:, None, :]
        + jnp.transpose(corner)[:, :, None]
    ).reshape(3, 2 * sites)
    phase = phases(momenta, coords).reshape(4, 2 * sites)
    quarters = jnp.where(
        place % 2 == 0,
        jnp.array([fourth * n for n in ORDER[0]], jnp.int32),
        jnp.array([fourth * n for n in ORDER[1]], jnp.int32),
    )
    partial = pair_sums(quarters, own, sib, phase)
    parts = lax.all_to_all(partial.reshape(groups, 4 * rows, -1), "space", 0, 0, tiled=False)
    parts = parts.reshape(groups // 2, 2, 4 * rows, -1).astype(jnp.float32)
    mine = (jnp.sum(parts, axis=0) * (1.0 / math.sqrt(sites * groups))).astype(jnp.bfloat16)
    pieces = [mine] + [
        lax.ppermute(mine, "tm", [(n, n ^ s) for n in range(times)]) for s in range(1, times)
    ]
    me = lax.axis_index("tm")
    whole = jnp.zeros((times,) + mine.shape, mine.dtype)
    for s, piece in enumerate(pieces):
        whole = lax.dynamic_update_slice_in_dim(whole, piece[None], me ^ s, 0)
    found = whole.reshape(times, 2, rows, 2, 2, fourth, 4, fourth)
    found = jnp.transpose(found, (0, 2, 3, 4, 1, 5, 6, 7))
    full = assemble(found)
    full = jnp.transpose(full, (0, 1, 2, 4, 3, 5)).astype(jnp.float32)
    return full.reshape(times, rows, 2, 2 * nvec * nvec)


def solution(mesh):
    return jax.shard_map(
        body,
        mesh=mesh,
        in_specs=(P("tm", None, None, None, "space"), P(), P()),
        out_specs=P(None, "space", None, None),
        check_vma=False,
    )
```

time: 422 us -> 254 us (0.60)
  waiting for transfers between devices: 157 us -> 41.7 us
  other arithmetic: 109 us -> 19.4 us
  matrix products: 32.4 us -> 0 us
  local copies, waits for them, and re-layouts: 105 us -> 137 us
  Pallas kernels: 0 us -> 31 us
  starting transfers between devices: 0.04 us -> 21.8 us
  between operations: 13.4 us -> 0.24 us
    all_gather x2 -> x0, waiting for transfers between devices: 156 us -> none  [the longest x1 96.7 us: body(): gathered = lax.all_gather(finished[None], 'tm', axis=0, tiled=True)]
    another operation x64 -> x2, other arithmetic: 86.6 us -> 0.02 us  [the longest x1 0.01 us: local_coords(): jnp.stack([site // (BRICK * BRICK_Z), site // BRICK_Z % BRICK, site % BRI...]
    unnamed x3 -> x46, local copies, waits for them, and re-layouts: 7.95 us -> 64.2 us
    dot_general x16 -> x0, matrix products: 32.4 us -> none  [advance(): jnp.einsum('imjqcg,qcrkg->imjrk', crossed, mixing(vec_block), preferred_e...]
    pallas_call x0 -> x1, Pallas kernels: none -> 31 us  [pair_sums(): pl.pallas_call(pair_kernel, out_shape=jax.ShapeDtypeStruct((4 * nvec, pai...]
    all_to_all x0 -> x1, waiting for transfers between devices: none -> 24.9 us  [body(): lax.all_to_all(partial.reshape(groups, 4 * rows, -1), 'space', 0, 0, tile...]
    gather x32 -> x0, local copies, waits for them, and re-layouts: 18.3 us -> none  [advance(): jnp.take(offsets, brick_ids, axis=0)]
    reshape x16 -> x4, local copies, waits for them, and re-layouts: 25.2 us -> 43 us  [the longest x2 26.8 us: body(): return full.reshape(times, rows, 2, 2 * nvec * nvec)]
  transfers between devices with their start and end apart: 2 -> 9, of which waited for: 2 -> 5; matrix products, arithmetic and copies ran while one was open for 0% -> 1% of each run, Pallas kernels for 0% -> 0%
where the time goes in v1:
time: 254 us; the launch traced here: 251 us
  local copies, waits for them, and re-layouts  137 us (54%)
  waiting for transfers between devices  41.7 us (16%)
  Pallas kernels  31 us (12%)
  starting transfers between devices  21.8 us (9%)
  other arithmetic  19.4 us (8%)
    unnamed x46, local copies, waits for them, and re-layouts  64.2 us
    pallas_call x1, Pallas kernels, pair_sums(): pl.pallas_call(pair_kernel, out_shape=jax.ShapeDtypeStruct((4 * nvec, pai...  31 us
    slice x1, local copies, waits for them, and re-layouts, assemble(): b = [[found[..., c, :, m, :] for m in range(4)] for c in range(2)]  28.6 us
    reshape x2, local copies, waits for them, and re-layouts, body(): return full.reshape(times, rows, 2, 2 * nvec * nvec)  26.8 us
    all_to_all x1, waiting for transfers between devices, body(): lax.all_to_all(partial.reshape(groups, 4 * rows, -1), 'space', 0, 0, tile...  24.9 us
    ppermute x7, waiting for transfers between devices, body(): lax.ppermute(mine, 'tm', [(n, n ^ s) for n in range(times)])  16.8 us
    reshape x1, local copies, waits for them, and re-layouts, body(): found = whole.reshape(times, 2, rows, 2, 2, fourth, 4, fourth)  16.1 us
    ppermute x7, starting transfers between devices, body(): lax.ppermute(mine, 'tm', [(n, n ^ s) for n in range(times)])  15.5 us
  transfers between devices with their start and end apart: 9, of which 5 were waited for; matrix products, arithmetic and copies ran while one was open for 1% of the time, Pallas kernels for 0%

profile of v1, /device:TPU:0, one launch (start us, length us, event | category | flops | bytes accessed | tf_op | source)
XLA Modules:
  0.0 251.0 jit_solution(6707144029502297088)
XLA Ops:
  3.3 31.0 %pair_sums.1 = bf16[384,2304]{1,0:T(8,128)(2,1)} custom-call(s32[4]{0:T(128)S(1)} %broadcast_select_fusion.quarter_ref, bf16[6,96,512]{2,1,0:T(8,128)(2,1)S(1)} %bitcast.125, bf16[6,96,512]{2,1,0:T(8,128)(2,1)S(1)} %collective-permute-done.sib_ref, f32[4,1024]{1,0:T(4,128)S(1)} %reshape.213.phase_ref), custom_call_target="tpu_custom_call" | custom-call | tf_op jit(solution)/shard_map/pair_sums/pallas_call | solution.py:137
  34.2 6.3 %all-to-all-start = ((bf16[16,24,2304]{2,1,0:T(8,128)(2,1)}), bf16[16,24,2304]{2,1,0:T(8,128)(2,1)S(1)}, u32[]{:S(2)}, u32[]{:S(2)}) async-start(bf16[16,24,2304]{2,1,0:T(8,128)(2,1)} %bitcast.3), calls=%async_computation | async-start | bytes 3538944 | tf_op jit(solution)/shard_map/all_to_all | solution.py:193
  40.5 24.9 %all-to-all-done = bf16[16,24,2304]{2,1,0:T(8,128)(2,1)S(1)} async-done(((bf16[16,24,2304]{2,1,0:T(8,128)(2,1)}), bf16[16,24,2304]{2,1,0:T(8,128)(2,1)S(1)}, u32[]{:S(2)}, u32[]{:S(2)}) %all-to-all-start) | async-done | bytes 1769504 | tf_op jit(solution)/shard_map/all_to_all | solution.py:193
  65.8 2.0 collective-permute-start.1
  67.8 3.7 %collective-permute-start.2 = (bf16[2,24,2304]{2,1,0:T(8,128)(2,1)S(1)}, bf16[2,24,2304]{2,1,0:T(8,128)(2,1)S(1)}, u32[]{:S(2)}, u32[]{:S(2)}) collective-permute-start(bf16[2,24,2304]{2,1,0:T(8,128)(2,1)S(1)} %get-tuple-element.6), channel_id=1, source_target_pairs={{0,2},{1,3},{2,0},{3,1},{4,6},{5,7},{6,4},{7,5},{8,10},{9,11},{10,... | collective-permute-start | bytes 663560 | tf_op jit(solution)/shard_map/ppermute | solution.py:197
  71.5 2.7 %collective-permute-start.4 = (bf16[2,24,2304]{2,1,0:T(8,128)(2,1)S(1)}, bf16[2,24,2304]{2,1,0:T(8,128)(2,1)S(1)}, u32[]{:S(2)}, u32[]{:S(2)}) collective-permute-start(bf16[2,24,2304]{2,1,0:T(8,128)(2,1)S(1)} %get-tuple-element.6), channel_id=1, source_target_pairs={{0,4},{1,5},{2,6},{3,7},{4,0},{5,1},{6,2},{7,3},{8,12},{9,13},{10,... | collective-permute-start | bytes 663560 | tf_op jit(solution)/shard_map/ppermute | solution.py:197
  74.5 6.8 %collective-permute-start.6 = (bf16[2,24,2304]{2,1,0:T(8,128)(2,1)S(1)}, bf16[2,24,2304]{2,1,0:T(8,128)(2,1)S(1)}, u32[]{:S(2)}, u32[]{:S(2)}) collective-permute-start(bf16[2,24,2304]{2,1,0:T(8,128)(2,1)S(1)} %get-tuple-element.6), channel_id=1, source_target_pairs={{0,6},{1,7},{2,4},{3,5},{4,2},{5,3},{6,0},{7,1},{8,14},{9,15},{10,... | collective-permute-start | bytes 663560 | tf_op jit(solution)/shard_map/ppermute | solution.py:197
  81.3 7.4 %collective-permute-done.2 = bf16[2,24,2304]{2,1,0:T(8,128)(2,1)S(1)} collective-permute-done((bf16[2,24,2304]{2,1,0:T(8,128)(2,1)S(1)}, bf16[2,24,2304]{2,1,0:T(8,128)(2,1)S(1)}, u32[]{:S(2)}, u32[]{:S(2)}) %collective-permute-start.2) | collective-permute-done | bytes 221216 | tf_op jit(solution)/shard_map/ppermute | solution.py:197
  88.9 3.5 %collective-permute-done.6 = bf16[2,24,2304]{2,1,0:T(8,128)(2,1)S(1)} collective-permute-done((bf16[2,24,2304]{2,1,0:T(8,128)(2,1)S(1)}, bf16[2,24,2304]{2,1,0:T(8,128)(2,1)S(1)}, u32[]{:S(2)}, u32[]{:S(2)}) %collective-permute-start.6) | collective-permute-done | bytes 221216 | tf_op jit(solution)/shard_map/ppermute | solution.py:197
  92.4 5.9 %collective-permute-done.7 = bf16[2,24,2304]{2,1,0:T(8,128)(2,1)S(1)} collective-permute-done((bf16[2,24,2304]{2,1,0:T(8,128)(2,1)S(1)}, bf16[2,24,2304]{2,1,0:T(8,128)(2,1)S(1)}, u32[]{:S(2)}, u32[]{:S(2)}) %collective-permute-start.7) | collective-permute-done | bytes 221216 | tf_op jit(solution)/shard_map/ppermute | solution.py:197
  98.3 16.1 %reshape.215 = bf16[8,2,6,2,2,24,4,24]{7,6,5,4,3,2,1,0:T(4,128)(2,1)} reshape(bf16[8,2,24,2304]{3,2,1,0:T(8,128)(2,1)S(1)} %bitcast_dynamic-update-slice_fusion) | data formatting | bytes 3538944 | tf_op jit(solution)/shard_map/reshape | solution.py:203
  114.5 28.6 %fusion.14 = (bf16[8,6,2,2,1,24,1,24]{7,6,5,3,2,1,4,0:T(2,128)(2,1)S(1)}, bf16[8,6,2,2,1,24,1,24]{7,6,5,3,2,1,4,0:T(2,128)(2,1)}, bf16[8,6,2,2,1,24,1,24]{7,6,5,...) fusion(bf16[8,6,2,2,2,24,4,24]{7,6,5,3,2,1,4,0:T(4,128)(2,1)} %, ...), kind=kLoop, calls=%fused_computation.67 | loop fusion | bytes 3538944 | tf_op jit(solution)/shard_map/slice | solution.py:154
  143.1 5.9 %copy.175 = bf16[8,6,2,2,1,24,1,24]{5,7,3,2,1,0,4,6:T(8,128)(2,1)} copy(bf16[8,6,2,2,1,24,1,24]{7,6,5,3,2,1,4,0:T(2,128)(2,1)} %get-tuple-element.8) | data formatting | bytes 442368
  149.0 1.9 copy.187
  150.8 5.9 %copy.172 = bf16[8,6,2,2,1,24,1,24]{5,7,3,2,1,0,4,6:T(8,128)(2,1)} copy(bf16[8,6,2,2,1,24,1,24]{7,6,5,3,2,1,4,0:T(2,128)(2,1)} %get-tuple-element.9) | data formatting | bytes 442368
  156.7 2.9 %copy.188 = bf16[8,6,2,2,1,24,1,24]{7,5,6,3,2,1,4,0:T(8,128)(2,1)} copy(bf16[8,6,2,2,1,24,1,24]{7,6,5,3,2,1,4,0:T(2,128)(2,1)} %get-tuple-element.9) | data formatting | bytes 442368
  159.7 5.9 %copy.173 = bf16[8,6,2,2,1,24,1,24]{5,7,3,2,1,0,4,6:T(8,128)(2,1)} copy(bf16[8,6,2,2,1,24,1,24]{7,6,5,3,2,1,4,0:T(2,128)(2,1)} %get-tuple-element.10) | data formatting | bytes 442368
  165.6 2.9 %copy.189 = bf16[8,6,2,2,1,24,1,24]{7,5,6,3,2,1,4,0:T(8,128)(2,1)} copy(bf16[8,6,2,2,1,24,1,24]{7,6,5,3,2,1,4,0:T(2,128)(2,1)} %get-tuple-element.10) | data formatting | bytes 442368
  168.5 5.9 %copy.174 = bf16[8,6,2,2,1,24,1,24]{5,7,3,2,1,0,4,6:T(8,128)(2,1)} copy(bf16[8,6,2,2,1,24,1,24]{7,6,5,3,2,1,4,0:T(2,128)(2,1)} %get-tuple-element.12) | data formatting | bytes 442368
  174.3 2.9 %copy.190 = bf16[8,6,2,2,1,24,1,24]{7,5,6,3,2,1,4,0:T(8,128)(2,1)} copy(bf16[8,6,2,2,1,24,1,24]{7,6,5,3,2,1,4,0:T(2,128)(2,1)} %get-tuple-element.12) | data formatting | bytes 442368
  177.2 5.9 %copy.169 = bf16[8,6,2,2,1,24,1,24]{5,7,3,2,1,0,4,6:T(8,128)(2,1)} copy(bf16[8,6,2,2,1,24,1,24]{7,6,5,3,2,1,4,0:T(2,128)(2,1)} %get-tuple-element.13) | data formatting | bytes 442368
  183.1 2.9 %copy.191 = bf16[8,6,2,2,1,24,1,24]{7,5,6,3,2,1,4,0:T(8,128)(2,1)} copy(bf16[8,6,2,2,1,24,1,24]{7,6,5,3,2,1,4,0:T(2,128)(2,1)} %get-tuple-element.13) | data formatting | bytes 442368
  186.0 3.4 %copy.170 = bf16[8,6,2,2,1,24,1,24]{5,7,3,2,1,0,4,6:T(8,128)(2,1)} copy(bf16[8,6,2,2,1,24,1,24]{7,6,5,3,2,1,4,0:T(2,128)(2,1)S(1)} %get-tuple-element.7) | data formatting | bytes 442368
  189.4 1.2 copy.192
  190.7 6.0 %copy.168 = bf16[8,6,2,2,1,24,1,24]{5,7,3,2,1,0,4,6:T(8,128)(2,1)} copy(bf16[8,6,2,2,1,24,1,24]{7,6,5,3,2,1,4,0:T(2,128)(2,1)} %get-tuple-element.14) | data formatting | bytes 442368
  196.7 3.4 %copy.171 = bf16[8,6,2,2,1,24,1,24]{5,7,3,2,1,0,4,6:T(8,128)(2,1)} copy(bf16[8,6,2,2,1,24,1,24]{7,6,5,3,2,1,4,0:T(2,128)(2,1)S(1)} %copy-done.1) | data formatting | bytes 442368
  200.2 1.5 fusion
  206.5 1.3 fusion.5
  207.7 1.2 fusion.6
  212.7 11.5 %convert_bitcast_fusion = f32[8,6,2,96,2,96]{5,3,4,2,1,0:T(8,128)S(1)} fusion(bf16[8,6,2,2,24,24]{5,4,3,2,1,0:T(8,128)(2,1)S(1)} %get-tuple-element.21, bf16[8,6,2,2,24,24]{5,4,3,2,1,0:T(8,128)(2,1)S(1)} %fusion, bf16[8,6,2,2,24,24]{5,4,3,2,1,0:T(8,128)(2,1)S(1)} %bitcast.129, bf16[8,6,2,2,24,24]{5,4,3,2,1,0:T(8,128)(2,1)S(1)} %fusion.1, ...), kind=kLoop, calls=%fused_computation | loop fusion | flops 56623104 | bytes 10616832 | tf_op jit(solution)/shard_map/reshape | solution.py:207
  224.2 11.0 %copy.158 = f32[8,6,2,96,2,96]{5,4,3,2,1,0:T(2,128)} copy(f32[8,6,2,96,2,96]{5,3,4,2,1,0:T(8,128)S(1)} %convert_bitcast_fusion) | data formatting | bytes 14155776 | tf_op jit(solution)/shard_map/reshape | solution.py:207
  235.2 15.9 %reshape.222 = f32[8,6,2,18432]{3,2,1,0:T(2,128)} reshape(f32[8,6,2,96,2,96]{5,4,3,2,1,0:T(2,128)} %copy.158) | data formatting | bytes 14155776 | tf_op jit(solution)/shard_map/reshape | solution.py:207
  (68 shorter events, 12.5 us)
Async XLA Ops:
  0.0 2.2 collective-permute-start
  2.2 1.1 copy-start
  34.2 31.2 %all-to-all-start = ((bf16[16,24,2304]{2,1,0:T(8,128)(2,1)}), bf16[16,24,2304]{2,1,0:T(8,128)(2,1)S(1)}, u32[]{:S(2)}, u32[]{:S(2)}) async-start(bf16[16,24,2304]{2,1,0:T(8,128)(2,1)} %bitcast.3), calls=%async_computation | async-start | bytes 3538944 | tf_op jit(solution)/shard_map/all_to_all | solution.py:193
  65.8 8.7 %collective-permute-start.1 = (bf16[2,24,2304]{2,1,0:T(8,128)(2,1)S(1)}, bf16[2,24,2304]{2,1,0:T(8,128)(2,1)S(1)}, u32[]{:S(2)}, u32[]{:S(2)}) collective-permute-start(bf16[2,24,2304]{2,1,0:T(8,128)(2,1)S(1)} %get-tuple-element.6), channel_id=1, source_target_pairs={{0,1},{1,0},{2,3},{3,2},{4,5},{5,4},{6,7},{7,6},{8,9},{9,8},{10,11... | collective-permute-start | bytes 663560 | tf_op jit(solution)/shard_map/ppermute | solution.py:197
  67.8 20.9 %collective-permute-start.2 = (bf16[2,24,2304]{2,1,0:T(8,128)(2,1)S(1)}, bf16[2,24,2304]{2,1,0:T(8,128)(2,1)S(1)}, u32[]{:S(2)}, u32[]{:S(2)}) collective-permute-start(bf16[2,24,2304]{2,1,0:T(8,128)(2,1)S(1)} %get-tuple-element.6), channel_id=1, source_target_pairs={{0,2},{1,3},{2,0},{3,1},{4,6},{5,7},{6,4},{7,5},{8,10},{9,11},{10,... | collective-permute-start | bytes 663560 | tf_op jit(solution)/shard_map/ppermute | solution.py:197
  71.5 17.3 %collective-permute-start.3 = (bf16[2,24,2304]{2,1,0:T(8,128)(2,1)S(1)}, bf16[2,24,2304]{2,1,0:T(8,128)(2,1)S(1)}, u32[]{:S(2)}, u32[]{:S(2)}) collective-permute-start(bf16[2,24,2304]{2,1,0:T(8,128)(2,1)S(1)} %get-tuple-element.6), channel_id=1, source_target_pairs={{0,3},{1,2},{2,1},{3,0},{4,7},{5,6},{6,5},{7,4},{8,11},{9,10},{10,... | collective-permute-start | bytes 663560 | tf_op jit(solution)/shard_map/ppermute | solution.py:197
  71.5 17.3 %collective-permute-start.4 = (bf16[2,24,2304]{2,1,0:T(8,128)(2,1)S(1)}, bf16[2,24,2304]{2,1,0:T(8,128)(2,1)S(1)}, u32[]{:S(2)}, u32[]{:S(2)}) collective-permute-start(bf16[2,24,2304]{2,1,0:T(8,128)(2,1)S(1)} %get-tuple-element.6), channel_id=1, source_target_pairs={{0,4},{1,5},{2,6},{3,7},{4,0},{5,1},{6,2},{7,3},{8,12},{9,13},{10,... | collective-permute-start | bytes 663560 | tf_op jit(solution)/shard_map/ppermute | solution.py:197
  74.2 14.6 %collective-permute-start.5 = (bf16[2,24,2304]{2,1,0:T(8,128)(2,1)S(1)}, bf16[2,24,2304]{2,1,0:T(8,128)(2,1)S(1)}, u32[]{:S(2)}, u32[]{:S(2)}) collective-permute-start(bf16[2,24,2304]{2,1,0:T(8,128)(2,1)S(1)} %get-tuple-element.6), channel_id=1, source_target_pairs={{0,5},{1,4},{2,7},{3,6},{4,1},{5,0},{6,3},{7,2},{8,13},{9,12},{10,... | collective-permute-start | bytes 663560 | tf_op jit(solution)/shard_map/ppermute | solution.py:197
  74.5 17.9 %collective-permute-start.6 = (bf16[2,24,2304]{2,1,0:T(8,128)(2,1)S(1)}, bf16[2,24,2304]{2,1,0:T(8,128)(2,1)S(1)}, u32[]{:S(2)}, u32[]{:S(2)}) collective-permute-start(bf16[2,24,2304]{2,1,0:T(8,128)(2,1)S(1)} %get-tuple-element.6), channel_id=1, source_target_pairs={{0,6},{1,7},{2,4},{3,5},{4,2},{5,3},{6,0},{7,1},{8,14},{9,15},{10,... | collective-permute-start | bytes 663560 | tf_op jit(solution)/shard_map/ppermute | solution.py:197
  88.8 9.5 %collective-permute-start.7 = (bf16[2,24,2304]{2,1,0:T(8,128)(2,1)S(1)}, bf16[2,24,2304]{2,1,0:T(8,128)(2,1)S(1)}, u32[]{:S(2)}, u32[]{:S(2)}) collective-permute-start(bf16[2,24,2304]{2,1,0:T(8,128)(2,1)S(1)} %get-tuple-element.6), channel_id=1, source_target_pairs={{0,7},{1,6},{2,5},{3,4},{4,3},{5,2},{6,1},{7,0},{8,15},{9,14},{10,... | collective-permute-start | bytes 663560 | tf_op jit(solution)/shard_map/ppermute | solution.py:197
  190.7 6.1 %copy-start.1 = (bf16[8,6,2,2,1,24,1,24]{7,6,5,3,2,1,4,0:T(2,128)(2,1)S(1)}, bf16[8,6,2,2,1,24,1,24]{7,6,5,3,2,1,4,0:T(2,128)(2,1)}, u32[]{:S(2)}) copy-start(bf16[8,6,2,2,1,24,1,24]{7,6,5,3,2,1,4,0:T(2,128)(2,1)} %get-tuple-element.11) | copy-start | bytes 663556
  200.2 1.6 copy-start.13
  201.8 1.3 copy-start.11
  203.1 1.7 copy-start.10
  204.8 1.7 copy-start.14
  204.8 3.0 %copy-start.12 = (bf16[8,6,2,2,1,24,1,24]{5,7,3,2,1,0,4,6:T(8,128)(2,1)S(1)}, bf16[8,6,2,2,1,24,1,24]{5,7,3,2,1,0,4,6:T(8,128)(2,1)}, u32[]{:S(2)}) copy-start(bf16[8,6,2,2,1,24,1,24]{5,7,3,2,1,0,4,6:T(8,128)(2,1)} %copy.169) | copy-start | bytes 663556
  206.5 2.5 %copy-start.8 = (bf16[8,6,2,2,1,24,1,24]{5,7,3,2,1,0,4,6:T(8,128)(2,1)S(1)}, bf16[8,6,2,2,1,24,1,24]{5,7,3,2,1,0,4,6:T(8,128)(2,1)}, u32[]{:S(2)}) copy-start(bf16[8,6,2,2,1,24,1,24]{5,7,3,2,1,0,4,6:T(8,128)(2,1)} %copy.168) | copy-start | bytes 663556
  206.5 2.5 %copy-start.9 = (bf16[8,6,2,2,1,24,1,24]{5,7,3,2,1,0,4,6:T(8,128)(2,1)S(1)}, bf16[8,6,2,2,1,24,1,24]{5,7,3,2,1,0,4,6:T(8,128)(2,1)}, u32[]{:S(2)}) copy-start(bf16[8,6,2,2,1,24,1,24]{5,7,3,2,1,0,4,6:T(8,128)(2,1)} %copy.171) | copy-start | bytes 663556
  207.7 2.3 copy-start.2
  210.0 1.3 copy-start.3
  210.0 1.6 copy-start.4
  210.0 2.0 copy-start.5
  210.0 2.3 copy-start.6
  210.0 2.7 %copy-start.7 = (bf16[8,6,2,2,1,24,1,24]{7,5,6,3,2,1,4,0:T(8,128)(2,1)S(1)}, bf16[8,6,2,2,1,24,1,24]{7,5,6,3,2,1,4,0:T(8,128)(2,1)}, u32[]{:S(2)}) copy-start(bf16[8,6,2,2,1,24,1,24]{7,5,6,3,2,1,4,0:T(8,128)(2,1)} %copy.192) | copy-start | bytes 663556

commit v2 on v1

--- a/solution.py
+++ b/solution.py
@@ -1,3 +1,4 @@
+import functools
 import math
 
 import jax
@@ -13,6 +14,7 @@
 LANES = 128
 ORDER = ((0, 1, 2, 3), (2, 0, 3, 1))
 GROUP = 4
+OWNERS = 16
 
 
 def local_coords(site):
@@ -84,10 +86,6 @@
             for local in range(GROUP):
                 r = group * GROUP + local
                 pieces = [[] for _ in range(6)]
-                for m in range(3):
-                    found = cross(rows_of(m * fourth + r, 1), rows_of((m + 1) * fourth, fourth))
-                    for n in range(6):
-                        pieces[n].append(found[n])
                 for unit in range(fourth // 8):
                     low = unit * 8
                     if low + 7 > r:
@@ -103,6 +101,10 @@
                         found = [jnp.where(above, u, w) for u, w in zip(upper, lower)]
                     for n in range(6):
                         pieces[n].append(found[n])
+                for m in range(3):
+                    found = cross(rows_of(m * fourth + r, 1), rows_of((m + 1) * fourth, fourth))
+                    for n in range(6):
+                        pieces[n].append(found[n])
                 for n in range(6):
                     pair_ref[
                         group, pl.ds(local * nvec, nvec), pl.ds(n * LANES, LANES)
@@ -120,7 +122,9 @@
     lax.fori_loop(0, chunks, advance, 0)
     row = lax.broadcasted_iota(jnp.int32, (4 * nvec, 4 * nvec), 0)
     col = lax.broadcasted_iota(jnp.int32, (4 * nvec, 4 * nvec), 1)
-    perm = jnp.where(col == (row % 4) * nvec + row // 4, 1.0, 0.0).astype(jnp.bfloat16)
+    own = nvec // OWNERS
+    source = row % (4 * own) // own * nvec + row // (4 * own) * own + row % own
+    perm = jnp.where(col == source, 1.0, 0.0).astype(jnp.bfloat16)
     for group in range(fourth // GROUP):
         width = GROUP * nvec
         cols = pl.ds(group * width, width)
@@ -150,23 +154,169 @@
     )(quarters, own, sib, phase)
 
 
-def assemble(found):
-    b = [[found[..., c, :, m, :] for m in range(4)] for c in range(2)]
-    t = [[-jnp.swapaxes(b[c][m], -1, -2) for m in range(4)] for c in range(2)]
-    n = found.shape[-1]
-    upper = jnp.arange(n)[None, :] > jnp.arange(n)[:, None]
-    lower = jnp.arange(n)[None, :] < jnp.arange(n)[:, None]
-    d0 = jnp.where(upper, b[0][3], t[0][3])
-    d3 = jnp.where(lower, b[0][3], t[0][3])
-    d2 = jnp.where(upper, b[1][3], t[1][3])
-    d1 = jnp.where(lower, b[1][3], t[1][3])
-    rows = [
-        [d0, b[0][0], t[1][0], b[1][1]],
-        [t[0][0], d1, b[0][1], t[1][2]],
-        [b[1][0], t[0][1], d2, b[0][2]],
-        [t[1][1], b[1][2], t[0][2], d3],
+def fold_kernel(scale, parts_ref, out_ref, flat_ref):
+    chips = parts_ref.shape[0] // 2
+    rows = parts_ref.shape[1]
+    lane = lax.broadcasted_iota(jnp.int32, (rows, LANES), 1)
+    tiles = parts_ref.shape[2] // LANES
+    span = flat_ref.shape[0] // rows
+    for core in range(2):
+        for trio in range(tiles // 3):
+            cols = [pl.ds((3 * trio + n) * LANES, LANES) for n in range(3)]
+            x = []
+            for n in range(3):
+                total = parts_ref[core, :, cols[n]].astype(jnp.float32)
+                for chip in range(1, chips):
+                    total += parts_ref[2 * chip + core, :, cols[n]].astype(jnp.float32)
+                x.append(total * scale)
+            found = [
+                x[0],
+                jnp.where(lane < 32, pltpu.roll(x[0], 32, 1), pltpu.roll(x[1], 32, 1)),
+                jnp.where(lane < 64, pltpu.roll(x[1], 64, 1), pltpu.roll(x[2], 64, 1)),
+                pltpu.roll(x[2], 96, 1),
+            ]
+            for n in range(4):
+                value = found[n]
+                if core == 1:
+                    value = jnp.where(
+                        lane < 24,
+                        pltpu.roll(value, 104, 1),
+                        jnp.where(
+                            lane < 48,
+                            pltpu.roll(value, 80, 1),
+                            jnp.where(lane < 72, pltpu.roll(value, 48, 1), pltpu.roll(value, 24, 1)),
+                        ),
+                    )
+                flat_ref[pl.ds(core * span // 2 + 4 * trio + n, rows, stride=span), :] = value
+    wide = lax.broadcasted_iota(jnp.int32, (span, LANES), 1)
+    kept = out_ref.shape[0]
+    for last in range(rows - kept):
+        extra = flat_ref[pl.ds((kept + last) * span, span), :]
+        for n in range(3):
+            b = 3 * last + n
+            out_ref[b] = jnp.where(
+                wide < 96, flat_ref[pl.ds(b * span, span), :], pltpu.roll(extra, 96 - 32 * n, 1)
+            ).astype(jnp.bfloat16)
+
+
+def fold(parts, scale):
+    groups, rows, pairs = parts.shape
+    span = 2 * pairs // 96
+    vmem = pl.BlockSpec(memory_space=pltpu.VMEM)
+    return pl.pallas_call(
+        functools.partial(fold_kernel, scale),
+        out_shape=jax.ShapeDtypeStruct((rows * 3 // 4, span, LANES), jnp.bfloat16),
+        in_specs=[vmem],
+        out_specs=vmem,
+        scratch_shapes=[pltpu.VMEM((rows * span, LANES), jnp.float32)],
+        compiler_params=pltpu.CompilerParams(vmem_limit_bytes=32 << 20),
+        name="fold",
+    )(parts)
+
+
+def antisymmetric(z, flip_ref, lane, row):
+    n = z.shape[0] // 2
+    flip_ref[:, pl.ds(0, 2 * n)] = -jnp.transpose(z)
+    z0, z1 = z[:n], z[n:]
+    t0, t1, t2, t3 = (flip_ref[pl.ds(q * n, n), :] for q in range(4))
+    in0, in1, in2 = lane < n, lane < 2 * n, lane < 3 * n
+
+    def roll(x, shift):
+        return pltpu.roll(x, shift % LANES, 1)
+
+    def pick(a, b, c, d):
+        return jnp.where(in0, a, jnp.where(in1, b, jnp.where(in2, c, d)))
+
+    def diagonal(start, upper, direct, flipped):
+        above = lane - start > row
+        below = lane - start < row
+        if not upper:
+            above, below = below, above
+        return jnp.where(above, direct, jnp.where(below, flipped, 0.0))
+
+    moved = roll(t2, n)
+    return [
+        pick(diagonal(0, True, z0, t0), z0, roll(t0, n), z1),
+        pick(t1, diagonal(n, False, roll(z1, -n), t2), z0, roll(t1, 2 * n)),
+        pick(z1, moved, diagonal(2 * n, True, z1, moved), z0),
+        pick(
+            roll(t3, -n),
+            z1,
+            roll(t3, 2 * n),
+            diagonal(3 * n, False, roll(z0, 3 * n), roll(t0, 3 * n)),
+        ),
     ]
-    return jnp.concatenate([jnp.concatenate(row, axis=-1) for row in rows], axis=-2)
+
+
+def fill_kernel(order_ref, *refs):
+    pieces = refs[:-4]
+    out_ref, here_ref, full_ref, flip_ref = refs[-4:]
+    step = pl.program_id(0)
+    for n, piece in enumerate(pieces):
+
+        @pl.when(step == n)
+        def _():
+            here_ref[...] = piece[...]
+
+    span = here_ref.shape[1]
+    rows = here_ref.shape[0] // 3
+    n = span // 2
+    lane = lax.broadcasted_iota(jnp.int32, (n, LANES), 1)
+    row = lax.broadcasted_iota(jnp.int32, (n, LANES), 0)
+    wide = lax.broadcasted_iota(jnp.int32, (span, LANES), 1)
+
+    def one(i, carry):
+        for p in range(2):
+            for part in range(2):
+                b = 2 * p + part
+                if b < 3:
+                    z = here_ref[b * rows + i].astype(jnp.float32)
+                else:
+                    kept = [here_ref[3 * i + k].astype(jnp.float32) for k in range(3)]
+                    z = jnp.where(
+                        wide < 32,
+                        pltpu.roll(kept[0], 32, 1),
+                        jnp.where(wide < 64, pltpu.roll(kept[1], 64, 1), pltpu.roll(kept[2], 96, 1)),
+                    )
+                for q, value in enumerate(antisymmetric(z, flip_ref.at[b], lane, row)):
+                    full_ref[part, pl.ds(q * n, n), :] = value
+            x = [full_ref[k % 2, pl.ds(k // 2, span, stride=2), :] for k in range(4)]
+            one_, two, three = (pltpu.roll(x[k], 128 - 32 * k, 1) for k in (1, 2, 3))
+            tiles = [
+                jnp.where(wide < 96, x[0], one_),
+                jnp.where(wide < 64, one_, two),
+                jnp.where(wide < 32, two, three),
+            ]
+            for k in range(3):
+                out_ref[0, i, pl.ds(2 * k + p, span, stride=6), :] = tiles[k]
+        return carry
+
+    lax.fori_loop(0, rows, one, 0)
+
+
+def fill(order, pieces, rows):
+    times = len(pieces)
+    span = pieces[0].shape[1]
+    whole = pl.BlockSpec(pieces[0].shape, lambda s, order: (0, 0, 0))
+    return pl.pallas_call(
+        fill_kernel,
+        out_shape=jax.ShapeDtypeStruct((times, rows, 6 * span, LANES), jnp.float32),
+        grid_spec=pltpu.PrefetchScalarGridSpec(
+            num_scalar_prefetch=1,
+            grid=(times,),
+            in_specs=[whole] * times,
+            out_specs=pl.BlockSpec(
+                (1, rows, 6 * span, LANES), lambda s, order: (order[s], 0, 0, 0)
+            ),
+            scratch_shapes=[
+                pltpu.VMEM(pieces[0].shape, pieces[0].dtype),
+                pltpu.VMEM((2, 2 * span, LANES), jnp.float32),
+                pltpu.VMEM((4, LANES, LANES), jnp.float32),
+            ],
+        ),
+        compiler_params=pltpu.CompilerParams(vmem_limit_bytes=32 << 20),
+        name="fill",
+    )(order, *pieces)
 
 
 def body(vectors, momenta, offsets):
@@ -191,20 +341,14 @@
     )
     partial = pair_sums(quarters, own, sib, phase)
     parts = lax.all_to_all(partial.reshape(groups, 4 * rows, -1), "space", 0, 0, tiled=False)
-    parts = parts.reshape(groups // 2, 2, 4 * rows, -1).astype(jnp.float32)
-    mine = (jnp.sum(parts, axis=0) * (1.0 / math.sqrt(sites * groups))).astype(jnp.bfloat16)
+    mine = fold(parts, 1.0 / math.sqrt(sites * groups))
     pieces = [mine] + [
         lax.ppermute(mine, "tm", [(n, n ^ s) for n in range(times)]) for s in range(1, times)
     ]
-    me = lax.axis_index("tm")
-    whole = jnp.zeros((times,) + mine.shape, mine.dtype)
-    for s, piece in enumerate(pieces):
-        whole = lax.dynamic_update_slice_in_dim(whole, piece[None], me ^ s, 0)
-    found = whole.reshape(times, 2, rows, 2, 2, fourth, 4, fourth)
-    found = jnp.transpose(found, (0, 2, 3, 4, 1, 5, 6, 7))
-    full = assemble(found)
-    full = jnp.transpose(full, (0, 1, 2, 4, 3, 5)).astype(jnp.float32)
-    return full.reshape(times, rows, 2, 2 * nvec * nvec)
+    order = lax.axis_index("tm") ^ jnp.arange(times, dtype=jnp.int32)
+    full = fill(order, pieces, rows)
+    full = full.reshape(times, rows, -1, 2, LANES)
+    return jnp.swapaxes(full, 2, 3).reshape(times, rows, 2, 2 * nvec * nvec)
 
 
 def solution(mesh):

time: 254 us -> 124 us (0.49)
  local copies, waits for them, and re-layouts: 137 us -> 2.7 us
  blocking collectives: 0 us -> 30.3 us
  Pallas kernels: 31 us -> 58.4 us
  waiting for transfers between devices: 41.7 us -> 16.5 us
  other arithmetic: 19.4 us -> 0.45 us
  starting transfers between devices: 21.8 us -> 14.7 us
    unnamed x46 -> x4, local copies, waits for them, and re-layouts: 64.2 us -> 1.84 us
    reshape x3 -> x0, local copies, waits for them, and re-layouts: 43 us -> none  [the longest x2 26.8 us: body(): return full.reshape(times, rows, 2, 2 * nvec * nvec)]
    all_to_all x0 -> x1, blocking collectives: none -> 30.3 us  [body(): lax.all_to_all(partial.reshape(groups, 4 * rows, -1), 'space', 0, 0, tile...]
    slice x1 -> x0, local copies, waits for them, and re-layouts: 28.6 us -> none  [assemble(): b = [[found[..., c, :, m, :] for m in range(4)] for c in range(2)]]
    pallas_call x0 -> x2, Pallas kernels: none -> 28.4 us  [the longest x1 27.4 us: fill(): pl.pallas_call(fill_kernel, out_shape=jax.ShapeDtypeStruct((times, rows,...]
    all_to_all x1 -> x0, waiting for transfers between devices: 24.9 us -> none  [body(): lax.all_to_all(partial.reshape(groups, 4 * rows, -1), 'space', 0, 0, tile...]
    reshape x1 -> x0, other arithmetic: 11.5 us -> none  [body(): return full.reshape(times, rows, 2, 2 * nvec * nvec)]
    neg x6 -> x0, other arithmetic: 6.6 us -> none  [assemble(): t = [[-jnp.swapaxes(b[c][m], -1, -2) for m in range(4)] for c in range(2)]]
  transfers between devices with their start and end apart: 9 -> 8, of which waited for: 5 -> 6; matrix products, arithmetic and copies ran while one was open for 1% -> 2% of each run, Pallas kernels for 0% -> 0%
where the time goes in v2:
time: 124 us; the launch traced here: 123 us
  Pallas kernels  58.4 us (47%)
  blocking collectives  30.3 us (24%)
  waiting for transfers between devices  16.5 us (13%)
  starting transfers between devices  14.7 us (12%)
  local copies, waits for them, and re-layouts  2.7 us (2%)
    all_to_all x1, blocking collectives, body(): lax.all_to_all(partial.reshape(groups, 4 * rows, -1), 'space', 0, 0, tile...  30.3 us
    pallas_call x1, Pallas kernels, pair_sums(): pl.pallas_call(pair_kernel, out_shape=jax.ShapeDtypeStruct((4 * nvec, pai...  30 us
    pallas_call x1, Pallas kernels, fill(): pl.pallas_call(fill_kernel, out_shape=jax.ShapeDtypeStruct((times, rows,...  27.4 us
    ppermute x7, waiting for transfers between devices, body(): lax.ppermute(mine, 'tm', [(n, n ^ s) for n in range(times)])  16.4 us
    ppermute x7, starting transfers between devices, body(): lax.ppermute(mine, 'tm', [(n, n ^ s) for n in range(times)])  14.7 us
  transfers between devices with their start and end apart: 8, of which 6 were waited for; matrix products, arithmetic and copies ran while one was open for 2% of the time, Pallas kernels for 0%

profile of v2, /device:TPU:0, one launch (start us, length us, event | category | flops | bytes accessed | tf_op | source)
XLA Modules:
  0.0 123.1 jit_solution(6614785571506889988)
XLA Ops:
  0.0 0.0 collective-permute-start
  0.0 0.8 copy.7
  0.8 0.8 constant_dynamic-slice_fusion.1
  1.6 0.1 add_bitcast_fusion.1
  1.7 0.1 add_bitcast_fusion
  1.8 0.1 multiply_reduce_fusion
  1.9 0.1 fusion.4
  2.1 0.1 collective-permute-done.sib_ref
  2.2 0.0 copy-start
  2.2 1.1 copy-done
  3.3 30.0 %pair_sums.1 = bf16[384,2304]{1,0:T(8,128)(2,1)S(1)} custom-call(s32[4]{0:T(128)S(1)} %broadcast_select_fusion.quarter_ref, bf16[6,96,512]{2,1,0:T(8,128)(2,1)S(1)} %bitcast.20, bf16[6,96,512]{2,1,0:T(8,128)(2,1)S(1)} %collective-permute-done.sib_ref, f32[4,1024]{1,0:T(4,128)S(1)} %reshape.194.phase_ref), custom_call_target="tpu_custom_call" | custom-call | tf_op jit(solution)/shard_map/pair_sums/pallas_call | solution.py:141
  33.3 30.3 %all_to_all.5.parts_ref = bf16[16,24,2304]{2,1,0:T(8,128)(2,1)S(1)} all-to-all(bf16[16,24,2304]{2,1,0:T(8,128)(2,1)S(1)} %bitcast.18), channel_id=1, replica_groups=mesh['space'=16,'tm'=8] {'space'}, dimensions={0} | all-to-all | bytes 3538944 | tf_op jit(solution)/shard_map/all_to_all | solution.py:343
  63.6 1.0 fold.1.refs_0_
  64.6 6.3 %collective-permute-start.7 = (bf16[18,48,128]{2,1,0:T(8,128)(2,1)S(1)}, bf16[18,48,128]{2,1,0:T(8,128)(2,1)S(1)}, u32[]{:S(2)}, u32[]{:S(2)}) collective-permute-start(bf16[18,48,128]{2,1,0:T(8,128)(2,1)S(1)} %fold.1.refs_0_), channel_id=1, source_target_pairs={{0,7},{1,6},{2,5},{3,4},{4,3},{5,2},{6,1},{7,0},{8,15},{9,14},{10,... | collective-permute-start | bytes 663560 | tf_op jit(solution)/shard_map/ppermute | solution.py:346
  70.9 0.2 collective-permute-start.6
  71.1 2.3 %collective-permute-start.5 = (bf16[18,48,128]{2,1,0:T(8,128)(2,1)S(1)}, bf16[18,48,128]{2,1,0:T(8,128)(2,1)S(1)}, u32[]{:S(2)}, u32[]{:S(2)}) collective-permute-start(bf16[18,48,128]{2,1,0:T(8,128)(2,1)S(1)} %fold.1.refs_0_), channel_id=1, source_target_pairs={{0,5},{1,4},{2,7},{3,6},{4,1},{5,0},{6,3},{7,2},{8,13},{9,12},{10,... | collective-permute-start | bytes 663560 | tf_op jit(solution)/shard_map/ppermute | solution.py:346
  73.3 1.5 %collective-permute-start.4 = (bf16[18,48,128]{2,1,0:T(8,128)(2,1)S(1)}, bf16[18,48,128]{2,1,0:T(8,128)(2,1)S(1)}, u32[]{:S(2)}, u32[]{:S(2)}) collective-permute-start(bf16[18,48,128]{2,1,0:T(8,128)(2,1)S(1)} %fold.1.refs_0_), channel_id=1, source_target_pairs={{0,4},{1,5},{2,6},{3,7},{4,0},{5,1},{6,2},{7,3},{8,12},{9,13},{10,... | collective-permute-start | bytes 663560 | tf_op jit(solution)/shard_map/ppermute | solution.py:346
  74.8 3.4 %collective-permute-start.3 = (bf16[18,48,128]{2,1,0:T(8,128)(2,1)S(1)}, bf16[18,48,128]{2,1,0:T(8,128)(2,1)S(1)}, u32[]{:S(2)}, u32[]{:S(2)}) collective-permute-start(bf16[18,48,128]{2,1,0:T(8,128)(2,1)S(1)} %fold.1.refs_0_), channel_id=1, source_target_pairs={{0,3},{1,2},{2,1},{3,0},{4,7},{5,6},{6,5},{7,4},{8,11},{9,10},{10,... | collective-permute-start | bytes 663560 | tf_op jit(solution)/shard_map/ppermute | solution.py:346
  78.2 0.0 collective-permute-done.7.refs_7_
  78.2 1.1 collective-permute-start.2
  79.3 4.0 %collective-permute-done.6.refs_6_ = bf16[18,48,128]{2,1,0:T(8,128)(2,1)S(1)} collective-permute-done((bf16[18,48,128]{2,1,0:T(8,128)(2,1)S(1)}, bf16[18,48,128]{2,1,0:T(8,128)(2,1)S(1)}, u32[]{:S(2)}, u32[]{:S(2)}) %collective-permute-start.6) | collective-permute-done | bytes 221216 | tf_op jit(solution)/shard_map/ppermute | solution.py:346
  83.3 0.0 collective-permute-start.1
  83.3 4.2 %collective-permute-done.5.refs_5_ = bf16[18,48,128]{2,1,0:T(8,128)(2,1)S(1)} collective-permute-done((bf16[18,48,128]{2,1,0:T(8,128)(2,1)S(1)}, bf16[18,48,128]{2,1,0:T(8,128)(2,1)S(1)}, u32[]{:S(2)}, u32[]{:S(2)}) %collective-permute-start.5) | collective-permute-done | bytes 221216 | tf_op jit(solution)/shard_map/ppermute | solution.py:346
  87.5 3.4 %collective-permute-done.4.refs_4_ = bf16[18,48,128]{2,1,0:T(8,128)(2,1)S(1)} collective-permute-done((bf16[18,48,128]{2,1,0:T(8,128)(2,1)S(1)}, bf16[18,48,128]{2,1,0:T(8,128)(2,1)S(1)}, u32[]{:S(2)}, u32[]{:S(2)}) %collective-permute-start.4) | collective-permute-done | bytes 221216 | tf_op jit(solution)/shard_map/ppermute | solution.py:346
  90.9 0.0 collective-permute-done.3.refs_3_
  90.9 0.2 collective-permute-done.2.refs_2_
  91.2 4.5 %collective-permute-done.1.refs_1_ = bf16[18,48,128]{2,1,0:T(8,128)(2,1)S(1)} collective-permute-done((bf16[18,48,128]{2,1,0:T(8,128)(2,1)S(1)}, bf16[18,48,128]{2,1,0:T(8,128)(2,1)S(1)}, u32[]{:S(2)}, u32[]{:S(2)}) %collective-permute-start.1) | collective-permute-done | bytes 221216 | tf_op jit(solution)/shard_map/ppermute | solution.py:346
  95.7 27.4 %fill.1 = f32[8,6,288,128]{3,2,1,0:T(8,128)} custom-call(s32[8]{0:T(128)S(1)} %iota_xor_fusion.order_ref, bf16[18,48,128]{2,1,0:T(8,128)(2,1)S(1)} %fold.1.refs_0_, bf16[18,48,128]{2,1,0:T(8,128)(2,1)S(1)} %collective-permute-done.1.refs_1_, bf16[18,48,128]{2,1,0:T(8,128)(2,1)S(1)} %collective-permute-done.2.refs_2_, ...), custom_call_target="tpu_custom_call" | custom-call | tf_op jit(solution)/shard_map/fill/pallas_call | solution.py:301
  (9 shorter events, 0.1 us)
Async XLA Ops:
  0.0 2.2 %collective-permute-start = (bf16[6,96,512]{2,1,0:T(8,128)(2,1)}, bf16[6,96,512]{2,1,0:T(8,128)(2,1)S(1)}, u32[]{:S(2)}, u32[]{:S(2)}) collective-permute-start(bf16[6,96,512]{2,1,0:T(8,128)(2,1)} %bitcast.19), channel_id=1, source_target_pairs={{0,8},{8,0},{16,24},{24,16},{32,40},{40,32},{48,56},{56,48},{64,72... | collective-permute-start | bytes 1769480 | tf_op jit(solution)/shard_map/ppermute | solution.py:330
  2.2 1.1 copy-start
  64.6 13.6 %collective-permute-start.7 = (bf16[18,48,128]{2,1,0:T(8,128)(2,1)S(1)}, bf16[18,48,128]{2,1,0:T(8,128)(2,1)S(1)}, u32[]{:S(2)}, u32[]{:S(2)}) collective-permute-start(bf16[18,48,128]{2,1,0:T(8,128)(2,1)S(1)} %fold.1.refs_0_), channel_id=1, source_target_pairs={{0,7},{1,6},{2,5},{3,4},{4,3},{5,2},{6,1},{7,0},{8,15},{9,14},{10,... | collective-permute-start | bytes 663560 | tf_op jit(solution)/shard_map/ppermute | solution.py:346
  70.9 12.4 %collective-permute-start.6 = (bf16[18,48,128]{2,1,0:T(8,128)(2,1)S(1)}, bf16[18,48,128]{2,1,0:T(8,128)(2,1)S(1)}, u32[]{:S(2)}, u32[]{:S(2)}) collective-permute-start(bf16[18,48,128]{2,1,0:T(8,128)(2,1)S(1)} %fold.1.refs_0_), channel_id=1, source_target_pairs={{0,6},{1,7},{2,4},{3,5},{4,2},{5,3},{6,0},{7,1},{8,14},{9,15},{10,... | collective-permute-start | bytes 663560 | tf_op jit(solution)/shard_map/ppermute | solution.py:346
  71.1 16.5 %collective-permute-start.5 = (bf16[18,48,128]{2,1,0:T(8,128)(2,1)S(1)}, bf16[18,48,128]{2,1,0:T(8,128)(2,1)S(1)}, u32[]{:S(2)}, u32[]{:S(2)}) collective-permute-start(bf16[18,48,128]{2,1,0:T(8,128)(2,1)S(1)} %fold.1.refs_0_), channel_id=1, source_target_pairs={{0,5},{1,4},{2,7},{3,6},{4,1},{5,0},{6,3},{7,2},{8,13},{9,12},{10,... | collective-permute-start | bytes 663560 | tf_op jit(solution)/shard_map/ppermute | solution.py:346
  73.3 17.6 %collective-permute-start.4 = (bf16[18,48,128]{2,1,0:T(8,128)(2,1)S(1)}, bf16[18,48,128]{2,1,0:T(8,128)(2,1)S(1)}, u32[]{:S(2)}, u32[]{:S(2)}) collective-permute-start(bf16[18,48,128]{2,1,0:T(8,128)(2,1)S(1)} %fold.1.refs_0_), channel_id=1, source_target_pairs={{0,4},{1,5},{2,6},{3,7},{4,0},{5,1},{6,2},{7,3},{8,12},{9,13},{10,... | collective-permute-start | bytes 663560 | tf_op jit(solution)/shard_map/ppermute | solution.py:346
  74.8 16.2 %collective-permute-start.3 = (bf16[18,48,128]{2,1,0:T(8,128)(2,1)S(1)}, bf16[18,48,128]{2,1,0:T(8,128)(2,1)S(1)}, u32[]{:S(2)}, u32[]{:S(2)}) collective-permute-start(bf16[18,48,128]{2,1,0:T(8,128)(2,1)S(1)} %fold.1.refs_0_), channel_id=1, source_target_pairs={{0,3},{1,2},{2,1},{3,0},{4,7},{5,6},{6,5},{7,4},{8,11},{9,10},{10,... | collective-permute-start | bytes 663560 | tf_op jit(solution)/shard_map/ppermute | solution.py:346
  78.2 13.0 %collective-permute-start.2 = (bf16[18,48,128]{2,1,0:T(8,128)(2,1)S(1)}, bf16[18,48,128]{2,1,0:T(8,128)(2,1)S(1)}, u32[]{:S(2)}, u32[]{:S(2)}) collective-permute-start(bf16[18,48,128]{2,1,0:T(8,128)(2,1)S(1)} %fold.1.refs_0_), channel_id=1, source_target_pairs={{0,2},{1,3},{2,0},{3,1},{4,6},{5,7},{6,4},{7,5},{8,10},{9,11},{10,... | collective-permute-start | bytes 663560 | tf_op jit(solution)/shard_map/ppermute | solution.py:346
  83.3 12.4 %collective-permute-start.1 = (bf16[18,48,128]{2,1,0:T(8,128)(2,1)S(1)}, bf16[18,48,128]{2,1,0:T(8,128)(2,1)S(1)}, u32[]{:S(2)}, u32[]{:S(2)}) collective-permute-start(bf16[18,48,128]{2,1,0:T(8,128)(2,1)S(1)} %fold.1.refs_0_), channel_id=1, source_target_pairs={{0,1},{1,0},{2,3},{3,2},{4,5},{5,4},{6,7},{7,6},{8,9},{9,8},{10,11... | collective-permute-start | bytes 663560 | tf_op jit(solution)/shard_map/ppermute | solution.py:346

commit v3 on v2

--- a/solution.py
+++ b/solution.py
@@ -13,7 +13,7 @@
 BRICK_Z = 8
 LANES = 128
 ORDER = ((0, 1, 2, 3), (2, 0, 3, 1))
-GROUP = 4
+GROUP = 8
 OWNERS = 16
 
 
@@ -214,11 +214,24 @@
     )(parts)
 
 
-def antisymmetric(z, flip_ref, lane, row):
+def flipped_rows(z, lane):
     n = z.shape[0] // 2
-    flip_ref[:, pl.ds(0, 2 * n)] = -jnp.transpose(z)
     z0, z1 = z[:n], z[n:]
-    t0, t1, t2, t3 = (flip_ref[pl.ds(q * n, n), :] for q in range(4))
+    return jnp.concatenate(
+        [
+            jnp.where(lane < 3 * n, z0, z1),
+            z0,
+            jnp.where(lane < 3 * n, z1, z0),
+            jnp.where(lane < n, z0, z1),
+        ],
+        axis=0,
+    ).astype(jnp.bfloat16)
+
+
+def antisymmetric(z, t, lane, row):
+    n = z.shape[0] // 2
+    z0, z1 = z[:n], z[n:]
+    t0, t1, t2, t3 = (t[q * n : (q + 1) * n] for q in range(4))
     in0, in1, in2 = lane < n, lane < 2 * n, lane < 3 * n
 
     def roll(x, shift):
@@ -234,29 +247,25 @@
             above, below = below, above
         return jnp.where(above, direct, jnp.where(below, flipped, 0.0))
 
-    moved = roll(t2, n)
     return [
-        pick(diagonal(0, True, z0, t0), z0, roll(t0, n), z1),
-        pick(t1, diagonal(n, False, roll(z1, -n), t2), z0, roll(t1, 2 * n)),
-        pick(z1, moved, diagonal(2 * n, True, z1, moved), z0),
-        pick(
-            roll(t3, -n),
-            z1,
-            roll(t3, 2 * n),
-            diagonal(3 * n, False, roll(z0, 3 * n), roll(t0, 3 * n)),
-        ),
+        pick(diagonal(0, True, z0, t0), z0, t0, z1),
+        pick(t1, diagonal(n, False, roll(z1, -n), roll(t2, -n)), z0, t1),
+        pick(z1, t2, diagonal(2 * n, True, z1, t2), z0),
+        pick(t3, z1, t3, diagonal(3 * n, False, roll(z0, 3 * n), t0)),
     ]
 
 
-def fill_kernel(order_ref, *refs):
-    pieces = refs[:-4]
+def fill_kernel(halves, skip, order_ref, *refs):
+    pieces = refs[skip:-4]
     out_ref, here_ref, full_ref, flip_ref = refs[-4:]
     step = pl.program_id(0)
-    for n, piece in enumerate(pieces):
+    for n in range(len(pieces) // halves):
 
         @pl.when(step == n)
         def _():
-            here_ref[...] = piece[...]
+            size = here_ref.shape[0] // halves
+            for half in range(halves):
+                here_ref[pl.ds(half * size, size)] = pieces[n * halves + half][...]
 
     span = here_ref.shape[1]
     rows = here_ref.shape[0] // 3
@@ -265,22 +274,40 @@
     row = lax.broadcasted_iota(jnp.int32, (n, LANES), 0)
     wide = lax.broadcasted_iota(jnp.int32, (span, LANES), 1)
 
-    def one(i, carry):
-        for p in range(2):
-            for part in range(2):
-                b = 2 * p + part
-                if b < 3:
-                    z = here_ref[b * rows + i].astype(jnp.float32)
-                else:
-                    kept = [here_ref[3 * i + k].astype(jnp.float32) for k in range(3)]
-                    z = jnp.where(
+    size = 2 * span
+    minus = jnp.where(
+        lax.broadcasted_iota(jnp.int32, (size, LANES), 0)
+        == lax.broadcasted_iota(jnp.int32, (size, LANES), 1),
+        -1.0,
+        0.0,
+    ).astype(jnp.bfloat16)
+
+    def first(i):
+        z = []
+        for b in range(4):
+            if b < 3:
+                z.append(here_ref[b * rows + i].astype(jnp.float32))
+            else:
+                kept = [here_ref[3 * i + k].astype(jnp.float32) for k in range(3)]
+                z.append(
+                    jnp.where(
                         wide < 32,
                         pltpu.roll(kept[0], 32, 1),
                         jnp.where(wide < 64, pltpu.roll(kept[1], 64, 1), pltpu.roll(kept[2], 96, 1)),
                     )
-                for q, value in enumerate(antisymmetric(z, flip_ref.at[b], lane, row)):
-                    full_ref[part, pl.ds(q * n, n), :] = value
-            x = [full_ref[k % 2, pl.ds(k // 2, span, stride=2), :] for k in range(4)]
+                )
+            flip_ref[i, pl.ds(b * LANES, size), :] = flipped_rows(z[b], lane)
+        t = lax.dot_general(
+            minus, flip_ref[i], (((1,), (1,)), ((), ())), preferred_element_type=jnp.float32
+        )
+        for p in range(2):
+            for part in range(2):
+                b = 2 * p + part
+                here = t[:, b * LANES : (b + 1) * LANES]
+                for q, value in enumerate(antisymmetric(z[b], here, lane, row)):
+                    full_ref[i, b, pl.ds(q * n, n), :] = value
+        for p in range(2):
+            x = [full_ref[i, 2 * p + k % 2, pl.ds(k // 2, span, stride=2), :] for k in range(4)]
             one_, two, three = (pltpu.roll(x[k], 128 - 32 * k, 1) for k in (1, 2, 3))
             tiles = [
                 jnp.where(wide < 96, x[0], one_),
@@ -289,34 +316,38 @@
             ]
             for k in range(3):
                 out_ref[0, i, pl.ds(2 * k + p, span, stride=6), :] = tiles[k]
-        return carry
-
-    lax.fori_loop(0, rows, one, 0)
-
-
-def fill(order, pieces, rows):
-    times = len(pieces)
-    span = pieces[0].shape[1]
-    whole = pl.BlockSpec(pieces[0].shape, lambda s, order: (0, 0, 0))
+
+    for i in range(rows):
+        first(i)
+
+
+def fill(into, order, pieces, times, rows):
+    halves = len(pieces[0])
+    flat = [half for piece in pieces for half in piece]
+    kept, span = halves * flat[0].shape[0], flat[0].shape[1]
+    whole = pl.BlockSpec(flat[0].shape, lambda s, order: (0, 0, 0))
+    shape = jax.ShapeDtypeStruct((times, rows, 6 * span, LANES), jnp.float32)
+    skip = 0 if into is None else 1
     return pl.pallas_call(
-        fill_kernel,
-        out_shape=jax.ShapeDtypeStruct((times, rows, 6 * span, LANES), jnp.float32),
+        functools.partial(fill_kernel, halves, skip),
+        out_shape=shape,
         grid_spec=pltpu.PrefetchScalarGridSpec(
             num_scalar_prefetch=1,
-            grid=(times,),
-            in_specs=[whole] * times,
+            grid=(len(pieces),),
+            in_specs=[pl.BlockSpec(memory_space=pl.ANY)] * skip + [whole] * len(flat),
             out_specs=pl.BlockSpec(
                 (1, rows, 6 * span, LANES), lambda s, order: (order[s], 0, 0, 0)
             ),
             scratch_shapes=[
-                pltpu.VMEM(pieces[0].shape, pieces[0].dtype),
-                pltpu.VMEM((2, 2 * span, LANES), jnp.float32),
-                pltpu.VMEM((4, LANES, LANES), jnp.float32),
+                pltpu.VMEM((kept, span, LANES), flat[0].dtype),
+                pltpu.VMEM((rows, 4, 2 * span, LANES), jnp.float32),
+                pltpu.VMEM((rows, 4 * LANES, LANES), jnp.bfloat16),
             ],
         ),
+        input_output_aliases={1: 0} if skip else {},
         compiler_params=pltpu.CompilerParams(vmem_limit_bytes=32 << 20),
         name="fill",
-    )(order, *pieces)
+    )(order, *([] if into is None else [into]), *flat)
 
 
 def body(vectors, momenta, offsets):
@@ -342,11 +373,31 @@
     partial = pair_sums(quarters, own, sib, phase)
     parts = lax.all_to_all(partial.reshape(groups, 4 * rows, -1), "space", 0, 0, tiled=False)
     mine = fold(parts, 1.0 / math.sqrt(sites * groups))
-    pieces = [mine] + [
-        lax.ppermute(mine, "tm", [(n, n ^ s) for n in range(times)]) for s in range(1, times)
-    ]
-    order = lax.axis_index("tm") ^ jnp.arange(times, dtype=jnp.int32)
-    full = fill(order, pieces, rows)
+    me = lax.axis_index("tm")
+    half, z = me // 4, me % 4
+
+    def turn(x, by):
+        return lax.ppermute(
+            x, "tm", [(4 * h + n, 4 * h + (n + by) % 4) for h in range(times // 4) for n in range(4)]
+        )
+
+    cut = mine.shape[0] // 2
+    other = lax.ppermute(mine, "tm", [(n, n ^ 4) for n in range(times)])
+    left, right = turn(mine, 1), turn(mine, -1)
+    far = (turn(left[:cut], 1), turn(right[cut:], -1))
+    left2, right2 = turn(other, 1), turn(other, -1)
+    far2 = (turn(left2[:cut], 1), turn(right2[cut:], -1))
+    same, across = 4 * half, 4 * (1 - half)
+    before, after, opposite = (z + 3) % 4, (z + 1) % 4, (z + 2) % 4
+
+    def at(*order):
+        return jnp.stack(order).astype(jnp.int32)
+
+    full = fill(None, at(me), [(mine,)], times, rows)
+    full = fill(full, at(same + before, same + after), [(left,), (right,)], times, rows)
+    full = fill(full, at(across + z), [(other,)], times, rows)
+    full = fill(full, at(across + before, across + after), [(left2,), (right2,)], times, rows)
+    full = fill(full, at(same + opposite, across + opposite), [far, far2], times, rows)
     full = full.reshape(times, rows, -1, 2, LANES)
     return jnp.swapaxes(full, 2, 3).reshape(times, rows, 2, 2 * nvec * nvec)
 

time: 124 us -> 98.7 us (0.80)
  Pallas kernels: 58.4 us -> 43 us
  waiting for transfers between devices: 16.5 us -> 3.88 us
  starting transfers between devices: 14.7 us -> 17.8 us
    pallas_call x1 -> x5, Pallas kernels: 27.4 us -> 12.8 us  [fill(): pl.pallas_call(functools.partial(fill_kernel, halves, skip), out_shape=sh...]
    ppermute x7 -> x9, waiting for transfers between devices: 16.4 us -> 3.82 us  [the longest x8 2.05 us: turn(): lax.ppermute(x, 'tm', [(4 * h + n, 4 * h + (n + by) % 4) for h in range(t...]
    ppermute x7 -> x9, starting transfers between devices: 14.7 us -> 17.8 us  [the longest x8 15 us: turn(): lax.ppermute(x, 'tm', [(4 * h + n, 4 * h + (n + by) % 4) for h in range(t...]
  transfers between devices with their start and end apart: 8 -> 10, of which waited for: 6 -> 3; matrix products, arithmetic and copies ran while one was open for 2% -> 2% of each run, Pallas kernels for 0% -> 10%
where the time goes in v3:
time: 98.7 us; the launch traced here: 98.5 us
  Pallas kernels  43 us (44%)
  blocking collectives  30.3 us (31%)
  starting transfers between devices  17.8 us (18%)
  waiting for transfers between devices  3.88 us (4%)
  local copies, waits for them, and re-layouts  2.74 us (3%)
    all_to_all x1, blocking collectives, body(): lax.all_to_all(partial.reshape(groups, 4 * rows, -1), 'space', 0, 0, tile...  30.3 us
    pallas_call x1, Pallas kernels, pair_sums(): pl.pallas_call(pair_kernel, out_shape=jax.ShapeDtypeStruct((4 * nvec, pai...  29.1 us
    ppermute x8, starting transfers between devices, turn(): lax.ppermute(x, 'tm', [(4 * h + n, 4 * h + (n + by) % 4) for h in range(t...  15 us
    pallas_call x5, Pallas kernels, fill(): pl.pallas_call(functools.partial(fill_kernel, halves, skip), out_shape=sh...  12.8 us
    ppermute x1, starting transfers between devices, body(): other = lax.ppermute(mine, 'tm', [(n, n ^ 4) for n in range(times)])  2.82 us
    ppermute x8, waiting for transfers between devices, turn(): lax.ppermute(x, 'tm', [(4 * h + n, 4 * h + (n + by) % 4) for h in range(t...  2.05 us
  transfers between devices with their start and end apart: 10, of which 3 were waited for; matrix products, arithmetic and copies ran while one was open for 2% of the time, Pallas kernels for 10%

profile of v3, /device:TPU:0, one launch (start us, length us, event | category | flops | bytes accessed | tf_op | source)
XLA Modules:
  0.0 98.5 jit_solution(16968801288408976632)
XLA Ops:
  0.0 0.0 collective-permute-start
  0.0 0.8 constant_dynamic-slice_fusion.1
  0.9 0.1 add_bitcast_fusion.1
  1.0 0.1 add_bitcast_fusion
  1.1 0.8 copy.11
  1.8 0.1 multiply_reduce_fusion
  1.9 0.1 fusion.4
  2.2 0.1 collective-permute-done.sib_ref
  2.2 1.1 %copy-done = bf16[1,2,3,96,512]{4,3,2,1,0:T(8,128)(2,1)S(1)} copy-done((bf16[1,2,3,96,512]{4,3,2,1,0:T(8,128)(2,1)S(1)}, bf16[1,2,3,96,512]{4,3,2,1,0:T(8,128)(2,1)}, u32[]{:S(2)}) %copy-start) | copy-done | bytes 589848
  3.3 29.1 %pair_sums.1 = bf16[384,2304]{1,0:T(8,128)(2,1)S(1)} custom-call(s32[4]{0:T(128)S(1)} %broadcast_select_fusion.quarter_ref, bf16[6,96,512]{2,1,0:T(8,128)(2,1)S(1)} %bitcast.28, bf16[6,96,512]{2,1,0:T(8,128)(2,1)S(1)} %collective-permute-done.sib_ref, f32[4,1024]{1,0:T(4,128)S(1)} %reshape.194.phase_ref), custom_call_target="tpu_custom_call" | custom-call | tf_op jit(solution)/shard_map/pair_sums/pallas_call | solution.py:141
  32.4 30.3 %all_to_all.5.parts_ref = bf16[16,24,2304]{2,1,0:T(8,128)(2,1)S(1)} all-to-all(bf16[16,24,2304]{2,1,0:T(8,128)(2,1)S(1)} %bitcast.26), channel_id=1, replica_groups=mesh['space'=16,'tm'=8] {'space'}, dimensions={0} | all-to-all | bytes 3538944 | tf_op jit(solution)/shard_map/all_to_all | solution.py:374
  62.7 1.0 %fold.1.refs_0_ = bf16[18,48,128]{2,1,0:T(8,128)(2,1)S(1)} custom-call(bf16[16,24,2304]{2,1,0:T(8,128)(2,1)S(1)} %all_to_all.5.parts_ref), custom_call_target="tpu_custom_call" | custom-call | tf_op jit(solution)/shard_map/fold/pallas_call | solution.py:206
  63.8 2.8 %collective-permute-start.3 = (bf16[18,48,128]{2,1,0:T(8,128)(2,1)S(1)}, bf16[18,48,128]{2,1,0:T(8,128)(2,1)S(1)}, u32[]{:S(2)}, u32[]{:S(2)}) collective-permute-start(bf16[18,48,128]{2,1,0:T(8,128)(2,1)S(1)} %fold.1.refs_0_), channel_id=1, source_target_pairs={{0,4},{1,5},{2,6},{3,7},{4,0},{5,1},{6,2},{7,3},{8,12},{9,13},{10,... | collective-permute-start | bytes 663560 | tf_op jit(solution)/shard_map/ppermute | solution.py:385
  66.6 1.9 %collective-permute-start.1 = (bf16[18,48,128]{2,1,0:T(8,128)(2,1)S(1)}, bf16[18,48,128]{2,1,0:T(8,128)(2,1)S(1)}, u32[]{:S(2)}, u32[]{:S(2)}) collective-permute-start(bf16[18,48,128]{2,1,0:T(8,128)(2,1)S(1)} %fold.1.refs_0_), channel_id=1, source_target_pairs={{0,1},{1,2},{2,3},{3,0},{4,5},{5,6},{6,7},{7,4},{8,9},{9,10},{10,1... | collective-permute-start | bytes 663560 | tf_op jit(solution)/shard_map/ppermute | solution.py:380
  68.5 2.1 %collective-permute-start.2 = (bf16[18,48,128]{2,1,0:T(8,128)(2,1)S(1)}, bf16[18,48,128]{2,1,0:T(8,128)(2,1)S(1)}, u32[]{:S(2)}, u32[]{:S(2)}) collective-permute-start(bf16[18,48,128]{2,1,0:T(8,128)(2,1)S(1)} %fold.1.refs_0_), channel_id=1, source_target_pairs={{0,3},{1,0},{2,1},{3,2},{4,7},{5,4},{6,5},{7,6},{8,11},{9,8},{10,9... | collective-permute-start | bytes 663560 | tf_op jit(solution)/shard_map/ppermute | solution.py:380
  70.6 1.8 %collective-permute-done.3.refs_1_ = bf16[18,48,128]{2,1,0:T(8,128)(2,1)S(1)} collective-permute-done((bf16[18,48,128]{2,1,0:T(8,128)(2,1)S(1)}, bf16[18,48,128]{2,1,0:T(8,128)(2,1)S(1)}, u32[]{:S(2)}, u32[]{:S(2)}) %collective-permute-start.3) | collective-permute-done | bytes 221216 | tf_op jit(solution)/shard_map/ppermute | solution.py:385
  72.4 1.9 %collective-permute-start.4 = (bf16[18,48,128]{2,1,0:T(8,128)(2,1)S(1)}, bf16[18,48,128]{2,1,0:T(8,128)(2,1)S(1)}, u32[]{:S(2)}, u32[]{:S(2)}) collective-permute-start(bf16[18,48,128]{2,1,0:T(8,128)(2,1)S(1)} %collective-permute-done.3.refs_1_), channel_id=1, source_target_pairs={{0,1},{1,2},{2,3},{3,0},{4,5},{5,6},{6,7},{7,4},{8,9},{9,10},{10,1... | collective-permute-start | bytes 663560 | tf_op jit(solution)/shard_map/ppermute | solution.py:380
  74.3 2.1 %collective-permute-start.5 = (bf16[18,48,128]{2,1,0:T(8,128)(2,1)S(1)}, bf16[18,48,128]{2,1,0:T(8,128)(2,1)S(1)}, u32[]{:S(2)}, u32[]{:S(2)}) collective-permute-start(bf16[18,48,128]{2,1,0:T(8,128)(2,1)S(1)} %collective-permute-done.3.refs_1_), channel_id=1, source_target_pairs={{0,3},{1,0},{2,1},{3,2},{4,7},{5,4},{6,5},{7,6},{8,11},{9,8},{10,9... | collective-permute-start | bytes 663560 | tf_op jit(solution)/shard_map/ppermute | solution.py:380
  76.4 0.1 pad_add_fusion.1.order_ref
  76.5 0.1 pad_add_fusion.2.order_ref
  76.6 0.0 collective-permute-done.1.refs_1_
  76.6 0.1 collective-permute-start.6
  76.7 3.3 %collective-permute-start.7 = (bf16[9,48,128]{2,1,0:T(8,128)(2,1)S(1)}, bf16[9,48,128]{2,1,0:T(8,128)(2,1)S(1)}, u32[]{:S(2)}, u32[]{:S(2)}) collective-permute-start(bf16[9,48,128]{2,1,0:T(8,128)(2,1)S(1)} %slice.17), channel_id=1, source_target_pairs={{0,3},{1,0},{2,1},{3,2},{4,7},{5,4},{6,5},{7,6},{8,11},{9,8},{10,9... | collective-permute-start | bytes 331784 | tf_op jit(solution)/shard_map/ppermute | solution.py:380
  80.0 2.0 %collective-permute-done.4.refs_1_ = bf16[18,48,128]{2,1,0:T(8,128)(2,1)S(1)} collective-permute-done((bf16[18,48,128]{2,1,0:T(8,128)(2,1)S(1)}, bf16[18,48,128]{2,1,0:T(8,128)(2,1)S(1)}, u32[]{:S(2)}, u32[]{:S(2)}) %collective-permute-start.4) | collective-permute-done | bytes 221216 | tf_op jit(solution)/shard_map/ppermute | solution.py:380
  82.0 0.1 collective-permute-start.8
  82.1 3.5 %collective-permute-start.9 = (bf16[9,48,128]{2,1,0:T(8,128)(2,1)S(1)}, bf16[9,48,128]{2,1,0:T(8,128)(2,1)S(1)}, u32[]{:S(2)}, u32[]{:S(2)}) collective-permute-start(bf16[9,48,128]{2,1,0:T(8,128)(2,1)S(1)} %slice.19), channel_id=1, source_target_pairs={{0,3},{1,0},{2,1},{3,2},{4,7},{5,4},{6,5},{7,6},{8,11},{9,8},{10,9... | collective-permute-start | bytes 331784 | tf_op jit(solution)/shard_map/ppermute | solution.py:380
  85.6 0.1 pad_add_fusion.3.order_ref
  85.7 1.7 %fill.5.refs_0_ = f32[8,6,288,128]{3,2,1,0:T(8,128)} custom-call(s32[1]{0:T(128)} %bitcast.7.order_ref, bf16[18,48,128]{2,1,0:T(8,128)(2,1)S(1)} %fold.1.refs_0_), custom_call_target="tpu_custom_call" | custom-call | tf_op jit(solution)/shard_map/fill/pallas_call | solution.py:331
  87.4 3.1 %fill.6.refs_0_ = f32[8,6,288,128]{3,2,1,0:T(8,128)} custom-call(s32[2]{0:T(128)S(1)} %pad_add_fusion.3.order_ref, f32[8,6,288,128]{3,2,1,0:T(8,128)} %fill.5.refs_0_, bf16[18,48,128]{2,1,0:T(8,128)(2,1)S(1)} %collective-permute-done.1.refs_1_, bf16[18,48,128]{2,1,0:T(8,128)(2,1)S(1)} %collective-permute-done.2.refs_2_), custom_call_target="tpu_custom_call", output_to_operand_aliasing={{}: (1, {})} | custom-call | tf_op jit(solution)/shard_map/fill/pallas_call | solution.py:331
  90.5 1.7 %fill.7.refs_0_ = f32[8,6,288,128]{3,2,1,0:T(8,128)} custom-call(s32[1]{0:T(128)} %bitcast.4.order_ref, f32[8,6,288,128]{3,2,1,0:T(8,128)} %fill.6.refs_0_, bf16[18,48,128]{2,1,0:T(8,128)(2,1)S(1)} %collective-permute-done.3.refs_1_), custom_call_target="tpu_custom_call", output_to_operand_aliasing={{}: (1, {})} | custom-call | tf_op jit(solution)/shard_map/fill/pallas_call | solution.py:331
  92.2 3.1 %fill.8.refs_0_ = f32[8,6,288,128]{3,2,1,0:T(8,128)} custom-call(s32[2]{0:T(128)S(1)} %pad_add_fusion.2.order_ref, f32[8,6,288,128]{3,2,1,0:T(8,128)} %fill.7.refs_0_, bf16[18,48,128]{2,1,0:T(8,128)(2,1)S(1)} %collective-permute-done.4.refs_1_, bf16[18,48,128]{2,1,0:T(8,128)(2,1)S(1)} %collective-permute-done.5.refs_2_), custom_call_target="tpu_custom_call", output_to_operand_aliasing={{}: (1, {})} | custom-call | tf_op jit(solution)/shard_map/fill/pallas_call | solution.py:331
  95.4 3.1 %fill.9 = f32[8,6,288,128]{3,2,1,0:T(8,128)} custom-call(s32[2]{0:T(128)S(1)} %pad_add_fusion.1.order_ref, f32[8,6,288,128]{3,2,1,0:T(8,128)} %fill.8.refs_0_, bf16[9,48,128]{2,1,0:T(8,128)(2,1)S(1)} %collective-permute-done.6.refs_1_, bf16[9,48,128]{2,1,0:T(8,128)(2,1)S(1)} %collective-permute-done.7.refs_2_, ...), custom_call_target="tpu_custom_call", output_to_operand_aliasing={{}: (1, {})} | custom-call | tf_op jit(solution)/shard_map/fill/pallas_call | solution.py:331
  (19 shorter events, 0.2 us)
Async XLA Ops:
  0.0 2.2 %collective-permute-start = (bf16[6,96,512]{2,1,0:T(8,128)(2,1)}, bf16[6,96,512]{2,1,0:T(8,128)(2,1)S(1)}, u32[]{:S(2)}, u32[]{:S(2)}) collective-permute-start(bf16[6,96,512]{2,1,0:T(8,128)(2,1)} %bitcast.27), channel_id=1, source_target_pairs={{0,8},{8,0},{16,24},{24,16},{32,40},{40,32},{48,56},{56,48},{64,72... | collective-permute-start | bytes 1769480 | tf_op jit(solution)/shard_map/ppermute | solution.py:361
  2.2 1.1 %copy-start = (bf16[1,2,3,96,512]{4,3,2,1,0:T(8,128)(2,1)S(1)}, bf16[1,2,3,96,512]{4,3,2,1,0:T(8,128)(2,1)}, u32[]{:S(2)}) copy-start(bf16[1,2,3,96,512]{4,3,2,1,0:T(8,128)(2,1)} %param.5) | copy-start | bytes 1769476
  63.8 8.6 %collective-permute-start.3 = (bf16[18,48,128]{2,1,0:T(8,128)(2,1)S(1)}, bf16[18,48,128]{2,1,0:T(8,128)(2,1)S(1)}, u32[]{:S(2)}, u32[]{:S(2)}) collective-permute-start(bf16[18,48,128]{2,1,0:T(8,128)(2,1)S(1)} %fold.1.refs_0_), channel_id=1, source_target_pairs={{0,4},{1,5},{2,6},{3,7},{4,0},{5,1},{6,2},{7,3},{8,12},{9,13},{10,... | collective-permute-start | bytes 663560 | tf_op jit(solution)/shard_map/ppermute | solution.py:385
  66.6 10.0 %collective-permute-start.1 = (bf16[18,48,128]{2,1,0:T(8,128)(2,1)S(1)}, bf16[18,48,128]{2,1,0:T(8,128)(2,1)S(1)}, u32[]{:S(2)}, u32[]{:S(2)}) collective-permute-start(bf16[18,48,128]{2,1,0:T(8,128)(2,1)S(1)} %fold.1.refs_0_), channel_id=1, source_target_pairs={{0,1},{1,2},{2,3},{3,0},{4,5},{5,6},{6,7},{7,4},{8,9},{9,10},{10,1... | collective-permute-start | bytes 663560 | tf_op jit(solution)/shard_map/ppermute | solution.py:380
  68.5 8.2 %collective-permute-start.2 = (bf16[18,48,128]{2,1,0:T(8,128)(2,1)S(1)}, bf16[18,48,128]{2,1,0:T(8,128)(2,1)S(1)}, u32[]{:S(2)}, u32[]{:S(2)}) collective-permute-start(bf16[18,48,128]{2,1,0:T(8,128)(2,1)S(1)} %fold.1.refs_0_), channel_id=1, source_target_pairs={{0,3},{1,0},{2,1},{3,2},{4,7},{5,4},{6,5},{7,6},{8,11},{9,8},{10,9... | collective-permute-start | bytes 663560 | tf_op jit(solution)/shard_map/ppermute | solution.py:380
  72.4 9.6 %collective-permute-start.4 = (bf16[18,48,128]{2,1,0:T(8,128)(2,1)S(1)}, bf16[18,48,128]{2,1,0:T(8,128)(2,1)S(1)}, u32[]{:S(2)}, u32[]{:S(2)}) collective-permute-start(bf16[18,48,128]{2,1,0:T(8,128)(2,1)S(1)} %collective-permute-done.3.refs_1_), channel_id=1, source_target_pairs={{0,1},{1,2},{2,3},{3,0},{4,5},{5,6},{6,7},{7,4},{8,9},{9,10},{10,1... | collective-permute-start | bytes 663560 | tf_op jit(solution)/shard_map/ppermute | solution.py:380
  74.3 7.8 %collective-permute-start.5 = (bf16[18,48,128]{2,1,0:T(8,128)(2,1)S(1)}, bf16[18,48,128]{2,1,0:T(8,128)(2,1)S(1)}, u32[]{:S(2)}, u32[]{:S(2)}) collective-permute-start(bf16[18,48,128]{2,1,0:T(8,128)(2,1)S(1)} %collective-permute-done.3.refs_1_), channel_id=1, source_target_pairs={{0,3},{1,0},{2,1},{3,2},{4,7},{5,4},{6,5},{7,6},{8,11},{9,8},{10,9... | collective-permute-start | bytes 663560 | tf_op jit(solution)/shard_map/ppermute | solution.py:380
  76.6 18.8 %collective-permute-start.6 = (bf16[9,48,128]{2,1,0:T(8,128)(2,1)S(1)}, bf16[9,48,128]{2,1,0:T(8,128)(2,1)S(1)}, u32[]{:S(2)}, u32[]{:S(2)}) collective-permute-start(bf16[9,48,128]{2,1,0:T(8,128)(2,1)S(1)} %slice.16), channel_id=1, source_target_pairs={{0,1},{1,2},{2,3},{3,0},{4,5},{5,6},{6,7},{7,4},{8,9},{9,10},{10,1... | collective-permute-start | bytes 331784 | tf_op jit(solution)/shard_map/ppermute | solution.py:380
  76.7 18.7 %collective-permute-start.7 = (bf16[9,48,128]{2,1,0:T(8,128)(2,1)S(1)}, bf16[9,48,128]{2,1,0:T(8,128)(2,1)S(1)}, u32[]{:S(2)}, u32[]{:S(2)}) collective-permute-start(bf16[9,48,128]{2,1,0:T(8,128)(2,1)S(1)} %slice.17), channel_id=1, source_target_pairs={{0,3},{1,0},{2,1},{3,2},{4,7},{5,4},{6,5},{7,6},{8,11},{9,8},{10,9... | collective-permute-start | bytes 331784 | tf_op jit(solution)/shard_map/ppermute | solution.py:380
  82.0 13.3 %collective-permute-start.8 = (bf16[9,48,128]{2,1,0:T(8,128)(2,1)S(1)}, bf16[9,48,128]{2,1,0:T(8,128)(2,1)S(1)}, u32[]{:S(2)}, u32[]{:S(2)}) collective-permute-start(bf16[9,48,128]{2,1,0:T(8,128)(2,1)S(1)} %slice.18), channel_id=1, source_target_pairs={{0,1},{1,2},{2,3},{3,0},{4,5},{5,6},{6,7},{7,4},{8,9},{9,10},{10,1... | collective-permute-start | bytes 331784 | tf_op jit(solution)/shard_map/ppermute | solution.py:380
  82.1 13.2 %collective-permute-start.9 = (bf16[9,48,128]{2,1,0:T(8,128)(2,1)S(1)}, bf16[9,48,128]{2,1,0:T(8,128)(2,1)S(1)}, u32[]{:S(2)}, u32[]{:S(2)}) collective-permute-start(bf16[9,48,128]{2,1,0:T(8,128)(2,1)S(1)} %slice.19), channel_id=1, source_target_pairs={{0,3},{1,0},{2,1},{3,2},{4,7},{5,4},{6,5},{7,6},{8,11},{9,8},{10,9... | collective-permute-start | bytes 331784 | tf_op jit(solution)/shard_map/ppermute | solution.py:380

commit v4 on v3

--- a/solution.py
+++ b/solution.py
@@ -31,16 +31,13 @@
     real, imag = [], []
     for colour in range(3):
         a, b = (colour + 1) % 3, (colour + 2) % 3
-        real.append(
-            (j[0][a] * k[0][b] - j[1][a] * k[1][b]) - (j[0][b] * k[0][a] - j[1][b] * k[1][a])
-        )
-        imag.append(
-            (j[0][a] * k[1][b] + j[1][a] * k[0][b]) - (j[0][b] * k[1][a] + j[1][b] * k[0][a])
-        )
+        shared = j[2][a] * k[0][b] - j[2][b] * k[0][a]
+        real.append(shared - (j[1][a] * k[1][b] - j[1][b] * k[1][a]))
+        imag.append(shared + (j[0][a] * k[2][b] - j[0][b] * k[2][a]))
     return real + imag
 
 
-def pair_kernel(quarter_ref, own_ref, sib_ref, phase_ref, out_ref, vec_ref, mix_ref, pair_ref, acc_ref):
+def pair_kernel(quarter_ref, own_ref, sib_ref, phase_ref, out_ref, vec_ref, mix_ref, pair_ref, pair2_ref, acc_ref):
     nvec = own_ref.shape[1]
     sites = own_ref.shape[2]
     fourth = nvec // 4
@@ -69,57 +66,78 @@
                     mix_ref[chunk, second, on_imag] = w_real
             for m in range(4):
                 rows = pl.ds(pl.multiple_of(quarter_ref[m], 8), fourth)
-                for part in range(6):
-                    vec_ref[chunk, part, pl.ds(m * fourth, fourth), :] = ref[
-                        part, rows, here
-                    ].astype(jnp.float32)
+                block = pl.ds(m * fourth, fourth)
+                for colour in range(3):
+                    real = ref[colour, rows, here].astype(jnp.float32)
+                    imag = ref[3 + colour, rows, here].astype(jnp.float32)
+                    for n, value in enumerate((real, imag, real + imag, imag - real)):
+                        vec_ref[chunk, 3 * n + colour, block, :] = value
     acc_ref[...] = jnp.zeros_like(acc_ref)
 
-    def advance(chunk, carry):
-        def rows_of(first, count):
-            return [
-                [vec_ref[chunk, 3 * part + c, pl.ds(first, count), :] for c in range(3)]
-                for part in range(2)
-            ]
-
-        for group in range(fourth // GROUP):
+    def rows_of(chunk, planes, first, count):
+        return [
+            [vec_ref[chunk, 3 * n + c, pl.ds(first, count), :] for c in range(3)]
+            for n in planes
+        ]
+
+
+    def build(chunk, r, into):
+        pieces = [[] for _ in range(6)]
+        for unit in range(fourth // 8):
+            low = unit * 8
+            if low + 7 > r:
+                upper = cross(rows_of(chunk, (0, 1, 2), r, 1), rows_of(chunk, (0, 2, 3), low, 8))
+            if low < r:
+                lower = cross(rows_of(chunk, (0, 1, 2), 3 * fourth + r, 1), rows_of(chunk, (0, 2, 3), 3 * fourth + low, 8))
+            if low >= r:
+                found = upper
+            elif low + 7 <= r:
+                found = lower
+            else:
+                above = lax.broadcasted_iota(jnp.int32, (8, LANES), 0) > r - low
+                found = [jnp.where(above, u, w) for u, w in zip(upper, lower)]
+            for n in range(6):
+                pieces[n].append(found[n])
+        for m in range(3):
+            found = cross(rows_of(chunk, (0, 1, 2), m * fourth + r, 1), rows_of(chunk, (0, 2, 3), (m + 1) * fourth, fourth))
+            for n in range(6):
+                pieces[n].append(found[n])
+        for n in range(6):
+            into[pl.ds(r % GROUP * nvec, nvec), pl.ds(n * LANES, LANES)] = jnp.concatenate(pieces[n], axis=0).astype(jnp.bfloat16)
+
+    steps = fourth // GROUP
+    pieces_of = GROUP * nvec // 256
+    buffers = (pair_ref, pair2_ref)
+
+    def contract(chunk, group, source, piece):
+        cols = pl.ds(group * GROUP * nvec + piece * 256, 256)
+        acc_ref[:, cols] += lax.dot_general(
+            mix_ref[chunk],
+            source[pl.ds(piece * 256, 256), :],
+            (((1,), (1,)), ((), ())),
+            preferred_element_type=jnp.float32,
+        )
+
+    buffers[1][...] = jnp.zeros_like(buffers[1])
+
+    def advance(it, carry):
+        for gs in range(2 * steps):
+            chunk, group = 2 * it + gs // steps, gs % steps
+            if gs == 0:
+                before, last = jnp.maximum(2 * it - 1, 0), steps - 1
+            else:
+                before, last = 2 * it + (gs - 1) // steps, (gs - 1) % steps
+            done = 0
             for local in range(GROUP):
-                r = group * GROUP + local
-                pieces = [[] for _ in range(6)]
-                for unit in range(fourth // 8):
-                    low = unit * 8
-                    if low + 7 > r:
-                        upper = cross(rows_of(r, 1), rows_of(low, 8))
-                    if low < r:
-                        lower = cross(rows_of(3 * fourth + r, 1), rows_of(3 * fourth + low, 8))
-                    if low >= r:
-                        found = upper
-                    elif low + 7 <= r:
-                        found = lower
-                    else:
-                        above = lax.broadcasted_iota(jnp.int32, (8, LANES), 0) > r - low
-                        found = [jnp.where(above, u, w) for u, w in zip(upper, lower)]
-                    for n in range(6):
-                        pieces[n].append(found[n])
-                for m in range(3):
-                    found = cross(rows_of(m * fourth + r, 1), rows_of((m + 1) * fourth, fourth))
-                    for n in range(6):
-                        pieces[n].append(found[n])
-                for n in range(6):
-                    pair_ref[
-                        group, pl.ds(local * nvec, nvec), pl.ds(n * LANES, LANES)
-                    ] = jnp.concatenate(pieces[n], axis=0).astype(jnp.bfloat16)
-            width = GROUP * nvec
-            cols = pl.ds(group * width, width)
-            acc_ref[:, cols] += lax.dot_general(
-                mix_ref[chunk],
-                pair_ref[group],
-                (((1,), (1,)), ((), ())),
-                preferred_element_type=jnp.float32,
-            )
+                build(chunk, group * GROUP + local, buffers[gs % 2])
+                while done < pieces_of and (done + 1) * GROUP <= (local + 1) * pieces_of:
+                    contract(before, last, buffers[(gs + 1) % 2], done)
+                    done += 1
         return carry
 
-    lax.fori_loop(0, chunks, advance, 0)
+    lax.fori_loop(0, chunks // 2, advance, 0)
+    for piece in range(pieces_of):
+        contract(chunks - 1, steps - 1, buffers[1], piece)
     row = lax.broadcasted_iota(jnp.int32, (4 * nvec, 4 * nvec), 0)
     col = lax.broadcasted_iota(jnp.int32, (4 * nvec, 4 * nvec), 1)
     own = nvec // OWNERS
@@ -144,9 +162,10 @@
         in_specs=[pl.BlockSpec(memory_space=pltpu.SMEM), vmem, vmem, vmem],
         out_specs=vmem,
         scratch_shapes=[
-            pltpu.VMEM((chunks, 6, nvec, LANES), jnp.float32),
+            pltpu.VMEM((chunks, 12, nvec, LANES), jnp.float32),
             pltpu.VMEM((chunks, 4 * nvec, 6 * LANES), jnp.bfloat16),
-            pltpu.VMEM((nvec // 4 // GROUP, GROUP * nvec, 6 * LANES), jnp.bfloat16),
+            pltpu.VMEM((GROUP * nvec, 6 * LANES), jnp.bfloat16),
+            pltpu.VMEM((GROUP * nvec, 6 * LANES), jnp.bfloat16),
             pltpu.VMEM((4 * nvec, pairs), jnp.float32),
         ],
         compiler_params=pltpu.CompilerParams(vmem_limit_bytes=48 << 20),
@@ -393,10 +412,13 @@
     def at(*order):
         return jnp.stack(order).astype(jnp.int32)
 
-    full = fill(None, at(me), [(mine,)], times, rows)
-    full = fill(full, at(same + before, same + after), [(left,), (right,)], times, rows)
-    full = fill(full, at(across + z), [(other,)], times, rows)
-    full = fill(full, at(across + before, across + after), [(left2,), (right2,)], times, rows)
+    full = fill(
+        None,
+        at(me, same + before, same + after, across + z, across + before, across + after),
+        [(mine,), (left,), (right,), (other,), (left2,), (right2,)],
+        times,
+        rows,
+    )
     full = fill(full, at(same + opposite, across + opposite), [far, far2], times, rows)
     full = full.reshape(times, rows, -1, 2, LANES)
     return jnp.swapaxes(full, 2, 3).reshape(times, rows, 2, 2 * nvec * nvec)

time: 98.7 us -> 91.6 us (0.928)
  Pallas kernels: 43 us -> 36.3 us
    pallas_call x1, Pallas kernels: 29.1 us -> 25.5 us  [pair_sums(): pl.pallas_call(pair_kernel, out_shape=jax.ShapeDtypeStruct((4 * nvec, pai...]
    pallas_call x5 -> x2, Pallas kernels: 12.8 us -> 9.78 us  [fill(): pl.pallas_call(functools.partial(fill_kernel, halves, skip), out_shape=sh...]
  transfers between devices with their start and end apart: 10 -> 10, of which waited for: 3 -> 3; matrix products, arithmetic and copies ran while one was open for 2% -> 2% of each run, Pallas kernels for 10% -> 7%
where the time goes in v4:
time: 91.6 us; the launch traced here: 91.4 us
  Pallas kernels  36.3 us (40%)
  blocking collectives  30.3 us (33%)
  starting transfers between devices  18.3 us (20%)
  waiting for transfers between devices  3.03 us (3%)
  local copies, waits for them, and re-layouts  2.82 us (3%)
    all_to_all x1, blocking collectives, body(): lax.all_to_all(partial.reshape(groups, 4 * rows, -1), 'space', 0, 0, tile...  30.3 us
    pallas_call x1, Pallas kernels, pair_sums(): pl.pallas_call(pair_kernel, out_shape=jax.ShapeDtypeStruct((4 * nvec, pai...  25.5 us
    ppermute x8, starting transfers between devices, turn(): lax.ppermute(x, 'tm', [(4 * h + n, 4 * h + (n + by) % 4) for h in range(t...  15.5 us
    pallas_call x2, Pallas kernels, fill(): pl.pallas_call(functools.partial(fill_kernel, halves, skip), out_shape=sh...  9.78 us
    ppermute x1, starting transfers between devices, body(): other = lax.ppermute(mine, 'tm', [(n, n ^ 4) for n in range(times)])  2.78 us
    unnamed x4, local copies, waits for them, and re-layouts  1.84 us
  transfers between devices with their start and end apart: 10, of which 3 were waited for; matrix products, arithmetic and copies ran while one was open for 2% of the time, Pallas kernels for 7%

profile of v4, /device:TPU:0, one launch (start us, length us, event | category | flops | bytes accessed | tf_op | source)
XLA Modules:
  0.0 91.4 jit_solution(18401881848882294535)
XLA Ops:
  0.0 0.0 collective-permute-start
  0.0 0.8 copy.8
  0.8 0.8 constant_dynamic-slice_fusion.1
  1.6 0.1 add_bitcast_fusion.1
  1.7 0.1 add_bitcast_fusion
  1.8 0.1 multiply_reduce_fusion
  1.9 0.1 fusion.4
  2.1 0.1 collective-permute-done.sib_ref
  2.2 1.1 %copy-done = bf16[1,2,3,96,512]{4,3,2,1,0:T(8,128)(2,1)S(1)} copy-done((bf16[1,2,3,96,512]{4,3,2,1,0:T(8,128)(2,1)S(1)}, bf16[1,2,3,96,512]{4,3,2,1,0:T(8,128)(2,1)}, u32[]{:S(2)}) %copy-start) | copy-done | bytes 589848
  3.3 25.5 %pair_sums.1 = bf16[384,2304]{1,0:T(8,128)(2,1)S(1)} custom-call(s32[4]{0:T(128)S(1)} %broadcast_select_fusion.quarter_ref, bf16[6,96,512]{2,1,0:T(8,128)(2,1)S(1)} %bitcast.28, bf16[6,96,512]{2,1,0:T(8,128)(2,1)S(1)} %collective-permute-done.sib_ref, f32[4,1024]{1,0:T(4,128)S(1)} %reshape.194.phase_ref), custom_call_target="tpu_custom_call" | custom-call | tf_op jit(solution)/shard_map/pair_sums/pallas_call | solution.py:159
  28.8 30.3 %all_to_all.5.parts_ref = bf16[16,24,2304]{2,1,0:T(8,128)(2,1)S(1)} all-to-all(bf16[16,24,2304]{2,1,0:T(8,128)(2,1)S(1)} %bitcast.26), channel_id=1, replica_groups=mesh['space'=16,'tm'=8] {'space'}, dimensions={0} | all-to-all | bytes 3538944 | tf_op jit(solution)/shard_map/all_to_all | solution.py:393
  59.1 1.0 %fold.1.refs_0_ = bf16[18,48,128]{2,1,0:T(8,128)(2,1)S(1)} custom-call(bf16[16,24,2304]{2,1,0:T(8,128)(2,1)S(1)} %all_to_all.5.parts_ref), custom_call_target="tpu_custom_call" | custom-call | tf_op jit(solution)/shard_map/fold/pallas_call | solution.py:225
  60.2 2.8 %collective-permute-start.3 = (bf16[18,48,128]{2,1,0:T(8,128)(2,1)S(1)}, bf16[18,48,128]{2,1,0:T(8,128)(2,1)S(1)}, u32[]{:S(2)}, u32[]{:S(2)}) collective-permute-start(bf16[18,48,128]{2,1,0:T(8,128)(2,1)S(1)} %fold.1.refs_0_), channel_id=1, source_target_pairs={{0,4},{1,5},{2,6},{3,7},{4,0},{5,1},{6,2},{7,3},{8,12},{9,13},{10,... | collective-permute-start | bytes 663560 | tf_op jit(solution)/shard_map/ppermute | solution.py:404
  62.9 4.1 %collective-permute-start.2 = (bf16[18,48,128]{2,1,0:T(8,128)(2,1)S(1)}, bf16[18,48,128]{2,1,0:T(8,128)(2,1)S(1)}, u32[]{:S(2)}, u32[]{:S(2)}) collective-permute-start(bf16[18,48,128]{2,1,0:T(8,128)(2,1)S(1)} %fold.1.refs_0_), channel_id=1, source_target_pairs={{0,3},{1,0},{2,1},{3,2},{4,7},{5,4},{6,5},{7,6},{8,11},{9,8},{10,9... | collective-permute-start | bytes 663560 | tf_op jit(solution)/shard_map/ppermute | solution.py:399
  67.0 0.0 collective-permute-start.1
  67.0 1.8 %collective-permute-done.3.refs_3_ = bf16[18,48,128]{2,1,0:T(8,128)(2,1)S(1)} collective-permute-done((bf16[18,48,128]{2,1,0:T(8,128)(2,1)S(1)}, bf16[18,48,128]{2,1,0:T(8,128)(2,1)S(1)}, u32[]{:S(2)}, u32[]{:S(2)}) %collective-permute-start.3) | collective-permute-done | bytes 221216 | tf_op jit(solution)/shard_map/ppermute | solution.py:404
  68.8 4.0 %collective-permute-start.5 = (bf16[18,48,128]{2,1,0:T(8,128)(2,1)S(1)}, bf16[18,48,128]{2,1,0:T(8,128)(2,1)S(1)}, u32[]{:S(2)}, u32[]{:S(2)}) collective-permute-start(bf16[18,48,128]{2,1,0:T(8,128)(2,1)S(1)} %collective-permute-done.3.refs_3_), channel_id=1, source_target_pairs={{0,3},{1,0},{2,1},{3,2},{4,7},{5,4},{6,5},{7,6},{8,11},{9,8},{10,9... | collective-permute-start | bytes 663560 | tf_op jit(solution)/shard_map/ppermute | solution.py:399
  72.8 0.0 collective-permute-start.4
  72.8 0.1 stack.53.order_ref
  72.9 0.0 collective-permute-done.2.refs_2_
  72.9 3.5 %collective-permute-start.7 = (bf16[9,48,128]{2,1,0:T(8,128)(2,1)S(1)}, bf16[9,48,128]{2,1,0:T(8,128)(2,1)S(1)}, u32[]{:S(2)}, u32[]{:S(2)}) collective-permute-start(bf16[9,48,128]{2,1,0:T(8,128)(2,1)S(1)} %slice.17), channel_id=1, source_target_pairs={{0,3},{1,0},{2,1},{3,2},{4,7},{5,4},{6,5},{7,6},{8,11},{9,8},{10,9... | collective-permute-start | bytes 331784 | tf_op jit(solution)/shard_map/ppermute | solution.py:399
  76.4 0.0 collective-permute-done.1.refs_1_
  76.4 0.1 collective-permute-start.6
  76.5 1.2 %collective-permute-done.5.refs_5_ = bf16[18,48,128]{2,1,0:T(8,128)(2,1)S(1)} collective-permute-done((bf16[18,48,128]{2,1,0:T(8,128)(2,1)S(1)}, bf16[18,48,128]{2,1,0:T(8,128)(2,1)S(1)}, u32[]{:S(2)}, u32[]{:S(2)}) %collective-permute-start.5) | collective-permute-done | bytes 221216 | tf_op jit(solution)/shard_map/ppermute | solution.py:399
  77.7 3.8 %collective-permute-start.9 = (bf16[9,48,128]{2,1,0:T(8,128)(2,1)S(1)}, bf16[9,48,128]{2,1,0:T(8,128)(2,1)S(1)}, u32[]{:S(2)}, u32[]{:S(2)}) collective-permute-start(bf16[9,48,128]{2,1,0:T(8,128)(2,1)S(1)} %slice.19), channel_id=1, source_target_pairs={{0,3},{1,0},{2,1},{3,2},{4,7},{5,4},{6,5},{7,6},{8,11},{9,8},{10,9... | collective-permute-start | bytes 331784 | tf_op jit(solution)/shard_map/ppermute | solution.py:399
  81.4 0.0 collective-permute-done.4.refs_4_
  81.4 0.1 collective-permute-start.8
  81.5 0.1 pad_add_fusion.1.order_ref
  81.6 6.7 %fill.2.refs_0_ = f32[8,6,288,128]{3,2,1,0:T(8,128)} custom-call(s32[6]{0:T(128)S(1)} %stack.53.order_ref, bf16[18,48,128]{2,1,0:T(8,128)(2,1)S(1)} %fold.1.refs_0_, bf16[18,48,128]{2,1,0:T(8,128)(2,1)S(1)} %collective-permute-done.1.refs_1_, bf16[18,48,128]{2,1,0:T(8,128)(2,1)S(1)} %collective-permute-done.2.refs_2_, ...), custom_call_target="tpu_custom_call" | custom-call | tf_op jit(solution)/shard_map/fill/pallas_call | solution.py:350
  88.2 0.0 collective-permute-done.6.refs_1_
  88.2 0.0 collective-permute-done.9.refs_4_
  88.3 3.1 %fill.3 = f32[8,6,288,128]{3,2,1,0:T(8,128)} custom-call(s32[2]{0:T(128)S(1)} %pad_add_fusion.1.order_ref, f32[8,6,288,128]{3,2,1,0:T(8,128)} %fill.2.refs_0_, bf16[9,48,128]{2,1,0:T(8,128)(2,1)S(1)} %collective-permute-done.6.refs_1_, bf16[9,48,128]{2,1,0:T(8,128)(2,1)S(1)} %collective-permute-done.7.refs_2_, ...), custom_call_target="tpu_custom_call", output_to_operand_aliasing={{}: (1, {})} | custom-call | tf_op jit(solution)/shard_map/fill/pallas_call | solution.py:350
  (15 shorter events, 0.1 us)
Async XLA Ops:
  0.0 2.2 %collective-permute-start = (bf16[6,96,512]{2,1,0:T(8,128)(2,1)}, bf16[6,96,512]{2,1,0:T(8,128)(2,1)S(1)}, u32[]{:S(2)}, u32[]{:S(2)}) collective-permute-start(bf16[6,96,512]{2,1,0:T(8,128)(2,1)} %bitcast.27), channel_id=1, source_target_pairs={{0,8},{8,0},{16,24},{24,16},{32,40},{40,32},{48,56},{56,48},{64,72... | collective-permute-start | bytes 1769480 | tf_op jit(solution)/shard_map/ppermute | solution.py:380
  2.2 1.1 %copy-start = (bf16[1,2,3,96,512]{4,3,2,1,0:T(8,128)(2,1)S(1)}, bf16[1,2,3,96,512]{4,3,2,1,0:T(8,128)(2,1)}, u32[]{:S(2)}) copy-start(bf16[1,2,3,96,512]{4,3,2,1,0:T(8,128)(2,1)} %param.5) | copy-start | bytes 1769476
  60.2 8.6 %collective-permute-start.3 = (bf16[18,48,128]{2,1,0:T(8,128)(2,1)S(1)}, bf16[18,48,128]{2,1,0:T(8,128)(2,1)S(1)}, u32[]{:S(2)}, u32[]{:S(2)}) collective-permute-start(bf16[18,48,128]{2,1,0:T(8,128)(2,1)S(1)} %fold.1.refs_0_), channel_id=1, source_target_pairs={{0,4},{1,5},{2,6},{3,7},{4,0},{5,1},{6,2},{7,3},{8,12},{9,13},{10,... | collective-permute-start | bytes 663560 | tf_op jit(solution)/shard_map/ppermute | solution.py:404
  62.9 9.9 %collective-permute-start.2 = (bf16[18,48,128]{2,1,0:T(8,128)(2,1)S(1)}, bf16[18,48,128]{2,1,0:T(8,128)(2,1)S(1)}, u32[]{:S(2)}, u32[]{:S(2)}) collective-permute-start(bf16[18,48,128]{2,1,0:T(8,128)(2,1)S(1)} %fold.1.refs_0_), channel_id=1, source_target_pairs={{0,3},{1,0},{2,1},{3,2},{4,7},{5,4},{6,5},{7,6},{8,11},{9,8},{10,9... | collective-permute-start | bytes 663560 | tf_op jit(solution)/shard_map/ppermute | solution.py:399
  67.0 9.4 %collective-permute-start.1 = (bf16[18,48,128]{2,1,0:T(8,128)(2,1)S(1)}, bf16[18,48,128]{2,1,0:T(8,128)(2,1)S(1)}, u32[]{:S(2)}, u32[]{:S(2)}) collective-permute-start(bf16[18,48,128]{2,1,0:T(8,128)(2,1)S(1)} %fold.1.refs_0_), channel_id=1, source_target_pairs={{0,1},{1,2},{2,3},{3,0},{4,5},{5,6},{6,7},{7,4},{8,9},{9,10},{10,1... | collective-permute-start | bytes 663560 | tf_op jit(solution)/shard_map/ppermute | solution.py:399
  68.8 8.9 %collective-permute-start.5 = (bf16[18,48,128]{2,1,0:T(8,128)(2,1)S(1)}, bf16[18,48,128]{2,1,0:T(8,128)(2,1)S(1)}, u32[]{:S(2)}, u32[]{:S(2)}) collective-permute-start(bf16[18,48,128]{2,1,0:T(8,128)(2,1)S(1)} %collective-permute-done.3.refs_3_), channel_id=1, source_target_pairs={{0,3},{1,0},{2,1},{3,2},{4,7},{5,4},{6,5},{7,6},{8,11},{9,8},{10,9... | collective-permute-start | bytes 663560 | tf_op jit(solution)/shard_map/ppermute | solution.py:399
  72.8 8.6 %collective-permute-start.4 = (bf16[18,48,128]{2,1,0:T(8,128)(2,1)S(1)}, bf16[18,48,128]{2,1,0:T(8,128)(2,1)S(1)}, u32[]{:S(2)}, u32[]{:S(2)}) collective-permute-start(bf16[18,48,128]{2,1,0:T(8,128)(2,1)S(1)} %collective-permute-done.3.refs_3_), channel_id=1, source_target_pairs={{0,1},{1,2},{2,3},{3,0},{4,5},{5,6},{6,7},{7,4},{8,9},{9,10},{10,1... | collective-permute-start | bytes 663560 | tf_op jit(solution)/shard_map/ppermute | solution.py:399
  72.9 15.4 %collective-permute-start.7 = (bf16[9,48,128]{2,1,0:T(8,128)(2,1)S(1)}, bf16[9,48,128]{2,1,0:T(8,128)(2,1)S(1)}, u32[]{:S(2)}, u32[]{:S(2)}) collective-permute-start(bf16[9,48,128]{2,1,0:T(8,128)(2,1)S(1)} %slice.17), channel_id=1, source_target_pairs={{0,3},{1,0},{2,1},{3,2},{4,7},{5,4},{6,5},{7,6},{8,11},{9,8},{10,9... | collective-permute-start | bytes 331784 | tf_op jit(solution)/shard_map/ppermute | solution.py:399
  76.4 11.9 %collective-permute-start.6 = (bf16[9,48,128]{2,1,0:T(8,128)(2,1)S(1)}, bf16[9,48,128]{2,1,0:T(8,128)(2,1)S(1)}, u32[]{:S(2)}, u32[]{:S(2)}) collective-permute-start(bf16[9,48,128]{2,1,0:T(8,128)(2,1)S(1)} %slice.16), channel_id=1, source_target_pairs={{0,1},{1,2},{2,3},{3,0},{4,5},{5,6},{6,7},{7,4},{8,9},{9,10},{10,1... | collective-permute-start | bytes 331784 | tf_op jit(solution)/shard_map/ppermute | solution.py:399
  77.7 10.6 %collective-permute-start.9 = (bf16[9,48,128]{2,1,0:T(8,128)(2,1)S(1)}, bf16[9,48,128]{2,1,0:T(8,128)(2,1)S(1)}, u32[]{:S(2)}, u32[]{:S(2)}) collective-permute-start(bf16[9,48,128]{2,1,0:T(8,128)(2,1)S(1)} %slice.19), channel_id=1, source_target_pairs={{0,3},{1,0},{2,1},{3,2},{4,7},{5,4},{6,5},{7,6},{8,11},{9,8},{10,9... | collective-permute-start | bytes 331784 | tf_op jit(solution)/shard_map/ppermute | solution.py:399
  81.4 6.8 %collective-permute-start.8 = (bf16[9,48,128]{2,1,0:T(8,128)(2,1)S(1)}, bf16[9,48,128]{2,1,0:T(8,128)(2,1)S(1)}, u32[]{:S(2)}, u32[]{:S(2)}) collective-permute-start(bf16[9,48,128]{2,1,0:T(8,128)(2,1)S(1)} %slice.18), channel_id=1, source_target_pairs={{0,1},{1,2},{2,3},{3,0},{4,5},{5,6},{6,7},{7,4},{8,9},{9,10},{10,1... | collective-permute-start | bytes 331784 | tf_op jit(solution)/shard_map/ppermute | solution.py:399

commit v5 on v4

--- a/solution.py
+++ b/solution.py
@@ -15,6 +15,7 @@
 ORDER = ((0, 1, 2, 3), (2, 0, 3, 1))
 GROUP = 8
 OWNERS = 16
+WIDE = 2
 
 
 def local_coords(site):
@@ -37,12 +38,12 @@
     return real + imag
 
 
-def pair_kernel(quarter_ref, own_ref, sib_ref, phase_ref, out_ref, vec_ref, mix_ref, pair_ref, pair2_ref, acc_ref):
+def pair_kernel(quarter_ref, own_ref, sib_ref, phase_ref, out_ref, vec_ref, mix_ref, *rest):
+    buffers, acc_ref = rest[:-1], rest[-1]
     nvec = own_ref.shape[1]
     sites = own_ref.shape[2]
     fourth = nvec // 4
     chunks = 2 * sites // LANES
-    wide = 6 * LANES
     for half, ref in enumerate((own_ref, sib_ref)):
         for step in range(sites // LANES):
             here = pl.ds(step * LANES, LANES)
@@ -58,12 +59,12 @@
                     w_imag = (cosine * imag + sine * real).astype(jnp.bfloat16)
                     first = pl.ds(2 * p * nvec, nvec)
                     second = pl.ds((2 * p + 1) * nvec, nvec)
-                    on_real = pl.ds(colour * LANES, LANES)
-                    on_imag = pl.ds((3 + colour) * LANES, LANES)
-                    mix_ref[chunk, first, on_real] = w_real
-                    mix_ref[chunk, second, on_real] = w_imag
-                    mix_ref[chunk, first, on_imag] = -w_imag
-                    mix_ref[chunk, second, on_imag] = w_real
+                    on_real = pl.ds((chunk % WIDE * 6 + colour) * LANES, LANES)
+                    on_imag = pl.ds((chunk % WIDE * 6 + 3 + colour) * LANES, LANES)
+                    mix_ref[chunk // WIDE, first, on_real] = w_real
+                    mix_ref[chunk // WIDE, second, on_real] = w_imag
+                    mix_ref[chunk // WIDE, first, on_imag] = -w_imag
+                    mix_ref[chunk // WIDE, second, on_imag] = w_real
             for m in range(4):
                 rows = pl.ds(pl.multiple_of(quarter_ref[m], 8), fourth)
                 block = pl.ds(m * fourth, fourth)
@@ -81,63 +82,72 @@
         ]
 
 
-    def build(chunk, r, into):
+    def merge(above, upper, lower):
+        return [
+            [jnp.where(above, u, w) for u, w in zip(plane_u, plane_w)]
+            for plane_u, plane_w in zip(upper, lower)
+        ]
+
+    def build(chunk, r, into, column):
+        def left(first):
+            return rows_of(chunk, (0, 1, 2), first, 1)
+
+        def right(first, count):
+            return rows_of(chunk, (0, 2, 3), first, count)
+
         pieces = [[] for _ in range(6)]
-        for unit in range(fourth // 8):
-            low = unit * 8
-            if low + 7 > r:
-                upper = cross(rows_of(chunk, (0, 1, 2), r, 1), rows_of(chunk, (0, 2, 3), low, 8))
-            if low < r:
-                lower = cross(rows_of(chunk, (0, 1, 2), 3 * fourth + r, 1), rows_of(chunk, (0, 2, 3), 3 * fourth + low, 8))
+        last = 3 * fourth
+        for low in range(0, fourth, 8):
             if low >= r:
-                found = upper
+                found = cross(left(r), right(low, 8))
             elif low + 7 <= r:
-                found = lower
+                found = cross(left(last + r), right(last + low, 8))
             else:
                 above = lax.broadcasted_iota(jnp.int32, (8, LANES), 0) > r - low
-                found = [jnp.where(above, u, w) for u, w in zip(upper, lower)]
+                found = cross(
+                    merge(above, left(r), left(last + r)),
+                    merge(above, right(low, 8), right(last + low, 8)),
+                )
             for n in range(6):
                 pieces[n].append(found[n])
         for m in range(3):
-            found = cross(rows_of(chunk, (0, 1, 2), m * fourth + r, 1), rows_of(chunk, (0, 2, 3), (m + 1) * fourth, fourth))
+            found = cross(left(m * fourth + r), right((m + 1) * fourth, fourth))
             for n in range(6):
                 pieces[n].append(found[n])
         for n in range(6):
-            into[pl.ds(r % GROUP * nvec, nvec), pl.ds(n * LANES, LANES)] = jnp.concatenate(pieces[n], axis=0).astype(jnp.bfloat16)
+            into[pl.ds(r % GROUP * nvec, nvec), pl.ds((column + n) * LANES, LANES)] = (
+                jnp.concatenate(pieces[n], axis=0).astype(jnp.bfloat16)
+            )
 
     steps = fourth // GROUP
     pieces_of = GROUP * nvec // 256
-    buffers = (pair_ref, pair2_ref)
-
-    def contract(chunk, group, source, piece):
+
+    def contract(chunk, group, piece):
         cols = pl.ds(group * GROUP * nvec + piece * 256, 256)
         acc_ref[:, cols] += lax.dot_general(
             mix_ref[chunk],
-            source[pl.ds(piece * 256, 256), :],
+            buffers[group][pl.ds(piece * 256, 256), :],
             (((1,), (1,)), ((), ())),
             preferred_element_type=jnp.float32,
         )
 
-    buffers[1][...] = jnp.zeros_like(buffers[1])
+    buffers[-1][...] = jnp.zeros_like(buffers[-1])
 
     def advance(it, carry):
-        for gs in range(2 * steps):
-            chunk, group = 2 * it + gs // steps, gs % steps
-            if gs == 0:
-                before, last = jnp.maximum(2 * it - 1, 0), steps - 1
-            else:
-                before, last = 2 * it + (gs - 1) // steps, (gs - 1) % steps
+        for group in range(steps):
+            before = jnp.maximum(it - 1, 0) if group == 0 else it
             done = 0
             for local in range(GROUP):
-                build(chunk, group * GROUP + local, buffers[gs % 2])
+                for half in range(WIDE):
+                    build(WIDE * it + half, group * GROUP + local, buffers[group], 6 * half)
                 while done < pieces_of and (done + 1) * GROUP <= (local + 1) * pieces_of:
-                    contract(before, last, buffers[(gs + 1) % 2], done)
+                    contract(before, (group - 1) % steps, done)
                     done += 1
         return carry
 
-    lax.fori_loop(0, chunks // 2, advance, 0)
+    lax.fori_loop(0, chunks // WIDE, advance, 0)
     for piece in range(pieces_of):
-        contract(chunks - 1, steps - 1, buffers[1], piece)
+        contract(chunks // WIDE - 1, steps - 1, piece)
     row = lax.broadcasted_iota(jnp.int32, (4 * nvec, 4 * nvec), 0)
     col = lax.broadcasted_iota(jnp.int32, (4 * nvec, 4 * nvec), 1)
     own = nvec // OWNERS
@@ -163,11 +173,10 @@
         out_specs=vmem,
         scratch_shapes=[
             pltpu.VMEM((chunks, 12, nvec, LANES), jnp.float32),
-            pltpu.VMEM((chunks, 4 * nvec, 6 * LANES), jnp.bfloat16),
-            pltpu.VMEM((GROUP * nvec, 6 * LANES), jnp.bfloat16),
-            pltpu.VMEM((GROUP * nvec, 6 * LANES), jnp.bfloat16),
-            pltpu.VMEM((4 * nvec, pairs), jnp.float32),
-        ],
+            pltpu.VMEM((chunks // WIDE, 4 * nvec, WIDE * 6 * LANES), jnp.bfloat16),
+        ]
+        + [pltpu.VMEM((GROUP * nvec, WIDE * 6 * LANES), jnp.bfloat16)] * (nvec // 4 // GROUP)
+        + [pltpu.VMEM((4 * nvec, pairs), jnp.float32)],
         compiler_params=pltpu.CompilerParams(vmem_limit_bytes=48 << 20),
         name="pair_sums",
     )(quarters, own, sib, phase)
@@ -401,24 +410,22 @@
         )
 
     cut = mine.shape[0] // 2
+    same, across = 4 * half, 4 * (1 - half)
+    before, after, opposite = (z + 3) % 4, (z + 1) % 4, (z + 2) % 4
+
+    def at(*order):
+        return jnp.stack(order).astype(jnp.int32)
+
     other = lax.ppermute(mine, "tm", [(n, n ^ 4) for n in range(times)])
     left, right = turn(mine, 1), turn(mine, -1)
+    full = fill(None, at(me), [(mine,)], times, rows)
+    other, full = lax.optimization_barrier((other, full))
+    left2, right2 = turn(other, 1), turn(other, -1)
     far = (turn(left[:cut], 1), turn(right[cut:], -1))
-    left2, right2 = turn(other, 1), turn(other, -1)
+    full = fill(full, at(across + z, same + before, same + after), [(other,), (left,), (right,)], times, rows)
+    left2, right2, full = lax.optimization_barrier((left2, right2, full))
     far2 = (turn(left2[:cut], 1), turn(right2[cut:], -1))
-    same, across = 4 * half, 4 * (1 - half)
-    before, after, opposite = (z + 3) % 4, (z + 1) % 4, (z + 2) % 4
-
-    def at(*order):
-        return jnp.stack(order).astype(jnp.int32)
-
-    full = fill(
-        None,
-        at(me, same + before, same + after, across + z, across + before, across + after),
-        [(mine,), (left,), (right,), (other,), (left2,), (right2,)],
-        times,
-        rows,
-    )
+    full = fill(full, at(across + before, across + after), [(left2,), (right2,)], times, rows)
     full = fill(full, at(same + opposite, across + opposite), [far, far2], times, rows)
     full = full.reshape(times, rows, -1, 2, LANES)
     return jnp.swapaxes(full, 2, 3).reshape(times, rows, 2, 2 * nvec * nvec)

time: 91.6 us -> 90.1 us (0.984)
  waiting for transfers between devices: 3.03 us -> 0.86 us
  Pallas kernels: 36.3 us -> 37.6 us
    pallas_call x2 -> x4, Pallas kernels: 9.78 us -> 12 us  [fill(): pl.pallas_call(functools.partial(fill_kernel, halves, skip), out_shape=sh...]
    ppermute x1, waiting for transfers between devices: 1.77 us -> 0.06 us  [body(): other = lax.ppermute(mine, 'tm', [(n, n ^ 4) for n in range(times)])]
    pallas_call x1, Pallas kernels: 25.5 us -> 24.5 us  [pair_sums(): pl.pallas_call(pair_kernel, out_shape=jax.ShapeDtypeStruct((4 * nvec, pai...]
  transfers between devices with their start and end apart: 10 -> 10, of which waited for: 3 -> 3; matrix products, arithmetic and copies ran while one was open for 2% -> 3% of each run, Pallas kernels for 7% -> 10%
where the time goes in v5:
time: 90.1 us; the launch traced here: 89.8 us
  Pallas kernels  37.6 us (42%)
  blocking collectives  30.3 us (34%)
  starting transfers between devices  17.6 us (20%)
  local copies, waits for them, and re-layouts  2.73 us (3%)
    all_to_all x1, blocking collectives, body(): lax.all_to_all(partial.reshape(groups, 4 * rows, -1), 'space', 0, 0, tile...  30.3 us
    pallas_call x1, Pallas kernels, pair_sums(): pl.pallas_call(pair_kernel, out_shape=jax.ShapeDtypeStruct((4 * nvec, pai...  24.5 us
    ppermute x8, starting transfers between devices, turn(): lax.ppermute(x, 'tm', [(4 * h + n, 4 * h + (n + by) % 4) for h in range(t...  14.8 us
    pallas_call x4, Pallas kernels, fill(): pl.pallas_call(functools.partial(fill_kernel, halves, skip), out_shape=sh...  12 us
    ppermute x1, starting transfers between devices, body(): other = lax.ppermute(mine, 'tm', [(n, n ^ 4) for n in range(times)])  2.78 us
    unnamed x4, local copies, waits for them, and re-layouts  1.84 us
  transfers between devices with their start and end apart: 10, of which 3 were waited for; matrix products, arithmetic and copies ran while one was open for 3% of the time, Pallas kernels for 10%

profile of v5, /device:TPU:0, one launch (start us, length us, event | category | flops | bytes accessed | tf_op | source)
XLA Modules:
  0.0 89.8 jit_solution(9804020653360152107)
XLA Ops:
  0.0 0.8 copy.10
  0.8 0.8 constant_dynamic-slice_fusion.1
  1.6 0.1 add_bitcast_fusion.1
  1.7 0.1 add_bitcast_fusion
  1.8 0.1 multiply_reduce_fusion
  1.9 0.1 fusion.4
  2.1 0.1 collective-permute-done.sib_ref
  2.2 1.1 %copy-done = bf16[1,2,3,96,512]{4,3,2,1,0:T(8,128)(2,1)S(1)} copy-done((bf16[1,2,3,96,512]{4,3,2,1,0:T(8,128)(2,1)S(1)}, bf16[1,2,3,96,512]{4,3,2,1,0:T(8,128)(2,1)}, u32[]{:S(2)}) %copy-start) | copy-done | bytes 589848
  3.3 24.5 %pair_sums.1 = bf16[384,2304]{1,0:T(8,128)(2,1)S(1)} custom-call(s32[4]{0:T(128)S(1)} %broadcast_select_fusion.quarter_ref, bf16[6,96,512]{2,1,0:T(8,128)(2,1)S(1)} %bitcast.28, bf16[6,96,512]{2,1,0:T(8,128)(2,1)S(1)} %collective-permute-done.sib_ref, f32[4,1024]{1,0:T(4,128)S(1)} %reshape.194.phase_ref), custom_call_target="tpu_custom_call" | custom-call | tf_op jit(solution)/shard_map/pair_sums/pallas_call | solution.py:169
  27.8 30.3 %all_to_all.5.parts_ref = bf16[16,24,2304]{2,1,0:T(8,128)(2,1)S(1)} all-to-all(bf16[16,24,2304]{2,1,0:T(8,128)(2,1)S(1)} %bitcast.26), channel_id=1, replica_groups=mesh['space'=16,'tm'=8] {'space'}, dimensions={0} | all-to-all | bytes 3538944 | tf_op jit(solution)/shard_map/all_to_all | solution.py:402
  58.1 1.0 %fold.1.refs_0_ = bf16[18,48,128]{2,1,0:T(8,128)(2,1)S(1)} custom-call(bf16[16,24,2304]{2,1,0:T(8,128)(2,1)S(1)} %all_to_all.5.parts_ref), custom_call_target="tpu_custom_call" | custom-call | tf_op jit(solution)/shard_map/fold/pallas_call | solution.py:234
  59.1 2.8 %collective-permute-start.1 = (bf16[18,48,128]{2,1,0:T(8,128)(2,1)S(1)}, bf16[18,48,128]{2,1,0:T(8,128)(2,1)S(1)}, u32[]{:S(2)}, u32[]{:S(2)}) collective-permute-start(bf16[18,48,128]{2,1,0:T(8,128)(2,1)S(1)} %fold.1.refs_0_), channel_id=1, source_target_pairs={{0,4},{1,5},{2,6},{3,7},{4,0},{5,1},{6,2},{7,3},{8,12},{9,13},{10,... | collective-permute-start | bytes 663560 | tf_op jit(solution)/shard_map/ppermute | solution.py:419
  61.9 4.1 %collective-permute-start.5 = (bf16[18,48,128]{2,1,0:T(8,128)(2,1)S(1)}, bf16[18,48,128]{2,1,0:T(8,128)(2,1)S(1)}, u32[]{:S(2)}, u32[]{:S(2)}) collective-permute-start(bf16[18,48,128]{2,1,0:T(8,128)(2,1)S(1)} %fold.1.refs_0_), channel_id=1, source_target_pairs={{0,3},{1,0},{2,1},{3,2},{4,7},{5,4},{6,5},{7,6},{8,11},{9,8},{10,9... | collective-permute-start | bytes 663560 | tf_op jit(solution)/shard_map/ppermute | solution.py:408
  66.0 1.7 %fill.4.refs_0_ = f32[8,6,288,128]{3,2,1,0:T(8,128)} custom-call(s32[1]{0:T(128)} %bitcast.8.order_ref, bf16[18,48,128]{2,1,0:T(8,128)(2,1)S(1)} %fold.1.refs_0_), custom_call_target="tpu_custom_call" | custom-call | tf_op jit(solution)/shard_map/fill/pallas_call | solution.py:359
  67.7 0.1 collective-permute-done.1.refs_1_
  67.8 4.0 %collective-permute-start.3 = (bf16[18,48,128]{2,1,0:T(8,128)(2,1)S(1)}, bf16[18,48,128]{2,1,0:T(8,128)(2,1)S(1)}, u32[]{:S(2)}, u32[]{:S(2)}) collective-permute-start(bf16[18,48,128]{2,1,0:T(8,128)(2,1)S(1)} %collective-permute-done.1.refs_1_), channel_id=1, source_target_pairs={{0,3},{1,0},{2,1},{3,2},{4,7},{5,4},{6,5},{7,6},{8,11},{9,8},{10,9... | collective-permute-start | bytes 663560 | tf_op jit(solution)/shard_map/ppermute | solution.py:408
  71.8 0.0 collective-permute-start.2
  71.8 0.1 pad_add_fusion.1.order_ref
  71.9 0.1 pad_add_fusion.3.order_ref
  72.0 0.0 collective-permute-done.5.refs_3_
  72.0 3.3 %collective-permute-start.7 = (bf16[9,48,128]{2,1,0:T(8,128)(2,1)S(1)}, bf16[9,48,128]{2,1,0:T(8,128)(2,1)S(1)}, u32[]{:S(2)}, u32[]{:S(2)}) collective-permute-start(bf16[9,48,128]{2,1,0:T(8,128)(2,1)S(1)} %slice.17), channel_id=1, source_target_pairs={{0,3},{1,0},{2,1},{3,2},{4,7},{5,4},{6,5},{7,6},{8,11},{9,8},{10,9... | collective-permute-start | bytes 331784 | tf_op jit(solution)/shard_map/ppermute | solution.py:408
  75.3 0.0 collective-permute-done.4.refs_2_
  75.3 0.1 collective-permute-start.6
  75.4 4.0 %fill.5.refs_0_ = f32[8,6,288,128]{3,2,1,0:T(8,128)} custom-call(s32[3]{0:T(128)S(1)} %pad_add_fusion.3.order_ref, f32[8,6,288,128]{3,2,1,0:T(8,128)} %fill.4.refs_0_, bf16[18,48,128]{2,1,0:T(8,128)(2,1)S(1)} %collective-permute-done.1.refs_1_, bf16[18,48,128]{2,1,0:T(8,128)(2,1)S(1)} %collective-permute-done.4.refs_2_, ...), custom_call_target="tpu_custom_call", output_to_operand_aliasing={{}: (1, {})} | custom-call | tf_op jit(solution)/shard_map/fill/pallas_call | solution.py:359
  79.4 0.0 collective-permute-done.3.refs_2_
  79.4 0.7 collective-permute-done.2.refs_1_
  80.2 0.1 collective-permute-start.8
  80.2 3.2 %collective-permute-start.9 = (bf16[9,48,128]{2,1,0:T(8,128)(2,1)S(1)}, bf16[9,48,128]{2,1,0:T(8,128)(2,1)S(1)}, u32[]{:S(2)}, u32[]{:S(2)}) collective-permute-start(bf16[9,48,128]{2,1,0:T(8,128)(2,1)S(1)} %slice.15), channel_id=1, source_target_pairs={{0,3},{1,0},{2,1},{3,2},{4,7},{5,4},{6,5},{7,6},{8,11},{9,8},{10,9... | collective-permute-start | bytes 331784 | tf_op jit(solution)/shard_map/ppermute | solution.py:408
  83.5 0.1 pad_add_fusion.2.order_ref
  83.5 3.1 %fill.6.refs_0_ = f32[8,6,288,128]{3,2,1,0:T(8,128)} custom-call(s32[2]{0:T(128)S(1)} %pad_add_fusion.2.order_ref, f32[8,6,288,128]{3,2,1,0:T(8,128)} %fill.5.refs_0_, bf16[18,48,128]{2,1,0:T(8,128)(2,1)S(1)} %collective-permute-done.2.refs_1_, bf16[18,48,128]{2,1,0:T(8,128)(2,1)S(1)} %collective-permute-done.3.refs_2_), custom_call_target="tpu_custom_call", output_to_operand_aliasing={{}: (1, {})} | custom-call | tf_op jit(solution)/shard_map/fill/pallas_call | solution.py:359
  86.7 0.0 collective-permute-done.7.refs_2_
  86.7 3.1 %fill.7 = f32[8,6,288,128]{3,2,1,0:T(8,128)} custom-call(s32[2]{0:T(128)S(1)} %pad_add_fusion.1.order_ref, f32[8,6,288,128]{3,2,1,0:T(8,128)} %fill.6.refs_0_, bf16[9,48,128]{2,1,0:T(8,128)(2,1)S(1)} %collective-permute-done.6.refs_1_, bf16[9,48,128]{2,1,0:T(8,128)(2,1)S(1)} %collective-permute-done.7.refs_2_, ...), custom_call_target="tpu_custom_call", output_to_operand_aliasing={{}: (1, {})} | custom-call | tf_op jit(solution)/shard_map/fill/pallas_call | solution.py:359
  (18 shorter events, 0.1 us)
Async XLA Ops:
  0.0 2.2 %collective-permute-start = (bf16[6,96,512]{2,1,0:T(8,128)(2,1)}, bf16[6,96,512]{2,1,0:T(8,128)(2,1)S(1)}, u32[]{:S(2)}, u32[]{:S(2)}) collective-permute-start(bf16[6,96,512]{2,1,0:T(8,128)(2,1)} %bitcast.27), channel_id=1, source_target_pairs={{0,8},{8,0},{16,24},{24,16},{32,40},{40,32},{48,56},{56,48},{64,72... | collective-permute-start | bytes 1769480 | tf_op jit(solution)/shard_map/ppermute | solution.py:389
  2.2 1.1 %copy-start = (bf16[1,2,3,96,512]{4,3,2,1,0:T(8,128)(2,1)S(1)}, bf16[1,2,3,96,512]{4,3,2,1,0:T(8,128)(2,1)}, u32[]{:S(2)}) copy-start(bf16[1,2,3,96,512]{4,3,2,1,0:T(8,128)(2,1)} %param.5) | copy-start | bytes 1769476
  59.1 8.6 %collective-permute-start.1 = (bf16[18,48,128]{2,1,0:T(8,128)(2,1)S(1)}, bf16[18,48,128]{2,1,0:T(8,128)(2,1)S(1)}, u32[]{:S(2)}, u32[]{:S(2)}) collective-permute-start(bf16[18,48,128]{2,1,0:T(8,128)(2,1)S(1)} %fold.1.refs_0_), channel_id=1, source_target_pairs={{0,4},{1,5},{2,6},{3,7},{4,0},{5,1},{6,2},{7,3},{8,12},{9,13},{10,... | collective-permute-start | bytes 663560 | tf_op jit(solution)/shard_map/ppermute | solution.py:419
  61.9 10.0 %collective-permute-start.5 = (bf16[18,48,128]{2,1,0:T(8,128)(2,1)S(1)}, bf16[18,48,128]{2,1,0:T(8,128)(2,1)S(1)}, u32[]{:S(2)}, u32[]{:S(2)}) collective-permute-start(bf16[18,48,128]{2,1,0:T(8,128)(2,1)S(1)} %fold.1.refs_0_), channel_id=1, source_target_pairs={{0,3},{1,0},{2,1},{3,2},{4,7},{5,4},{6,5},{7,6},{8,11},{9,8},{10,9... | collective-permute-start | bytes 663560 | tf_op jit(solution)/shard_map/ppermute | solution.py:408
  66.0 9.3 %collective-permute-start.4 = (bf16[18,48,128]{2,1,0:T(8,128)(2,1)S(1)}, bf16[18,48,128]{2,1,0:T(8,128)(2,1)S(1)}, u32[]{:S(2)}, u32[]{:S(2)}) collective-permute-start(bf16[18,48,128]{2,1,0:T(8,128)(2,1)S(1)} %fold.1.refs_0_), channel_id=1, source_target_pairs={{0,1},{1,2},{2,3},{3,0},{4,5},{5,6},{6,7},{7,4},{8,9},{9,10},{10,1... | collective-permute-start | bytes 663560 | tf_op jit(solution)/shard_map/ppermute | solution.py:408
  67.8 11.7 %collective-permute-start.3 = (bf16[18,48,128]{2,1,0:T(8,128)(2,1)S(1)}, bf16[18,48,128]{2,1,0:T(8,128)(2,1)S(1)}, u32[]{:S(2)}, u32[]{:S(2)}) collective-permute-start(bf16[18,48,128]{2,1,0:T(8,128)(2,1)S(1)} %collective-permute-done.1.refs_1_), channel_id=1, source_target_pairs={{0,3},{1,0},{2,1},{3,2},{4,7},{5,4},{6,5},{7,6},{8,11},{9,8},{10,9... | collective-permute-start | bytes 663560 | tf_op jit(solution)/shard_map/ppermute | solution.py:408
  71.8 8.3 %collective-permute-start.2 = (bf16[18,48,128]{2,1,0:T(8,128)(2,1)S(1)}, bf16[18,48,128]{2,1,0:T(8,128)(2,1)S(1)}, u32[]{:S(2)}, u32[]{:S(2)}) collective-permute-start(bf16[18,48,128]{2,1,0:T(8,128)(2,1)S(1)} %collective-permute-done.1.refs_1_), channel_id=1, source_target_pairs={{0,1},{1,2},{2,3},{3,0},{4,5},{5,6},{6,7},{7,4},{8,9},{9,10},{10,1... | collective-permute-start | bytes 663560 | tf_op jit(solution)/shard_map/ppermute | solution.py:408
  72.0 14.7 %collective-permute-start.7 = (bf16[9,48,128]{2,1,0:T(8,128)(2,1)S(1)}, bf16[9,48,128]{2,1,0:T(8,128)(2,1)S(1)}, u32[]{:S(2)}, u32[]{:S(2)}) collective-permute-start(bf16[9,48,128]{2,1,0:T(8,128)(2,1)S(1)} %slice.17), channel_id=1, source_target_pairs={{0,3},{1,0},{2,1},{3,2},{4,7},{5,4},{6,5},{7,6},{8,11},{9,8},{10,9... | collective-permute-start | bytes 331784 | tf_op jit(solution)/shard_map/ppermute | solution.py:408
  75.3 11.4 %collective-permute-start.6 = (bf16[9,48,128]{2,1,0:T(8,128)(2,1)S(1)}, bf16[9,48,128]{2,1,0:T(8,128)(2,1)S(1)}, u32[]{:S(2)}, u32[]{:S(2)}) collective-permute-start(bf16[9,48,128]{2,1,0:T(8,128)(2,1)S(1)} %slice.16), channel_id=1, source_target_pairs={{0,1},{1,2},{2,3},{3,0},{4,5},{5,6},{6,7},{7,4},{8,9},{9,10},{10,1... | collective-permute-start | bytes 331784 | tf_op jit(solution)/shard_map/ppermute | solution.py:408
  80.2 6.5 %collective-permute-start.8 = (bf16[9,48,128]{2,1,0:T(8,128)(2,1)S(1)}, bf16[9,48,128]{2,1,0:T(8,128)(2,1)S(1)}, u32[]{:S(2)}, u32[]{:S(2)}) collective-permute-start(bf16[9,48,128]{2,1,0:T(8,128)(2,1)S(1)} %slice.14), channel_id=1, source_target_pairs={{0,1},{1,2},{2,3},{3,0},{4,5},{5,6},{6,7},{7,4},{8,9},{9,10},{10,1... | collective-permute-start | bytes 331784 | tf_op jit(solution)/shard_map/ppermute | solution.py:408
  80.2 6.4 %collective-permute-start.9 = (bf16[9,48,128]{2,1,0:T(8,128)(2,1)S(1)}, bf16[9,48,128]{2,1,0:T(8,128)(2,1)S(1)}, u32[]{:S(2)}, u32[]{:S(2)}) collective-permute-start(bf16[9,48,128]{2,1,0:T(8,128)(2,1)S(1)} %slice.15), channel_id=1, source_target_pairs={{0,3},{1,0},{2,1},{3,2},{4,7},{5,4},{6,5},{7,6},{8,11},{9,8},{10,9... | collective-permute-start | bytes 331784 | tf_op jit(solution)/shard_map/ppermute | solution.py:408

commit v6 on v5

--- a/solution.py
+++ b/solution.py
@@ -1,4 +1,5 @@
 import functools
+import itertools
 import math
 
 import jax
@@ -13,7 +14,6 @@
 BRICK_Z = 8
 LANES = 128
 ORDER = ((0, 1, 2, 3), (2, 0, 3, 1))
-GROUP = 8
 OWNERS = 16
 WIDE = 2
 
@@ -38,13 +38,24 @@
     return real + imag
 
 
-def pair_kernel(quarter_ref, own_ref, sib_ref, phase_ref, out_ref, vec_ref, mix_ref, *rest):
-    buffers, acc_ref = rest[:-1], rest[-1]
+def pair_kernel(count, opening, closing, quarter_ref, *refs):
+    blocks, phase_ref = refs[:count], refs[count]
+    refs = refs[count + 1 :]
+    if not opening:
+        so_far_ref, refs = refs[0], refs[1:]
+    out_ref, vec_ref, mix_ref, *buffers = refs
+    if closing:
+        buffers, acc_ref = buffers[:-1], buffers[-1]
+    else:
+        acc_ref = out_ref
+    own_ref = blocks[0]
     nvec = own_ref.shape[1]
     sites = own_ref.shape[2]
     fourth = nvec // 4
-    chunks = 2 * sites // LANES
-    for half, ref in enumerate((own_ref, sib_ref)):
+    chunks = count * sites // LANES
+    share = fourth // 2
+    start = quarter_ref[4]
+    for half, ref in enumerate(blocks):
         for step in range(sites // LANES):
             here = pl.ds(step * LANES, LANES)
             chunk = half * (sites // LANES) + step
@@ -73,7 +84,7 @@
                     imag = ref[3 + colour, rows, here].astype(jnp.float32)
                     for n, value in enumerate((real, imag, real + imag, imag - real)):
                         vec_ref[chunk, 3 * n + colour, block, :] = value
-    acc_ref[...] = jnp.zeros_like(acc_ref)
+    acc_ref[...] = jnp.zeros_like(acc_ref) if opening else so_far_ref[...]
 
     def rows_of(chunk, planes, first, count):
         return [
@@ -97,125 +108,133 @@
 
         pieces = [[] for _ in range(6)]
         last = 3 * fourth
+        row = start + r
         for low in range(0, fourth, 8):
-            if low >= r:
-                found = cross(left(r), right(low, 8))
+            if low >= r + share:
+                found = cross(left(row), right(low, 8))
             elif low + 7 <= r:
-                found = cross(left(last + r), right(last + low, 8))
+                found = cross(left(last + row), right(last + low, 8))
             else:
-                above = lax.broadcasted_iota(jnp.int32, (8, LANES), 0) > r - low
+                above = lax.broadcasted_iota(jnp.int32, (8, LANES), 0) + low > row
                 found = cross(
-                    merge(above, left(r), left(last + r)),
+                    merge(above, left(row), left(last + row)),
                     merge(above, right(low, 8), right(last + low, 8)),
                 )
             for n in range(6):
                 pieces[n].append(found[n])
         for m in range(3):
-            found = cross(left(m * fourth + r), right((m + 1) * fourth, fourth))
+            found = cross(left(m * fourth + row), right((m + 1) * fourth, fourth))
             for n in range(6):
                 pieces[n].append(found[n])
         for n in range(6):
-            into[pl.ds(r % GROUP * nvec, nvec), pl.ds((column + n) * LANES, LANES)] = (
+            into[pl.ds(r * nvec, nvec), pl.ds((column + n) * LANES, LANES)] = (
                 jnp.concatenate(pieces[n], axis=0).astype(jnp.bfloat16)
             )
 
-    steps = fourth // GROUP
-    pieces_of = GROUP * nvec // 256
-
-    def contract(chunk, group, piece):
-        cols = pl.ds(group * GROUP * nvec + piece * 256, 256)
+    width = share * nvec
+    tiles = [(low, min(256, width - low)) for low in range(0, width, 256)]
+
+    def contract(chunk, source, tile):
+        cols = pl.ds(*tiles[tile])
         acc_ref[:, cols] += lax.dot_general(
-            mix_ref[chunk],
-            buffers[group][pl.ds(piece * 256, 256), :],
-            (((1,), (1,)), ((), ())),
-            preferred_element_type=jnp.float32,
+            mix_ref[chunk], source[cols, :], (((1,), (1,)), ((), ())), preferred_element_type=jnp.float32
         )
 
-    buffers[-1][...] = jnp.zeros_like(buffers[-1])
+    trips = chunks // WIDE // 2
+    if trips > 1:
+        buffers[1][...] = jnp.zeros_like(buffers[1])
 
     def advance(it, carry):
-        for group in range(steps):
-            before = jnp.maximum(it - 1, 0) if group == 0 else it
+        for turn in range(2):
+            chunk = 2 * it + turn
             done = 0
-            for local in range(GROUP):
+            for r in range(share):
                 for half in range(WIDE):
-                    build(WIDE * it + half, group * GROUP + local, buffers[group], 6 * half)
-                while done < pieces_of and (done + 1) * GROUP <= (local + 1) * pieces_of:
-                    contract(before, (group - 1) % steps, done)
+                    build(WIDE * chunk + half, r, buffers[turn], 6 * half)
+                while (trips > 1 or turn) and done < len(tiles) and (done + 1) * share <= (r + 1) * len(tiles):
+                    contract(jnp.maximum(chunk - 1, 0), buffers[1 - turn], done)
                     done += 1
         return carry
 
-    lax.fori_loop(0, chunks // WIDE, advance, 0)
-    for piece in range(pieces_of):
-        contract(chunks // WIDE - 1, steps - 1, piece)
+    if trips > 1:
+        lax.fori_loop(0, trips, advance, 0)
+    else:
+        advance(0, 0)
+    for tile in range(len(tiles)):
+        contract(chunks // WIDE - 1, buffers[1], tile)
+    if not closing:
+        return
     row = lax.broadcasted_iota(jnp.int32, (4 * nvec, 4 * nvec), 0)
     col = lax.broadcasted_iota(jnp.int32, (4 * nvec, 4 * nvec), 1)
     own = nvec // OWNERS
     source = row % (4 * own) // own * nvec + row // (4 * own) * own + row % own
     perm = jnp.where(col == source, 1.0, 0.0).astype(jnp.bfloat16)
-    for group in range(fourth // GROUP):
-        width = GROUP * nvec
-        cols = pl.ds(group * width, width)
+    for low in range(0, width, 3 * LANES):
+        cols = pl.ds(low, 3 * LANES)
         out_ref[:, cols] = jnp.dot(
             perm, acc_ref[:, cols].astype(jnp.bfloat16), preferred_element_type=jnp.float32
         ).astype(jnp.bfloat16)
 
 
-def pair_sums(quarters, own, sib, phase):
-    nvec, sites = own.shape[1], own.shape[2]
-    chunks = 2 * sites // LANES
-    pairs = nvec // 4 * nvec
+def pair_sums(quarters, blocks, phase, so_far, last):
+    nvec, sites = blocks[0].shape[1:]
+    count = len(blocks)
+    chunks = count * sites // LANES
+    pairs = nvec // 8 * nvec
     vmem = pl.BlockSpec(memory_space=pltpu.VMEM)
+    earlier = [] if so_far is None else [so_far]
+    total = pltpu.VMEM((4 * nvec, pairs), jnp.float32)
     return pl.pallas_call(
-        pair_kernel,
-        out_shape=jax.ShapeDtypeStruct((4 * nvec, pairs), jnp.bfloat16),
-        in_specs=[pl.BlockSpec(memory_space=pltpu.SMEM), vmem, vmem, vmem],
+        functools.partial(pair_kernel, count, so_far is None, last),
+        out_shape=jax.ShapeDtypeStruct((4 * nvec, pairs), jnp.bfloat16 if last else jnp.float32),
+        in_specs=[pl.BlockSpec(memory_space=pltpu.SMEM)] + [vmem] * (count + 1 + len(earlier)),
         out_specs=vmem,
         scratch_shapes=[
             pltpu.VMEM((chunks, 12, nvec, LANES), jnp.float32),
             pltpu.VMEM((chunks // WIDE, 4 * nvec, WIDE * 6 * LANES), jnp.bfloat16),
+            pltpu.VMEM((pairs, WIDE * 6 * LANES), jnp.bfloat16),
+            pltpu.VMEM((pairs, WIDE * 6 * LANES), jnp.bfloat16),
         ]
-        + [pltpu.VMEM((GROUP * nvec, WIDE * 6 * LANES), jnp.bfloat16)] * (nvec // 4 // GROUP)
-        + [pltpu.VMEM((4 * nvec, pairs), jnp.float32)],
+        + ([total] if last else []),
         compiler_params=pltpu.CompilerParams(vmem_limit_bytes=48 << 20),
         name="pair_sums",
-    )(quarters, own, sib, phase)
+    )(quarters, *blocks, phase, *earlier)
 
 
 def fold_kernel(scale, parts_ref, out_ref, flat_ref):
-    chips = parts_ref.shape[0] // 2
+    chips = parts_ref.shape[0] // 4
     rows = parts_ref.shape[1]
     lane = lax.broadcasted_iota(jnp.int32, (rows, LANES), 1)
     tiles = parts_ref.shape[2] // LANES
     span = flat_ref.shape[0] // rows
-    for core in range(2):
-        for trio in range(tiles // 3):
-            cols = [pl.ds((3 * trio + n) * LANES, LANES) for n in range(3)]
-            x = []
-            for n in range(3):
-                total = parts_ref[core, :, cols[n]].astype(jnp.float32)
-                for chip in range(1, chips):
-                    total += parts_ref[2 * chip + core, :, cols[n]].astype(jnp.float32)
-                x.append(total * scale)
-            found = [
-                x[0],
-                jnp.where(lane < 32, pltpu.roll(x[0], 32, 1), pltpu.roll(x[1], 32, 1)),
-                jnp.where(lane < 64, pltpu.roll(x[1], 64, 1), pltpu.roll(x[2], 64, 1)),
-                pltpu.roll(x[2], 96, 1),
-            ]
-            for n in range(4):
-                value = found[n]
-                if core == 1:
-                    value = jnp.where(
-                        lane < 24,
-                        pltpu.roll(value, 104, 1),
-                        jnp.where(
-                            lane < 48,
-                            pltpu.roll(value, 80, 1),
-                            jnp.where(lane < 72, pltpu.roll(value, 48, 1), pltpu.roll(value, 24, 1)),
-                        ),
-                    )
-                flat_ref[pl.ds(core * span // 2 + 4 * trio + n, rows, stride=span), :] = value
+    for core, side, trio in itertools.product(range(2), range(2), range(tiles // 3)):
+        cols = [pl.ds((3 * trio + n) * LANES, LANES) for n in range(3)]
+        x = []
+        for n in range(3):
+            total = 0.0
+            for chip in range(side * chips, (side + 1) * chips):
+                total += parts_ref[2 * chip + core, :, cols[n]].astype(jnp.float32)
+            x.append(total * scale)
+        found = [
+            x[0],
+            jnp.where(lane < 32, pltpu.roll(x[0], 32, 1), pltpu.roll(x[1], 32, 1)),
+            jnp.where(lane < 64, pltpu.roll(x[1], 64, 1), pltpu.roll(x[2], 64, 1)),
+            pltpu.roll(x[2], 96, 1),
+        ]
+        for n in range(4):
+            value = found[n]
+            if core == 1:
+                value = jnp.where(
+                    lane < 24,
+                    pltpu.roll(value, 104, 1),
+                    jnp.where(
+                        lane < 48,
+                        pltpu.roll(value, 80, 1),
+                        jnp.where(lane < 72, pltpu.roll(value, 48, 1), pltpu.roll(value, 24, 1)),
+                    ),
+                )
+            first = core * span // 2 + side * span // 4 + 4 * trio + n
+            flat_ref[pl.ds(first, rows, stride=span), :] = value
     wide = lax.broadcasted_iota(jnp.int32, (span, LANES), 1)
     kept = out_ref.shape[0]
     for last in range(rows - kept):
@@ -229,7 +248,7 @@
 
 def fold(parts, scale):
     groups, rows, pairs = parts.shape
-    span = 2 * pairs // 96
+    span = 4 * pairs // 96
     vmem = pl.BlockSpec(memory_space=pltpu.VMEM)
     return pl.pallas_call(
         functools.partial(fold_kernel, scale),
@@ -386,19 +405,28 @@
     fourth = nvec // 4
     place = lax.axis_index("space")
     own = vectors.reshape(6, nvec, sites)
-    sib = lax.ppermute(own, "space", [(n, n ^ 1) for n in range(groups)])
-    corner = jnp.stack([offsets[place], offsets[place ^ 1]])
+    half_of = groups // 2
+    swap = [(n, n ^ 1) for n in range(groups)]
+    sib = lax.ppermute(own, "space", swap)
+    near = lax.ppermute(own, "space", [(n, n ^ half_of) for n in range(groups)])
+    corner = jnp.stack([offsets[place ^ n] for n in (0, 1, half_of, half_of + 1)])
     coords = (
         local_coords(jnp.arange(sites, dtype=jnp.int32))[:, None, :]
         + jnp.transpose(corner)[:, :, None]
-    ).reshape(3, 2 * sites)
-    phase = phases(momenta, coords).reshape(4, 2 * sites)
+    ).reshape(3, 4 * sites)
+    phase = phases(momenta, coords).reshape(4, 4 * sites)
     quarters = jnp.where(
         place % 2 == 0,
         jnp.array([fourth * n for n in ORDER[0]], jnp.int32),
         jnp.array([fourth * n for n in ORDER[1]], jnp.int32),
     )
-    partial = pair_sums(quarters, own, sib, phase)
+    share = fourth // 2 * (place // half_of)
+    quarters = jnp.concatenate([quarters, share[None].astype(jnp.int32)])
+    sums = pair_sums(quarters, [own, sib], phase[:, : 2 * sites], None, False)
+    near, sums = lax.optimization_barrier((near, sums))
+    beyond = lax.ppermute(near, "space", swap)
+    sums = pair_sums(quarters, [near], phase[:, 2 * sites : 3 * sites], sums, False)
+    partial = pair_sums(quarters, [beyond], phase[:, 3 * sites :], sums, True)
     parts = lax.all_to_all(partial.reshape(groups, 4 * rows, -1), "space", 0, 0, tiled=False)
     mine = fold(parts, 1.0 / math.sqrt(sites * groups))
     me = lax.axis_index("tm")

time: 90.1 us -> 86.3 us (0.958)
  blocking collectives: 30.3 us -> 20.7 us
  Pallas kernels: 37.6 us -> 41.5 us
  starting transfers between devices: 17.6 us -> 20 us
    all_to_all x1, blocking collectives: 30.3 us -> 20.7 us  [body(): lax.all_to_all(partial.reshape(groups, 4 * rows, -1), 'space', 0, 0, tile...]
    pallas_call x1 -> x3, Pallas kernels: 24.5 us -> 28.5 us  [pair_sums(): pl.pallas_call(functools.partial(pair_kernel, count, so_far is None, last...]
    ppermute x1 -> x3, starting transfers between devices: 0.01 us -> 2.71 us  [the longest x1 1.57 us: body(): near = lax.ppermute(own, 'space', [(n, n ^ half_of) for n in range(groups)])]
  transfers between devices with their start and end apart: 10 -> 12, of which waited for: 3 -> 0; matrix products, arithmetic and copies ran while one was open for 3% -> 3% of each run, Pallas kernels for 10% -> 34%
where the time goes in v6:
time: 86.3 us; the launch traced here: 86.1 us
  Pallas kernels  41.5 us (48%)
  blocking collectives  20.7 us (24%)
  starting transfers between devices  20 us (23%)
  local copies, waits for them, and re-layouts  2.86 us (3%)
    pallas_call x3, Pallas kernels, pair_sums(): pl.pallas_call(functools.partial(pair_kernel, count, so_far is None, last...  28.5 us
    all_to_all x1, blocking collectives, body(): lax.all_to_all(partial.reshape(groups, 4 * rows, -1), 'space', 0, 0, tile...  20.7 us
    ppermute x8, starting transfers between devices, turn(): lax.ppermute(x, 'tm', [(4 * h + n, 4 * h + (n + by) % 4) for h in range(t...  14.2 us
    pallas_call x4, Pallas kernels, fill(): pl.pallas_call(functools.partial(fill_kernel, halves, skip), out_shape=sh...  12 us
    ppermute x1, starting transfers between devices, body(): other = lax.ppermute(mine, 'tm', [(n, n ^ 4) for n in range(times)])  3.11 us
    unnamed x4, local copies, waits for them, and re-layouts  1.85 us
  transfers between devices with their start and end apart: 12, of which 0 were waited for; matrix products, arithmetic and copies ran while one was open for 3% of the time, Pallas kernels for 34%

profile of v6, /device:TPU:0, one launch (start us, length us, event | category | flops | bytes accessed | tf_op | source)
XLA Modules:
  0.0 86.1 jit_solution(9688749217881911717)
XLA Ops:
  0.0 1.6 %collective-permute-start = (bf16[6,96,512]{2,1,0:T(8,128)(2,1)}, bf16[6,96,512]{2,1,0:T(8,128)(2,1)S(1)}, u32[]{:S(2)}, u32[]{:S(2)}) collective-permute-start(bf16[6,96,512]{2,1,0:T(8,128)(2,1)} %bitcast.29), channel_id=1, source_target_pairs={{0,64},{8,72},{16,80},{24,88},{32,96},{40,104},{48,112},{56,120},{... | collective-permute-start | bytes 1769480 | tf_op jit(solution)/shard_map/ppermute | solution.py:411
  1.6 0.9 %constant_dynamic-slice_fusion.3 = (s32[1,3]{0,1:T(4,128)S(1)}, s32[1,3]{0,1:T(4,128)S(1)}, s32[1,3]{0,1:T(4,128)S(1)}, s32[1,3]{0,1:T(4,128)S(1)}) fusion(s32[16,3]{0,1:T(4,128)} %param.7, s32[]{:T(128)S(6)} %select_n.126, s32[]{:T(128)S(6)} %select_n.127, s32[]{:T(128)S(6)} %select_n.129, s32[]{:T(128)S(6)} %select_n.128), kind=kLoop, calls=%fused_computation.28 | loop fusion | bytes 112 | tf_op jit(solution)/shard_map/dynamic_slice | solution.py:412
  2.6 0.1 add_bitcast_fusion.1
  2.6 0.1 add_bitcast_fusion
  2.7 0.8 copy.10
  3.5 0.1 multiply_reduce_fusion
  3.6 0.3 fusion.4
  4.0 0.1 pad_add_fusion.3.quarter_ref
  4.1 0.0 collective-permute-done.1.refs_1_
  4.1 1.1 %copy-done = bf16[1,2,3,96,512]{4,3,2,1,0:T(8,128)(2,1)S(1)} copy-done((bf16[1,2,3,96,512]{4,3,2,1,0:T(8,128)(2,1)S(1)}, bf16[1,2,3,96,512]{4,3,2,1,0:T(8,128)(2,1)}, u32[]{:S(2)}) %copy-start) | copy-done | bytes 589848
  5.2 13.9 %pair_sums.3.refs_2_ = f32[384,1152]{1,0:T(8,128)S(1)} custom-call(s32[5]{0:T(128)S(1)} %pad_add_fusion.3.quarter_ref, bf16[6,96,512]{2,1,0:T(8,128)(2,1)S(1)} %bitcast.30, bf16[6,96,512]{2,1,0:T(8,128)(2,1)S(1)} %collective-permute-done.1.refs_1_, f32[4,1024]{1,0:T(4,128)S(1)} %slice.28.refs_2_), custom_call_target="tpu_custom_call" | custom-call | tf_op jit(solution)/shard_map/pair_sums/pallas_call | solution.py:187
  19.1 1.1 %collective-permute-start.2 = (bf16[6,96,512]{2,1,0:T(8,128)(2,1)S(1)}, bf16[6,96,512]{2,1,0:T(8,128)(2,1)S(1)}, u32[]{:S(2)}, u32[]{:S(2)}) collective-permute-start(bf16[6,96,512]{2,1,0:T(8,128)(2,1)S(1)} %collective-permute-done.refs_0_), channel_id=1, source_target_pairs={{0,8},{8,0},{16,24},{24,16},{32,40},{40,32},{48,56},{56,48},{64,72... | collective-permute-start | bytes 1769480 | tf_op jit(solution)/shard_map/ppermute | solution.py:427
  20.2 6.7 %pair_sums.4.refs_2_ = f32[384,1152]{1,0:T(8,128)S(1)} custom-call(s32[5]{0:T(128)S(1)} %pad_add_fusion.3.quarter_ref, bf16[6,96,512]{2,1,0:T(8,128)(2,1)S(1)} %collective-permute-done.refs_0_, f32[4,512]{1,0:T(4,128)S(1)} %get-tuple-element.19.refs_1_, f32[384,1152]{1,0:T(8,128)S(1)} %pair_sums.3.refs_2_), custom_call_target="tpu_custom_call" | custom-call | tf_op jit(solution)/shard_map/pair_sums/pallas_call | solution.py:187
  27.0 7.9 %pair_sums.5 = bf16[384,1152]{1,0:T(8,128)(2,1)S(1)} custom-call(s32[5]{0:T(128)S(1)} %pad_add_fusion.3.quarter_ref, bf16[6,96,512]{2,1,0:T(8,128)(2,1)S(1)} %collective-permute-done.2.refs_0_, f32[4,512]{1,0:T(4,128)S(1)} %get-tuple-element.20.refs_1_, f32[384,1152]{1,0:T(8,128)S(1)} %pair_sums.4.refs_2_), custom_call_target="tpu_custom_call" | custom-call | tf_op jit(solution)/shard_map/pair_sums/pallas_call | solution.py:187
  34.8 20.7 %all_to_all.5.parts_ref = bf16[16,24,1152]{2,1,0:T(8,128)(2,1)S(1)} all-to-all(bf16[16,24,1152]{2,1,0:T(8,128)(2,1)S(1)} %bitcast.27), channel_id=1, replica_groups=mesh['space'=16,'tm'=8] {'space'}, dimensions={0} | all-to-all | bytes 1769472 | tf_op jit(solution)/shard_map/all_to_all | solution.py:430
  55.5 1.0 %fold.1.refs_0_ = bf16[18,48,128]{2,1,0:T(8,128)(2,1)S(1)} custom-call(bf16[16,24,1152]{2,1,0:T(8,128)(2,1)S(1)} %all_to_all.5.parts_ref), custom_call_target="tpu_custom_call" | custom-call | tf_op jit(solution)/shard_map/fold/pallas_call | solution.py:253
  56.5 3.1 %collective-permute-start.3 = (bf16[18,48,128]{2,1,0:T(8,128)(2,1)S(1)}, bf16[18,48,128]{2,1,0:T(8,128)(2,1)S(1)}, u32[]{:S(2)}, u32[]{:S(2)}) collective-permute-start(bf16[18,48,128]{2,1,0:T(8,128)(2,1)S(1)} %fold.1.refs_0_), channel_id=1, source_target_pairs={{0,4},{1,5},{2,6},{3,7},{4,0},{5,1},{6,2},{7,3},{8,12},{9,13},{10,... | collective-permute-start | bytes 663560 | tf_op jit(solution)/shard_map/ppermute | solution.py:447
  59.6 1.9 %collective-permute-start.6 = (bf16[18,48,128]{2,1,0:T(8,128)(2,1)S(1)}, bf16[18,48,128]{2,1,0:T(8,128)(2,1)S(1)}, u32[]{:S(2)}, u32[]{:S(2)}) collective-permute-start(bf16[18,48,128]{2,1,0:T(8,128)(2,1)S(1)} %fold.1.refs_0_), channel_id=1, source_target_pairs={{0,1},{1,2},{2,3},{3,0},{4,5},{5,6},{6,7},{7,4},{8,9},{9,10},{10,1... | collective-permute-start | bytes 663560 | tf_op jit(solution)/shard_map/ppermute | solution.py:436
  61.5 2.1 %collective-permute-start.7 = (bf16[18,48,128]{2,1,0:T(8,128)(2,1)S(1)}, bf16[18,48,128]{2,1,0:T(8,128)(2,1)S(1)}, u32[]{:S(2)}, u32[]{:S(2)}) collective-permute-start(bf16[18,48,128]{2,1,0:T(8,128)(2,1)S(1)} %fold.1.refs_0_), channel_id=1, source_target_pairs={{0,3},{1,0},{2,1},{3,2},{4,7},{5,4},{6,5},{7,6},{8,11},{9,8},{10,9... | collective-permute-start | bytes 663560 | tf_op jit(solution)/shard_map/ppermute | solution.py:436
  63.7 1.7 %fill.4.refs_0_ = f32[8,6,288,128]{3,2,1,0:T(8,128)} custom-call(s32[1]{0:T(128)} %bitcast.9.order_ref, bf16[18,48,128]{2,1,0:T(8,128)(2,1)S(1)} %fold.1.refs_0_), custom_call_target="tpu_custom_call" | custom-call | tf_op jit(solution)/shard_map/fill/pallas_call | solution.py:378
  65.4 1.3 %collective-permute-start.4 = (bf16[18,48,128]{2,1,0:T(8,128)(2,1)S(1)}, bf16[18,48,128]{2,1,0:T(8,128)(2,1)S(1)}, u32[]{:S(2)}, u32[]{:S(2)}) collective-permute-start(bf16[18,48,128]{2,1,0:T(8,128)(2,1)S(1)} %collective-permute-done.3.refs_1_), channel_id=1, source_target_pairs={{0,1},{1,2},{2,3},{3,0},{4,5},{5,6},{6,7},{7,4},{8,9},{9,10},{10,1... | collective-permute-start | bytes 663560 | tf_op jit(solution)/shard_map/ppermute | solution.py:436
  66.7 2.1 %collective-permute-start.5 = (bf16[18,48,128]{2,1,0:T(8,128)(2,1)S(1)}, bf16[18,48,128]{2,1,0:T(8,128)(2,1)S(1)}, u32[]{:S(2)}, u32[]{:S(2)}) collective-permute-start(bf16[18,48,128]{2,1,0:T(8,128)(2,1)S(1)} %collective-permute-done.3.refs_1_), channel_id=1, source_target_pairs={{0,3},{1,0},{2,1},{3,2},{4,7},{5,4},{6,5},{7,6},{8,11},{9,8},{10,9... | collective-permute-start | bytes 663560 | tf_op jit(solution)/shard_map/ppermute | solution.py:436
  68.8 0.1 pad_add_fusion.4.order_ref
  68.9 0.0 collective-permute-done.6.refs_2_
  68.9 0.1 collective-permute-start.8
  69.0 3.3 %collective-permute-start.9 = (bf16[9,48,128]{2,1,0:T(8,128)(2,1)S(1)}, bf16[9,48,128]{2,1,0:T(8,128)(2,1)S(1)}, u32[]{:S(2)}, u32[]{:S(2)}) collective-permute-start(bf16[9,48,128]{2,1,0:T(8,128)(2,1)S(1)} %slice.32), channel_id=1, source_target_pairs={{0,3},{1,0},{2,1},{3,2},{4,7},{5,4},{6,5},{7,6},{8,11},{9,8},{10,9... | collective-permute-start | bytes 331784 | tf_op jit(solution)/shard_map/ppermute | solution.py:436
  72.3 4.0 %fill.5.refs_0_ = f32[8,6,288,128]{3,2,1,0:T(8,128)} custom-call(s32[3]{0:T(128)S(1)} %pad_add_fusion.4.order_ref, f32[8,6,288,128]{3,2,1,0:T(8,128)} %fill.4.refs_0_, bf16[18,48,128]{2,1,0:T(8,128)(2,1)S(1)} %collective-permute-done.3.refs_1_, bf16[18,48,128]{2,1,0:T(8,128)(2,1)S(1)} %collective-permute-done.6.refs_2_, ...), custom_call_target="tpu_custom_call", output_to_operand_aliasing={{}: (1, {})} | custom-call | tf_op jit(solution)/shard_map/fill/pallas_call | solution.py:378
  76.4 0.1 collective-permute-start.10
  76.5 3.3 %collective-permute-start.11 = (bf16[9,48,128]{2,1,0:T(8,128)(2,1)S(1)}, bf16[9,48,128]{2,1,0:T(8,128)(2,1)S(1)}, u32[]{:S(2)}, u32[]{:S(2)}) collective-permute-start(bf16[9,48,128]{2,1,0:T(8,128)(2,1)S(1)} %slice.27), channel_id=1, source_target_pairs={{0,3},{1,0},{2,1},{3,2},{4,7},{5,4},{6,5},{7,6},{8,11},{9,8},{10,9... | collective-permute-start | bytes 331784 | tf_op jit(solution)/shard_map/ppermute | solution.py:436
  79.7 0.1 pad_add_fusion.1
  79.8 3.1 %fill.6.refs_0_ = f32[8,6,288,128]{3,2,1,0:T(8,128)} custom-call(s32[2]{0:T(128)S(1)} %get-tuple-element.28.order_ref, f32[8,6,288,128]{3,2,1,0:T(8,128)} %fill.5.refs_0_, bf16[18,48,128]{2,1,0:T(8,128)(2,1)S(1)} %collective-permute-done.4.refs_1_, bf16[18,48,128]{2,1,0:T(8,128)(2,1)S(1)} %collective-permute-done.5.refs_2_), custom_call_target="tpu_custom_call", output_to_operand_aliasing={{}: (1, {})} | custom-call | tf_op jit(solution)/shard_map/fill/pallas_call | solution.py:378
  83.0 3.1 %fill.7 = f32[8,6,288,128]{3,2,1,0:T(8,128)} custom-call(s32[2]{0:T(128)S(1)} %get-tuple-element.27.order_ref, f32[8,6,288,128]{3,2,1,0:T(8,128)} %fill.6.refs_0_, bf16[9,48,128]{2,1,0:T(8,128)(2,1)S(1)} %collective-permute-done.8.refs_1_, bf16[9,48,128]{2,1,0:T(8,128)(2,1)S(1)} %collective-permute-done.9.refs_2_, ...), custom_call_target="tpu_custom_call", output_to_operand_aliasing={{}: (1, {})} | custom-call | tf_op jit(solution)/shard_map/fill/pallas_call | solution.py:378
  (26 shorter events, 0.2 us)
Async XLA Ops:
  0.0 4.1 %collective-permute-start.1 = (bf16[6,96,512]{2,1,0:T(8,128)(2,1)}, bf16[6,96,512]{2,1,0:T(8,128)(2,1)S(1)}, u32[]{:S(2)}, u32[]{:S(2)}) collective-permute-start(bf16[6,96,512]{2,1,0:T(8,128)(2,1)} %bitcast.28), channel_id=1, source_target_pairs={{0,8},{8,0},{16,24},{24,16},{32,40},{40,32},{48,56},{56,48},{64,72... | collective-permute-start | bytes 1769480 | tf_op jit(solution)/shard_map/ppermute | solution.py:410
  0.0 19.1 %collective-permute-start = (bf16[6,96,512]{2,1,0:T(8,128)(2,1)}, bf16[6,96,512]{2,1,0:T(8,128)(2,1)S(1)}, u32[]{:S(2)}, u32[]{:S(2)}) collective-permute-start(bf16[6,96,512]{2,1,0:T(8,128)(2,1)} %bitcast.29), channel_id=1, source_target_pairs={{0,64},{8,72},{16,80},{24,88},{32,96},{40,104},{48,112},{56,120},{... | collective-permute-start | bytes 1769480 | tf_op jit(solution)/shard_map/ppermute | solution.py:411
  4.1 1.1 %copy-start = (bf16[1,2,3,96,512]{4,3,2,1,0:T(8,128)(2,1)S(1)}, bf16[1,2,3,96,512]{4,3,2,1,0:T(8,128)(2,1)}, u32[]{:S(2)}) copy-start(bf16[1,2,3,96,512]{4,3,2,1,0:T(8,128)(2,1)} %param.5) | copy-start | bytes 1769476
  19.1 7.9 %collective-permute-start.2 = (bf16[6,96,512]{2,1,0:T(8,128)(2,1)S(1)}, bf16[6,96,512]{2,1,0:T(8,128)(2,1)S(1)}, u32[]{:S(2)}, u32[]{:S(2)}) collective-permute-start(bf16[6,96,512]{2,1,0:T(8,128)(2,1)S(1)} %collective-permute-done.refs_0_), channel_id=1, source_target_pairs={{0,8},{8,0},{16,24},{24,16},{32,40},{40,32},{48,56},{56,48},{64,72... | collective-permute-start | bytes 1769480 | tf_op jit(solution)/shard_map/ppermute | solution.py:427
  56.5 8.9 %collective-permute-start.3 = (bf16[18,48,128]{2,1,0:T(8,128)(2,1)S(1)}, bf16[18,48,128]{2,1,0:T(8,128)(2,1)S(1)}, u32[]{:S(2)}, u32[]{:S(2)}) collective-permute-start(bf16[18,48,128]{2,1,0:T(8,128)(2,1)S(1)} %fold.1.refs_0_), channel_id=1, source_target_pairs={{0,4},{1,5},{2,6},{3,7},{4,0},{5,1},{6,2},{7,3},{8,12},{9,13},{10,... | collective-permute-start | bytes 663560 | tf_op jit(solution)/shard_map/ppermute | solution.py:447
  59.6 9.3 %collective-permute-start.6 = (bf16[18,48,128]{2,1,0:T(8,128)(2,1)S(1)}, bf16[18,48,128]{2,1,0:T(8,128)(2,1)S(1)}, u32[]{:S(2)}, u32[]{:S(2)}) collective-permute-start(bf16[18,48,128]{2,1,0:T(8,128)(2,1)S(1)} %fold.1.refs_0_), channel_id=1, source_target_pairs={{0,1},{1,2},{2,3},{3,0},{4,5},{5,6},{6,7},{7,4},{8,9},{9,10},{10,1... | collective-permute-start | bytes 663560 | tf_op jit(solution)/shard_map/ppermute | solution.py:436
  61.5 7.5 %collective-permute-start.7 = (bf16[18,48,128]{2,1,0:T(8,128)(2,1)S(1)}, bf16[18,48,128]{2,1,0:T(8,128)(2,1)S(1)}, u32[]{:S(2)}, u32[]{:S(2)}) collective-permute-start(bf16[18,48,128]{2,1,0:T(8,128)(2,1)S(1)} %fold.1.refs_0_), channel_id=1, source_target_pairs={{0,3},{1,0},{2,1},{3,2},{4,7},{5,4},{6,5},{7,6},{8,11},{9,8},{10,9... | collective-permute-start | bytes 663560 | tf_op jit(solution)/shard_map/ppermute | solution.py:436
  65.4 11.0 %collective-permute-start.4 = (bf16[18,48,128]{2,1,0:T(8,128)(2,1)S(1)}, bf16[18,48,128]{2,1,0:T(8,128)(2,1)S(1)}, u32[]{:S(2)}, u32[]{:S(2)}) collective-permute-start(bf16[18,48,128]{2,1,0:T(8,128)(2,1)S(1)} %collective-permute-done.3.refs_1_), channel_id=1, source_target_pairs={{0,1},{1,2},{2,3},{3,0},{4,5},{5,6},{6,7},{7,4},{8,9},{9,10},{10,1... | collective-permute-start | bytes 663560 | tf_op jit(solution)/shard_map/ppermute | solution.py:436
  66.7 9.7 %collective-permute-start.5 = (bf16[18,48,128]{2,1,0:T(8,128)(2,1)S(1)}, bf16[18,48,128]{2,1,0:T(8,128)(2,1)S(1)}, u32[]{:S(2)}, u32[]{:S(2)}) collective-permute-start(bf16[18,48,128]{2,1,0:T(8,128)(2,1)S(1)} %collective-permute-done.3.refs_1_), channel_id=1, source_target_pairs={{0,3},{1,0},{2,1},{3,2},{4,7},{5,4},{6,5},{7,6},{8,11},{9,8},{10,9... | collective-permute-start | bytes 663560 | tf_op jit(solution)/shard_map/ppermute | solution.py:436
  68.9 14.0 %collective-permute-start.8 = (bf16[9,48,128]{2,1,0:T(8,128)(2,1)S(1)}, bf16[9,48,128]{2,1,0:T(8,128)(2,1)S(1)}, u32[]{:S(2)}, u32[]{:S(2)}) collective-permute-start(bf16[9,48,128]{2,1,0:T(8,128)(2,1)S(1)} %slice.31), channel_id=1, source_target_pairs={{0,1},{1,2},{2,3},{3,0},{4,5},{5,6},{6,7},{7,4},{8,9},{9,10},{10,1... | collective-permute-start | bytes 331784 | tf_op jit(solution)/shard_map/ppermute | solution.py:436
  69.0 13.9 %collective-permute-start.9 = (bf16[9,48,128]{2,1,0:T(8,128)(2,1)S(1)}, bf16[9,48,128]{2,1,0:T(8,128)(2,1)S(1)}, u32[]{:S(2)}, u32[]{:S(2)}) collective-permute-start(bf16[9,48,128]{2,1,0:T(8,128)(2,1)S(1)} %slice.32), channel_id=1, source_target_pairs={{0,3},{1,0},{2,1},{3,2},{4,7},{5,4},{6,5},{7,6},{8,11},{9,8},{10,9... | collective-permute-start | bytes 331784 | tf_op jit(solution)/shard_map/ppermute | solution.py:436
  76.4 6.6 %collective-permute-start.10 = (bf16[9,48,128]{2,1,0:T(8,128)(2,1)S(1)}, bf16[9,48,128]{2,1,0:T(8,128)(2,1)S(1)}, u32[]{:S(2)}, u32[]{:S(2)}) collective-permute-start(bf16[9,48,128]{2,1,0:T(8,128)(2,1)S(1)} %slice.26), channel_id=1, source_target_pairs={{0,1},{1,2},{2,3},{3,0},{4,5},{5,6},{6,7},{7,4},{8,9},{9,10},{10,1... | collective-permute-start | bytes 331784 | tf_op jit(solution)/shard_map/ppermute | solution.py:436
  76.5 6.5 %collective-permute-start.11 = (bf16[9,48,128]{2,1,0:T(8,128)(2,1)S(1)}, bf16[9,48,128]{2,1,0:T(8,128)(2,1)S(1)}, u32[]{:S(2)}, u32[]{:S(2)}) collective-permute-start(bf16[9,48,128]{2,1,0:T(8,128)(2,1)S(1)} %slice.27), channel_id=1, source_target_pairs={{0,3},{1,0},{2,1},{3,2},{4,7},{5,4},{6,5},{7,6},{8,11},{9,8},{10,9... | collective-permute-start | bytes 331784 | tf_op jit(solution)/shard_map/ppermute | solution.py:436
